TPU v7x, 128 devices: a whole 4x4x4 slice. The times are simulated.
128 devices in a mesh: leaf: 16 (over y_hi, x, core), rep: 8 (over y_lo, z).
Axes of the slice: x: 4, y: 4 (y_hi: 2, y_lo: 2; y = y_hi * 2 + y_lo), z: 4, core: 2. Of those that a mesh axis runs over, the one named last changes fastest.
Arguments:
- local_right: float32 [16, 8, 2048, 128], P('leaf', 'rep'), may hold values from -6 to 6
- local_inverse: bfloat16 [16, 8, 16, 128, 128], P('leaf', 'rep'), may hold values from -1 to 1.4, as said below
- local_below: bfloat16 [16, 8, 15, 128, 128], P('leaf', 'rep'), may hold values from -0.5 to 0.5
- local_parent: int32 [16, 8, 15], P('leaf', 'rep'), may hold values from 1 to 15, as said below
- local_coupling: bfloat16 [16, 8, 4, 384, 2048], P('leaf', 'rep'), may hold values from -0.1 to 0.1
- separator_right: float32 [15, 384, 128], replicated, may hold values from -6 to 6
- separator_inverse: bfloat16 [15, 3, 128, 128], replicated, may hold values from -1 to 1.4, as said below
- separator_lower: bfloat16 [15, 384, 384], replicated, may hold values from -0.3125 to 0.3125
- parent_coupling: bfloat16 [14, 384, 384], replicated, may hold values from -0.3125 to 0.3125
Outputs:
- local_solution: float32 [16, 8, 2048, 128], P('leaf', 'rep')
- separator_solution: float32 [16, 4, 384, 128], P('leaf')
Inputs may be any that keep to these rules, and one draw needn't show every extreme that they name: `local_parent`: entry k of a device's list is larger than k. `local_inverse`: every block is lower triangular. `separator_inverse`: every block is lower triangular.
All inputs are finite; a program needn't handle non-finite values.
Results may differ from a plain program's by a relative error of at most 0.035.
Values sent between devices are 32-bit elements; how exact they have to be, the bound alone decides.
No kernel may reach another device: no remote copies, remote signals or barrier semaphores. Data moves between devices by JAX's collectives and lax.ppermute only.
A program may use at most 128 MiB of HBM per device.

v0:
```python
import jax
import jax.numpy as jnp
from jax import lax
from jax.sharding import PartitionSpec as P

NB = 128
LB = 16
SB = 3


def swapped(value, axis, distance):
    mask = 2**distance
    pairs = [(source, source ^ mask) for source in range(lax.axis_size(axis))]
    return lax.ppermute(value, axis, pairs)


def apply_lower(matrix, vector):
    return jnp.dot(matrix, vector.astype(jnp.bfloat16), preferred_element_type=jnp.float32)


def apply_upper(matrix, vector):
    return jnp.dot(matrix.T, vector.astype(jnp.bfloat16), preferred_element_type=jnp.float32)


def right_lower(vector_rows, matrix):
    return jnp.dot(vector_rows.astype(jnp.bfloat16), matrix.T, preferred_element_type=jnp.float32)


def right_upper(vector_rows, matrix):
    return jnp.dot(vector_rows.astype(jnp.bfloat16), matrix, preferred_element_type=jnp.float32)


def block_lookup_tables(below, parents):
    targets = jnp.concatenate([parents, jnp.full((1,), LB, jnp.int32)])
    padded = jnp.concatenate([below, jnp.zeros((1, NB, NB), below.dtype)], axis=0)
    orders = jnp.arange(LB, dtype=jnp.int32)
    return (targets, padded, orders)


def local_forward(righthand, inverse, below, parents):
    columns = righthand.shape[1]
    blocks = righthand.reshape(LB, NB, columns)
    targets, padded, orders = block_lookup_tables(below, parents)

    def advance(carried, items):
        current, inv_block, low_block, target, number = items
        result = apply_lower(inv_block, current - carried[number])
        carried = carried.at[target].add(apply_lower(low_block, result))
        return (carried, result)

    start = jnp.zeros((LB + 1, NB, columns), jnp.float32)
    _, results = lax.scan(advance, start, (blocks, inverse, padded, targets, orders))
    return results.reshape(LB * NB, columns)


def local_backward(forward, update_terms, inverse, below, parents):
    columns = forward.shape[1]
    remains = (forward - update_terms).reshape(LB, NB, columns)
    targets, padded, orders = block_lookup_tables(below, parents)

    def retreat(carried, items):
        current, inv_block, low_block, target, number = items
        result = apply_upper(inv_block, current - apply_upper(low_block, carried[target]))
        carried = carried.at[number].set(result.astype(jnp.bfloat16))
        return (carried, result)

    start = jnp.zeros((LB + 1, NB, columns), jnp.bfloat16)
    _, results = lax.scan(retreat, start, (remains, inverse, padded, targets, orders), reverse=True)
    return results.reshape(LB * NB, columns)


def separator_forward(righthand, inverse, lowerpart):
    solved = []
    rounded = []
    for position in range(SB):
        current = righthand[:, position * NB : (position + 1) * NB]
        if position > 0:
            earlier = jnp.concatenate(rounded, axis=1)
            current = current - jnp.dot(
                earlier,
                lowerpart[position * NB : (position + 1) * NB, : position * NB].T,
                preferred_element_type=jnp.float32,
            )
        result = right_lower(current, inverse[position])
        solved.append(result)
        rounded.append(result.astype(jnp.bfloat16))
    return (jnp.concatenate(solved, axis=1), jnp.concatenate(rounded, axis=1))


def separator_backward(righthand, inverse, lowerpart):
    solved = [None] * SB
    rounded = [None] * SB
    for position in reversed(range(SB)):
        current = righthand[:, position * NB : (position + 1) * NB]
        if position < SB - 1:
            later = jnp.concatenate(rounded[position + 1 :], axis=1)
            current = current - right_upper(
                later, lowerpart[(position + 1) * NB :, position * NB : (position + 1) * NB]
            )
        result = right_upper(current, inverse[position])
        solved[position] = result
        rounded[position] = result.astype(jnp.bfloat16)
    return (jnp.concatenate(solved, axis=1), jnp.concatenate(rounded, axis=1))


def pick_entry(array, number):
    return lax.dynamic_index_in_dim(array, number, 0, keepdims=False)


def separator_chain(updates, separator_right, separator_inverse, separator_lower, parent_coupling):
    leaf_count = lax.axis_size("leaf")
    levels = leaf_count.bit_length() - 1
    leaf_index = lax.axis_index("leaf")
    remaining = updates
    forward_seps = []
    numbers = []
    inverse_blocks = []
    lowers = []
    for height in range(1, levels + 1):
        remaining = remaining + swapped(remaining, "leaf", height - 1)
        number = (leaf_count >> height) - 1 + (leaf_index >> height)
        right_rows = pick_entry(separator_right, number).T
        inverse = pick_entry(separator_inverse, number)
        lowerpart = pick_entry(separator_lower, number)
        result, result_round = separator_forward(right_rows - remaining[0], inverse, lowerpart)
        forward_seps.append(result)
        numbers.append(number)
        inverse_blocks.append(inverse)
        lowers.append(lowerpart)
        if height < levels:
            coupling_matrix = pick_entry(parent_coupling, number - 1)
            remaining = remaining[1:]
            remaining = remaining.at[0].add(
                jnp.dot(result_round, coupling_matrix.T, preferred_element_type=jnp.float32)
            )
    solutions = [None] * levels
    above_round = None
    for height in range(levels, 0, -1):
        upward = forward_seps[height - 1]
        if height < levels:
            coupling_matrix = pick_entry(parent_coupling, numbers[height - 1] - 1)
            upward = upward - right_upper(above_round, coupling_matrix)
        result, above_round = separator_backward(
            upward, inverse_blocks[height - 1], lowers[height - 1]
        )
        solutions[height - 1] = result
    return jnp.stack(solutions, axis=0)


def on_device(
    local_right,
    local_inverse,
    local_below,
    local_parent,
    local_coupling,
    separator_right,
    separator_inverse,
    separator_lower,
    parent_coupling,
):
    forward = local_forward(
        local_right[0, 0], local_inverse[0, 0], local_below[0, 0], local_parent[0, 0]
    )
    coupling_matrix = local_coupling[0, 0]
    forward_pass_rounded = forward.astype(jnp.bfloat16)
    partials = jnp.einsum(
        "ekx,xn->enk", coupling_matrix, forward_pass_rounded, preferred_element_type=jnp.float32
    )
    updates = lax.psum(partials, "rep")
    solved = separator_chain(
        updates, separator_right, separator_inverse, separator_lower, parent_coupling
    )
    rounded_solution_rows = solved.astype(jnp.bfloat16)
    update_terms = jnp.einsum(
        "apy,anp->yn", coupling_matrix, rounded_solution_rows, preferred_element_type=jnp.float32
    )
    local_solution = local_backward(
        forward, update_terms, local_inverse[0, 0], local_below[0, 0], local_parent[0, 0]
    )
    return (local_solution[None, None], jnp.swapaxes(solved, 1, 2)[None])


def solution(mesh):
    in_specs = (
        P("leaf", "rep", None, None),
        P("leaf", "rep", None, None, None),
        P("leaf", "rep", None, None, None),
        P("leaf", "rep", None),
        P("leaf", "rep", None, None, None),
        P(),
        P(),
        P(),
        P(),
    )
    out_specs = (P("leaf", "rep", None, None), P("leaf", None, None, None))
    return jax.shard_map(
        on_device, mesh=mesh, in_specs=in_specs, out_specs=out_specs, check_vma=False
    )
```

profile of v0, /device:TPU:1, one launch (start us, length us, event | category | flops | bytes accessed | tf_op | source)
XLA Modules:
  0.0 456.3 jit_solution(9730714361711297936)
XLA Ops:
  10.4 144.4 %while.33 = (s32[]{:T(128)}, f32[17,128,128]{2,1,0:T(8,128)}, f32[16,128,128]{2,1,0:T(8,128)S(1)}, s32[16]{0:T(128)S(1)}, bf16[16,128,128]{2,1,0:T(8,128)(2,1)S(...) while((s32[]{:T(128)}, f32[17,128,128]{2,1,0:T(8,128)}, ...), condition=%wide.region_2.3_spmd, body=%wide.region_0.2_spmd.sunk | while | flops 8470553 | bytes 462066 | solution.py:52
  17.2 2.2 fusion.409
  26.3 2.2 fusion.409
  35.3 2.2 fusion.409
  53.3 2.2 fusion.409
  62.4 2.2 fusion.409
  80.4 2.2 fusion.409
  89.4 2.2 fusion.409
  98.5 2.2 fusion.409
  107.5 2.2 fusion.409
  116.5 2.2 fusion.409
  134.6 2.2 fusion.409
  143.6 2.2 fusion.409
  154.9 6.0 %fusion.40 = f32[4,128,384]{2,1,0:T(8,128)} fusion(bf16[2048,128,1]{1,0,2:T(8,128)(2,1)S(1)} %bitcast.313, bf16[1,1,4,384,2048]{4,3,2,1,0:T(8,128)(2,1)} %param.27), kind=kOutput, calls=%fused_computation.38 | convolution fusion | flops 805306368 | bytes 7602176 | tf_op jit(solution)/shard_map/ekx,xn->enk/dot_general | solution.py:166
  161.0 74.4 %all-reduce.3.cloned.1.call-done = f32[4,128,384]{2,1,0:T(8,128)} async-done(((f32[4,128,384]{2,1,0:T(8,128)}), f32[4,128,384]{2,1,0:T(8,128)}) %all-reduce.3.cloned.1.call-update) | async-done | bytes 786448 | tf_op jit(solution)/shard_map/psum | solution.py:169
  235.4 5.8 %collective-permute-start = (f32[4,128,384]{2,1,0:T(8,128)}, f32[4,128,384]{2,1,0:T(8,128)}, u32[]{:S(2)}, u32[]{:S(2)}) collective-permute-start(f32[4,128,384]{2,1,0:T(8,128)} %all-reduce.3.cloned.1.call-done), channel_id=1, source_target_pairs={{0,8},{8,0},{16,24},{24,16},{32,40},{40,32},{48,56},{56,48},{64,72... | collective-permute-start | bytes 2359304 | tf_op jit(solution)/shard_map/ppermute | solution.py:14
  244.0 2.4 dynamic-slice_bitcast_fusion
  257.6 13.3 %collective-permute-done.1 = f32[3,128,384]{2,1,0:T(8,128)} collective-permute-done((f32[3,128,384]{2,1,0:T(8,128)}, f32[3,128,384]{2,1,0:T(8,128)}, u32[]{:S(2)}, u32[]{:S(2)}) %collective-permute-start.1) | collective-permute-done | bytes 589856 | tf_op jit(solution)/shard_map/ppermute | solution.py:14
  278.6 2.8 collective-permute-start.2
  283.2 7.0 %collective-permute-done.2 = f32[2,128,384]{2,1,0:T(8,128)} collective-permute-done((f32[2,128,384]{2,1,0:T(8,128)S(1)}, f32[2,128,384]{2,1,0:T(8,128)}, u32[]{:S(2)}, u32[]{:S(2)}) %collective-permute-start.2) | collective-permute-done | bytes 393248 | tf_op jit(solution)/shard_map/ppermute | solution.py:14
  298.4 2.4 collective-permute-start.3
  302.3 2.3 collective-permute-done.3
  320.5 3.8 fusion.37
  325.8 122.6 %while.34 = (s32[]{:T(128)}, bf16[17,128,128]{2,1,0:T(8,128)(2,1)S(1)}, f32[16,128,128]{2,1,0:T(8,128)S(1)}, s32[16]{0:T(128)S(1)}, bf16[16,128,128]{2,1,0:T(8,1...) while((s32[]{:T(128)}, ...), condition=%wide.region_6.7_spmd, body=%wide.region_4.6_spmd.sunk | while | flops 8454170 | bytes 363271 | solution.py:68
  (252 shorter events, 171.7 us)
Async XLA Ops:
  7.2 242.0 %copy-start = (bf16[15,3,128,128]{3,2,1,0:T(8,128)(2,1)S(1)}, bf16[15,3,128,128]{3,2,1,0:T(8,128)(2,1)}, u32[]{:S(2)}) copy-start(bf16[15,3,128,128]{3,2,1,0:T(8,128)(2,1)} %param.29) | copy-start | bytes 4423684
  7.2 228.2 %all-reduce.3.cloned.1.call-start = ((), (), s32[]{:S(2)}) async-start(), calls=%async_computation | async-start | bytes 1572864 | tf_op jit(solution)/shard_map/psum | solution.py:169
  7.2 3.2 copy-start.20
  154.8 6.1 %copy-start.2 = (bf16[16,128,128]{2,1,0:T(8,128)(2,1)}, bf16[16,128,128]{2,1,0:T(8,128)(2,1)S(1)}, u32[]{:S(2)}) copy-start(bf16[16,128,128]{2,1,0:T(8,128)(2,1)S(1)} %get-tuple-element.562) | copy-start | bytes 1572868
  235.4 11.0 %collective-permute-start = (f32[4,128,384]{2,1,0:T(8,128)}, f32[4,128,384]{2,1,0:T(8,128)}, u32[]{:S(2)}, u32[]{:S(2)}) collective-permute-start(f32[4,128,384]{2,1,0:T(8,128)} %all-reduce.3.cloned.1.call-done), channel_id=1, source_target_pairs={{0,8},{8,0},{16,24},{24,16},{32,40},{40,32},{48,56},{56,48},{64,72... | collective-permute-start | bytes 2359304 | tf_op jit(solution)/shard_map/ppermute | solution.py:14
  244.0 2.4 copy-start.10
  246.3 2.1 copy-start.6
  255.6 15.3 %collective-permute-start.1 = (f32[3,128,384]{2,1,0:T(8,128)}, f32[3,128,384]{2,1,0:T(8,128)}, u32[]{:S(2)}, u32[]{:S(2)}) collective-permute-start(f32[3,128,384]{2,1,0:T(8,128)} %fusion.78), channel_id=1, source_target_pairs={{0,16},{8,24},{16,0},{24,8},{32,48},{40,56},{48,32},{56,40},{64,80... | collective-permute-start | bytes 1769480 | tf_op jit(solution)/shard_map/ppermute | solution.py:14
  257.6 14.6 %copy-start.7 = (f32[1,384,128]{1,2,0:T(8,128)S(1)}, f32[1,384,128]{1,2,0:T(8,128)}, u32[]{:S(2)}) copy-start(f32[1,384,128]{1,2,0:T(8,128)} %copy.14) | copy-start | bytes 589828
  278.6 11.5 %collective-permute-start.2 = (f32[2,128,384]{2,1,0:T(8,128)S(1)}, f32[2,128,384]{2,1,0:T(8,128)}, u32[]{:S(2)}, u32[]{:S(2)}) collective-permute-start(f32[2,128,384]{2,1,0:T(8,128)S(1)} %fusion.76), channel_id=1, source_target_pairs={{0,32},{8,40},{16,48},{24,56},{32,0},{40,8},{48,16},{56,24},{64,96... | collective-permute-start | bytes 1179656 | tf_op jit(solution)/shard_map/ppermute | solution.py:14
  283.2 17.7 %copy-start.5 = (f32[1,384,128]{2,1,0:T(8,128)S(1)}, f32[1,384,128]{2,1,0:T(8,128)}, u32[]{:S(2)}) copy-start(f32[1,384,128]{2,1,0:T(8,128)} %get-tuple-element.317) | copy-start | bytes 589828
  298.4 6.2 %collective-permute-start.3 = (f32[1,128,384]{2,1,0:T(8,128)}, f32[1,128,384]{2,1,0:T(8,128)S(1)}, u32[]{:S(2)}, u32[]{:S(2)}) collective-permute-start(f32[1,128,384]{2,1,0:T(8,128)} %slice_add_fusion), channel_id=1, source_target_pairs={{0,64},{8,72},{16,80},{24,88},{32,96},{40,104},{48,112},{56,120},{... | collective-permute-start | bytes 589832 | tf_op jit(solution)/shard_map/ppermute | solution.py:14
  300.9 4.8 %copy-start.4 = (bf16[384,384]{1,0:T(8,128)(2,1)S(1)}, bf16[384,384]{1,0:T(8,128)(2,1)}, u32[]{:S(2)}) copy-start(bf16[384,384]{1,0:T(8,128)(2,1)} %get-tuple-element.310) | copy-start | bytes 884740
  302.3 5.1 %copy-start.15 = (f32[128,128]{0,1:T(8,128)S(1)}, f32[128,128]{0,1:T(8,128)}, u32[]{:S(2)}) copy-start(f32[128,128]{0,1:T(8,128)} %get-tuple-element.331) | copy-start | bytes 196612
  302.3 5.1 %copy-start.16 = (f32[128,128]{0,1:T(8,128)S(1)}, f32[128,128]{0,1:T(8,128)}, u32[]{:S(2)}) copy-start(f32[128,128]{0,1:T(8,128)} %get-tuple-element.335) | copy-start | bytes 196612
  302.3 5.1 %copy-start.19 = (f32[128,128]{0,1:T(8,128)S(1)}, f32[128,128]{0,1:T(8,128)}, u32[]{:S(2)}) copy-start(f32[128,128]{0,1:T(8,128)} %get-tuple-element.333) | copy-start | bytes 196612
  305.7 5.6 %copy-start.13 = (f32[128,128]{0,1:T(8,128)S(1)}, f32[128,128]{0,1:T(8,128)}, u32[]{:S(2)}) copy-start(f32[128,128]{0,1:T(8,128)} %get-tuple-element.325) | copy-start | bytes 196612
  305.7 5.6 %copy-start.14 = (f32[128,128]{0,1:T(8,128)S(1)}, f32[128,128]{0,1:T(8,128)}, u32[]{:S(2)}) copy-start(f32[128,128]{0,1:T(8,128)} %get-tuple-element.329) | copy-start | bytes 196612
  305.7 5.6 %copy-start.18 = (f32[128,128]{0,1:T(8,128)S(1)}, f32[128,128]{0,1:T(8,128)}, u32[]{:S(2)}) copy-start(f32[128,128]{0,1:T(8,128)} %get-tuple-element.327) | copy-start | bytes 196612
  307.4 7.8 %copy-start.11 = (f32[128,128]{0,1:T(8,128)S(1)}, f32[128,128]{0,1:T(8,128)}, u32[]{:S(2)}) copy-start(f32[128,128]{0,1:T(8,128)} %get-tuple-element.319) | copy-start | bytes 196612
  307.4 7.8 %copy-start.12 = (f32[128,128]{0,1:T(8,128)S(1)}, f32[128,128]{0,1:T(8,128)}, u32[]{:S(2)}) copy-start(f32[128,128]{0,1:T(8,128)} %get-tuple-element.323) | copy-start | bytes 196612
  307.4 7.8 %copy-start.17 = (f32[128,128]{0,1:T(8,128)S(1)}, f32[128,128]{0,1:T(8,128)}, u32[]{:S(2)}) copy-start(f32[128,128]{0,1:T(8,128)} %get-tuple-element.321) | copy-start | bytes 196612
  319.0 1.5 copy-start.1
  448.5 1.0 copy-start.3
  (2 other events, 1.4 us)
Sparse Core Ops, SparseCore 0:
  161.1 74.2 all-reduce.2
where the time goes:
time: 463 us; the launch traced here: 456 us
  loops' own time  123 us (27%)
  matrix products  112 us (24%)
  waiting for transfers between devices  97.1 us (21%)
  local copies, waits for them, and re-layouts  55.8 us (12%)
  other arithmetic  41 us (9%)
  between operations  14.5 us (3%)
  starting transfers between devices  12.2 us (3%)
    psum x1, waiting for transfers between devices, on_device(): updates = lax.psum(partials, 'rep')  74.4 us
    another operation x1, loops' own time, local_forward(): lax.scan(advance, start, (blocks, inverse, padded, targets, orders))  62.2 us
    another operation x1, loops' own time, local_backward(): lax.scan(retreat, start, (remains, inverse, padded, targets, orders), rev...  61 us
    dot_general x32, matrix products, apply_lower(): jnp.dot(matrix, vector.astype(jnp.bfloat16), preferred_element_type=jnp.f...  51.9 us
    dynamic_slice x64, local copies, waits for them, and re-layouts, local_forward(): lax.scan(advance, start, (blocks, inverse, padded, targets, orders))  39 us
    another operation x32, other arithmetic  23.2 us
    ppermute x4, waiting for transfers between devices, swapped(): return lax.ppermute(value, axis, pairs)  22.6 us
    dot_general x16, matrix products, apply_upper(): jnp.dot(matrix.T, vector.astype(jnp.bfloat16), preferred_element_type=jnp...  19.2 us
  transfers between devices with their start and end apart: 5, of which 4 were waited for; matrix products, arithmetic and copies ran while one was open for 2% of the time, Pallas kernels for 0%

commit v1 on v0

v1 whole, which is shorter than its diff:
```python
import jax
import jax.numpy as jnp
from jax import lax
from jax.experimental import pallas as pl
from jax.experimental.pallas import tpu as pltpu
from jax.sharding import PartitionSpec as P

NB = 128
LB = 16
SB = 3
S = SB * NB
LEV = 4
CH = 8
F32 = jnp.float32
BF16 = jnp.bfloat16
VMEM = pl.BlockSpec(memory_space=pltpu.VMEM)
SMEM = pl.BlockSpec(memory_space=pltpu.SMEM)
HBM = pl.BlockSpec(memory_space=pltpu.HBM)


def limit(mib):
    return pltpu.CompilerParams(vmem_limit_bytes=mib << 20)


def mm(a, b):
    return jnp.dot(a, b, preferred_element_type=F32)


def mm_nt(a, b):
    return lax.dot_general(a, b, (((1,), (1,)), ((), ())), preferred_element_type=F32)


def first_number(height):
    return (1 << (LEV - height)) - 1


def forward_kernel(
    parent, place, right, inverse, below, coupling_hbm, sepright_hbm,
    forward_t, keep, send,
    coupling, sepright, acc, rounded, sem,
):
    leaf, rep = place[0], place[1]
    copies = [pltpu.make_async_copy(coupling_hbm, coupling, sem.at[0])]
    for h in range(1, LEV + 1):
        number = first_number(h) + (leaf >> h)
        copies.append(
            pltpu.make_async_copy(sepright_hbm.at[number], sepright.at[h - 1], sem.at[h])
        )
    for copy in copies:
        copy.start()
    acc[...] = jnp.zeros_like(acc)
    for k in range(LB):
        result = mm(inverse[k], (right[k] - acc[k]).astype(BF16))
        low = result.astype(BF16)
        rounded[k * NB : (k + 1) * NB, :] = low
        forward_t[k] = result.T
        if k < LB - 1:
            p = parent[k]
            acc[p] = acc[p] + mm(below[k], low)
    for copy in copies:
        copy.wait()
    values = rounded[...]
    first_core = lax.rem(leaf, 2) == 0
    for h in range(1, LEV + 1):
        owner = jnp.logical_and(rep == 0, lax.rem(leaf, 1 << h) == 0)
        flag = jnp.where(owner, 1.0, 0.0).astype(F32)
        for i in range(SB):
            at = (h - 1) * S + i * NB
            block = flag * sepright[h - 1, i * NB : (i + 1) * NB, :] - mm(
                coupling[at : at + NB, :], values
            )
            block = block.T
            upper, lower = block[: NB // 2], block[NB // 2 :]
            keep[:, at : at + NB] = jnp.where(first_core, upper, lower)
            send[:, at : at + NB] = jnp.where(first_core, lower, upper)


def separator_kernel(inverse, lowerpart, coupling, full, product):
    for m in range(full.shape[0]):
        i0, i1, i2 = inverse[m, 0], inverse[m, 1], inverse[m, 2]
        l10 = lowerpart[m, NB : 2 * NB, :NB]
        l20 = lowerpart[m, 2 * NB :, :NB]
        l21 = lowerpart[m, 2 * NB :, NB : 2 * NB]
        x10 = (-mm(i1, mm(l10, i0).astype(BF16))).astype(BF16)
        x21 = (-mm(i2, mm(l21, i1).astype(BF16))).astype(BF16)
        x20 = (-mm(i2, (mm(l20, i0) + mm(l21, x10)).astype(BF16))).astype(BF16)
        zero = jnp.zeros((NB, NB), BF16)
        rows = (
            jnp.concatenate([i0, zero, zero], axis=1),
            jnp.concatenate([x10, i1, zero], axis=1),
            jnp.concatenate([x20, x21, i2], axis=1),
        )
        matrix = jnp.concatenate(rows, axis=0)
        full[m] = matrix
        if m > 0:
            product[m - 1] = mm(coupling[m - 1], matrix).astype(BF16)


def subtree_kernel(parent, forward_t, inverse, below, coupling, weights, base, base_low):
    rows = 256
    total = coupling.shape[0]
    for k in reversed(range(LB)):
        inv = inverse[k]
        if k < LB - 1:
            p = parent[k]
            low = below[k]
        value = forward_t[k]
        if k < LB - 1:
            value = value - mm(base_low[p], low)
        value = mm(value.astype(BF16), inv)
        base[k] = value
        base_low[k] = value.astype(BF16)
        for at in range(0, total, rows):
            part = coupling[at : at + rows, k * NB : (k + 1) * NB]
            if k < LB - 1:
                part = (part.astype(F32) - mm(weights[p, at : at + rows, :], low)).astype(BF16)
            weights[k, at : at + rows, :] = mm(part, inv).astype(BF16)


def tree_kernel(place, gathered, full, product, out, res1, res2, res3):
    chip = place[0] >> 1
    span = [slice(h * S, (h + 1) * S) for h in range(LEV)]
    residues = []
    for g in range(8):
        r = gathered[g, :, span[0]]
        res1[g] = r
        residues.append(r.astype(BF16))
    for h in range(2, LEV + 1):
        groups = 1 << (LEV - h)
        width = 8 // groups
        children = first_number(h - 1) - 1
        following = []
        for g in range(groups):
            r = gathered[g * width, :, span[h - 1]]
            for j in range(1, width):
                r = r + gathered[g * width + j, :, span[h - 1]]
            for c in (2 * g, 2 * g + 1):
                r = r - mm_nt(residues[c], product[children + c])
            if h == 2:
                res2[g] = r
            if h == 3:
                res3[g] = r
            following.append(r if h == LEV else r.astype(BF16))
        residues = following
    own = [res1[chip], res2[chip >> 1], res3[chip >> 2], residues[0]]
    above = None
    for h in range(LEV, 0, -1):
        number = first_number(h) + (place[0] >> h)
        matrix = full[number]
        value = mm(mm_nt(own[h - 1].astype(BF16), matrix).astype(BF16), matrix)
        if h < LEV:
            value = value - mm(above, product[number - 1])
        above = value.astype(BF16)
        for j in range(out.shape[0]):
            out[j, :, span[h - 1]] = value


def finish_kernel(place, mine, other, base, weights, local, separators):
    first_core = lax.rem(place[0], 2) == 0
    a, b = mine[...], other[...]
    rows = jnp.concatenate([jnp.where(first_core, a, b), jnp.where(first_core, b, a)], axis=0)
    low = rows.astype(BF16)
    for k in range(0, LB, 2):
        pair = jnp.concatenate([weights[k], weights[k + 1]], axis=1)
        terms = mm(low, pair)
        for j in range(2):
            value = base[k + j] - terms[:, j * NB : (j + 1) * NB]
            local[(k + j) * NB : (k + j + 1) * NB, :] = value.T
    for i in range(rows.shape[1] // NB):
        separators[i * NB : (i + 1) * NB, :] = rows[:, i * NB : (i + 1) * NB].T


def shape(dims, dtype=F32):
    return jax.ShapeDtypeStruct(dims, dtype)


def on_device(
    local_right,
    local_inverse,
    local_below,
    local_parent,
    local_coupling,
    separator_right,
    separator_inverse,
    separator_lower,
    parent_coupling,
):
    rows = local_right.shape[2]
    columns = local_right.shape[3]
    half = columns // 2
    height = LEV * S
    nsep = separator_lower.shape[0]
    leaves = lax.axis_size("leaf")
    chips = [[2 * i + c for i in range(leaves // 2)] for c in range(2)]
    pairs = [(i, i ^ 1) for i in range(leaves)]
    place = jnp.stack([lax.axis_index("leaf"), lax.axis_index("rep")]).astype(jnp.int32)
    right = local_right.reshape(LB, NB, columns)
    inverse = local_inverse[0, 0]
    below = local_below[0, 0]
    parent = local_parent[0, 0]
    coupling = local_coupling.reshape(height, rows)

    forward_t, keep, send = pl.pallas_call(
        forward_kernel,
        out_shape=(shape((LB, columns, NB)), shape((half, height)), shape((half, height))),
        in_specs=[SMEM, SMEM, VMEM, VMEM, VMEM, HBM, HBM],
        out_specs=(VMEM, VMEM, VMEM),
        scratch_shapes=[
            pltpu.VMEM((height, rows), BF16),
            pltpu.VMEM((LEV, S, columns), F32),
            pltpu.VMEM((LB, NB, columns), F32),
            pltpu.VMEM((rows, columns), BF16),
            pltpu.SemaphoreType.DMA((LEV + 1,)),
        ],
        compiler_params=limit(22),
        name="forward",
    )(parent, place, right, inverse, below, coupling, separator_right)

    total = keep + lax.ppermute(send, "leaf", pairs)
    parts = lax.all_to_all(total.reshape(8, CH, height), "rep", 0, 0, tiled=True)
    sep_inverse, sep_lower, sep_coupling, _ = lax.optimization_barrier(
        (separator_inverse, separator_lower, parent_coupling, total)
    )
    full, product = pl.pallas_call(
        separator_kernel,
        out_shape=(pltpu.VMEM((nsep, S, S), BF16), pltpu.VMEM((nsep - 1, S, S), BF16)),
        in_specs=[VMEM] * 3,
        out_specs=(VMEM, VMEM),
        compiler_params=limit(22),
        cost_estimate=pl.CostEstimate(flops=6 * 10**9, transcendentals=0, bytes_accessed=2 * 10**7),
        name="separator",
    )(sep_inverse, sep_lower, sep_coupling)

    parts, full, product = lax.optimization_barrier((parts, full, product))
    summed = jnp.broadcast_to(jnp.sum(parts, axis=0, keepdims=True), (8, CH, height))
    gathered = lax.all_to_all(summed, "leaf", 0, 0, axis_index_groups=chips, tiled=True)
    forward_t, _ = lax.optimization_barrier((forward_t, summed))
    weights, base = pl.pallas_call(
        subtree_kernel,
        out_shape=(pltpu.VMEM((LB, height, NB), BF16), pltpu.VMEM((LB, columns, NB), F32)),
        in_specs=[SMEM] + [VMEM] * 4,
        out_specs=(VMEM, VMEM),
        scratch_shapes=[pltpu.VMEM((LB, columns, NB), BF16)],
        compiler_params=limit(22),
        cost_estimate=pl.CostEstimate(flops=8 * 10**9, transcendentals=0, bytes_accessed=2 * 10**7),
        name="subtree",
    )(parent, forward_t, inverse, below, coupling)

    gathered, weights, base = lax.optimization_barrier((gathered, weights, base))
    solved = pl.pallas_call(
        tree_kernel,
        out_shape=shape((8, CH, height)),
        in_specs=[SMEM] + [VMEM] * 3,
        out_specs=VMEM,
        scratch_shapes=[
            pltpu.VMEM((8, CH, S), F32),
            pltpu.VMEM((4, CH, S), F32),
            pltpu.VMEM((2, CH, S), F32),
        ],
        compiler_params=limit(16),
        name="tree",
    )(place, gathered, full, product)
    mine = lax.all_to_all(solved, "rep", 0, 0, tiled=True).reshape(half, height)
    other = lax.ppermute(mine, "leaf", pairs)
    local, separators = pl.pallas_call(
        finish_kernel,
        out_shape=(shape((rows, columns)), shape((height, columns))),
        in_specs=[SMEM] + [VMEM] * 4,
        out_specs=(VMEM, VMEM),
        compiler_params=limit(16),
        name="finish",
    )(place, mine, other, base, weights)
    return (local[None, None], separators.reshape(1, LEV, S, columns))


def solution(mesh):
    in_specs = (
        P("leaf", "rep", None, None),
        P("leaf", "rep", None, None, None),
        P("leaf", "rep", None, None, None),
        P("leaf", "rep", None),
        P("leaf", "rep", None, None, None),
        P(),
        P(),
        P(),
        P(),
    )
    out_specs = (P("leaf", "rep", None, None), P("leaf", None, None, None))
    return jax.shard_map(
        on_device, mesh=mesh, in_specs=in_specs, out_specs=out_specs, check_vma=False
    )
```

time: 463 us -> 109 us (0.24); the launches traced: 456 us -> 108 us
  loops' own time: 123 us -> 0 us
  matrix products: 112 us -> 0 us
  waiting for transfers between devices: 97.1 us -> 2.7 us
  Pallas kernels: 0 us -> 46.7 us
  other arithmetic: 41 us -> 0.89 us
  local copies, waits for them, and re-layouts: 55.8 us -> 29.1 us
  between operations: 14.5 us -> 0.74 us
  blocking collectives: 0 us -> 11.2 us
    another operation x2 -> x0, loops' own time: 123 us -> none  [the longest x1 62.2 us: local_forward(): lax.scan(advance, start, (blocks, inverse, padded, targets, orders))]
    dot_general x80 -> x0, matrix products: 112 us -> none  [the longest x32 51.9 us: apply_lower(): jnp.dot(matrix, vector.astype(jnp.bfloat16), preferred_element_type=jnp.f...]
    psum x1 -> x0, waiting for transfers between devices: 74.4 us -> none  [on_device(): updates = lax.psum(partials, 'rep')]
    pallas_call x0 -> x5, Pallas kernels: none -> 46.7 us  [the longest x1 25.2 us: on_device(): pl.pallas_call(subtree_kernel, out_shape=(pltpu.VMEM((LB, height, NB), BF...]
    dynamic_slice x69 -> x0, local copies, waits for them, and re-layouts: 44.4 us -> none  [the longest x64 39 us: local_forward(): lax.scan(advance, start, (blocks, inverse, padded, targets, orders))]
    unnamed x42 -> x38, local copies, waits for them, and re-layouts: 2.89 us -> 28.4 us
    another operation x34 -> x1, other arithmetic: 23.2 us -> 0.08 us  [on_device(): jnp.stack([lax.axis_index('leaf'), lax.axis_index('rep')]).astype(jnp.int32)]
    ppermute x4 -> x2, waiting for transfers between devices: 22.6 us -> 2.7 us  [the longest x1 1.35 us: on_device(): total = keep + lax.ppermute(send, 'leaf', pairs)]
  transfers between devices with their start and end apart: 5 -> 4, of which waited for: 4 -> 2; matrix products, arithmetic and copies ran while one was open for 2% -> 0% of each run, Pallas kernels for 0% -> 30%
where the time goes in v1:
time: 109 us; the launch traced here: 108 us
  Pallas kernels  46.7 us (43%)
  local copies, waits for them, and re-layouts  29.1 us (27%)
  starting transfers between devices  16.7 us (15%)
  blocking collectives  11.2 us (10%)
  waiting for transfers between devices  2.7 us (2%)
    unnamed x38, local copies, waits for them, and re-layouts  28.4 us
    pallas_call x1, Pallas kernels, on_device(): pl.pallas_call(subtree_kernel, out_shape=(pltpu.VMEM((LB, height, NB), BF...  25.2 us
    all_to_all x1, blocking collectives, on_device(): mine = lax.all_to_all(solved, 'rep', 0, 0, tiled=True).reshape(half, height)  11.2 us
    pallas_call x1, Pallas kernels, on_device(): pl.pallas_call(forward_kernel, out_shape=(shape((LB, columns, NB)), shape...  8.36 us
    pallas_call x1, Pallas kernels, on_device(): pl.pallas_call(separator_kernel, out_shape=(pltpu.VMEM((nsep, S, S), BF16...  7.31 us
    all_to_all x1, starting transfers between devices, on_device(): lax.all_to_all(summed, 'leaf', 0, 0, axis_index_groups=chips, tiled=True)  6.36 us
    all_to_all x1, starting transfers between devices, on_device(): lax.all_to_all(total.reshape(8, CH, height), 'rep', 0, 0, tiled=True)  6.13 us
    pallas_call x1, Pallas kernels, on_device(): pl.pallas_call(finish_kernel, out_shape=(shape((rows, columns)), shape((h...  2.95 us
  transfers between devices with their start and end apart: 4, of which 2 were waited for; matrix products, arithmetic and copies ran while one was open for 0% of the time, Pallas kernels for 30%

profile of v1, /device:TPU:1, one launch (start us, length us, event | category | flops | bytes accessed | tf_op | source)
XLA Modules:
  0.0 108.2 jit_solution(532485903196839677)
XLA Ops:
  0.7 2.8 %copy-done = bf16[1,1,4,384,2048]{4,3,2,1,0:T(8,128)(2,1)S(1)} copy-done((bf16[1,1,4,384,2048]{4,3,2,1,0:T(8,128)(2,1)S(1)}, bf16[1,1,4,384,2048]{4,3,2,1,0:T(8,128)(2,1)}, u32[]{:S(2)}) %copy-start) | copy-done | bytes 6291480
  3.5 1.8 %copy-done.8 = f32[15,384,128]{2,1,0:T(8,128)S(1)} copy-done((f32[15,384,128]{2,1,0:T(8,128)S(1)}, f32[15,384,128]{2,1,0:T(8,128)}, u32[]{:S(2)}) %copy-start.8) | copy-done | bytes 2949144
  5.3 1.2 %copy-done.9 = f32[1,1,2048,128]{3,2,1,0:T(8,128)S(1)} copy-done((f32[1,1,2048,128]{3,2,1,0:T(8,128)S(1)}, f32[1,1,2048,128]{3,2,1,0:T(8,128)}, u32[]{:S(2)}) %copy-start.9) | copy-done | bytes 1048600
  9.3 8.4 %forward.1 = (f32[16,128,128]{2,1,0:T(8,128)S(1)}, f32[64,1536]{1,0:T(8,128)S(1)}, f32[64,1536]{1,0:T(8,128)S(1)}) custom-call(s32[15]{0:T(128)S(1)} %bitcast.20, s32[2]{0:T(128)S(1)} %pad_add_fusion.place, f32[16,128,128]{2,1,0:T(8,128)S(1)} %bitcast.15, bf16[16,128,128]{2,1,0:T(8,128)(2,1)S(1)} %bitcast.16, bf16[15,128,128]{2,1,0:T(8,128)(2,1)S(1)} %bitcast.18, ...), custom_call_target="tpu_custom_call" | custom-call | tf_op jit(solution)/shard_map/forward/pallas_call | solution.py:203
  17.7 1.5 %collective-permute-start = (f32[64,1536]{1,0:T(8,128)S(1)}, f32[64,1536]{1,0:T(8,128)S(1)}, u32[]{:S(2)}, u32[]{:S(2)}) collective-permute-start(f32[64,1536]{1,0:T(8,128)S(1)} %get-tuple-element.22), channel_id=1, source_target_pairs={{0,8},{8,0},{16,24},{24,16},{32,40},{40,32},{48,56},{56,48},{64,72... | collective-permute-start | bytes 1179656 | tf_op jit(solution)/shard_map/ppermute | solution.py:219
  19.2 1.3 %collective-permute-done = f32[64,1536]{1,0:T(8,128)S(1)} collective-permute-done((f32[64,1536]{1,0:T(8,128)S(1)}, f32[64,1536]{1,0:T(8,128)S(1)}, u32[]{:S(2)}, u32[]{:S(2)}) %collective-permute-start) | collective-permute-done | bytes 393248 | tf_op jit(solution)/shard_map/ppermute | solution.py:219
  21.3 6.1 %all-to-all-start = ((f32[8,8,1536]{2,1,0:T(8,128)}), f32[8,8,1536]{2,1,0:T(8,128)S(1)}, u32[]{:S(2)}, u32[]{:S(2)}) async-start(f32[8,8,1536]{2,1,0:T(8,128)} %bitcast.7), calls=%async_computation | async-start | bytes 786432 | tf_op jit(solution)/shard_map/all_to_all | solution.py:220
  27.4 2.2 %copy-done.16 = bf16[15,384,384]{2,1,0:T(8,128)(2,1)S(1)} copy-done((bf16[15,384,384]{2,1,0:T(8,128)(2,1)S(1)}, bf16[15,384,384]{2,1,0:T(8,128)(2,1)}, u32[]{:S(2)}) %copy-start.16) | copy-done | bytes 4423704
  29.7 2.2 %copy-done.17 = bf16[14,384,384]{2,1,0:T(8,128)(2,1)S(1)} copy-done((bf16[14,384,384]{2,1,0:T(8,128)(2,1)S(1)}, bf16[14,384,384]{2,1,0:T(8,128)(2,1)}, u32[]{:S(2)}) %copy-start.17) | copy-done | bytes 4128792
  31.8 1.4 %copy-done.18 = bf16[15,3,128,128]{3,2,1,0:T(8,128)(2,1)S(1)} copy-done((bf16[15,3,128,128]{3,2,1,0:T(8,128)(2,1)S(1)}, bf16[15,3,128,128]{3,2,1,0:T(8,128)(2,1)}, u32[]{:S(2)}) %copy-start.18) | copy-done | bytes 1474584
  33.2 7.3 %separator.1 = (bf16[15,384,384]{2,1,0:T(8,128)(2,1)S(1)}, bf16[14,384,384]{2,1,0:T(8,128)(2,1)S(1)}) custom-call(bf16[15,3,128,128]{3,2,1,0:T(8,128)(2,1)S(1)} %copy-done.18, bf16[15,384,384]{2,1,0:T(8,128)(2,1)S(1)} %copy-done.16, bf16[14,384,384]{2,1,0:T(8,128)(2,1)S(1)} %copy-done.17), custom_call_target="tpu_custom_call" | custom-call | flops 6000000000 | bytes 20000000 | tf_op jit(solution)/shard_map/separator/pallas_call | solution.py:224
  40.6 2.1 %copy-done.4 = bf16[15,384,384]{2,1,0:T(8,128)(2,1)} copy-done((bf16[15,384,384]{2,1,0:T(8,128)(2,1)}, bf16[15,384,384]{2,1,0:T(8,128)(2,1)S(1)}, u32[]{:S(2)}) %copy-start.4) | copy-done | bytes 4423704
  42.7 2.0 %copy-done.6 = bf16[14,384,384]{2,1,0:T(8,128)(2,1)} copy-done((bf16[14,384,384]{2,1,0:T(8,128)(2,1)}, bf16[14,384,384]{2,1,0:T(8,128)(2,1)S(1)}, u32[]{:S(2)}) %copy-start.6) | copy-done | bytes 4128792
  45.5 6.4 %all-to-all-start.1 = ((f32[8,8,1536]{2,1,0:T(8,128)}), f32[8,8,1536]{2,1,0:T(8,128)S(1)}, u32[]{:S(2)}, u32[]{:S(2)}) async-start(f32[8,8,1536]{2,1,0:T(8,128)} %broadcast_in_dim.4), calls=%async_computation.1 | async-start | bytes 786432 | tf_op jit(solution)/shard_map/all_to_all | solution.py:236
  51.9 2.8 %copy-done.1 = bf16[1,1,4,384,2048]{4,3,2,1,0:T(8,128)(2,1)S(1)} copy-done((bf16[1,1,4,384,2048]{4,3,2,1,0:T(8,128)(2,1)S(1)}, bf16[1,1,4,384,2048]{4,3,2,1,0:T(8,128)(2,1)}, u32[]{:S(2)}) %copy-start.1) | copy-done | bytes 6291480
  54.7 25.2 %subtree.1 = (bf16[16,1536,128]{2,1,0:T(8,128)(2,1)S(1)}, f32[16,128,128]{2,1,0:T(8,128)S(1)}) custom-call(s32[15]{0:T(128)S(1)} %bitcast.21, f32[16,128,128]{2,1,0:T(8,128)S(1)} %get-tuple-element.30.forward_t, bf16[16,128,128]{2,1,0:T(8,128)(2,1)S(1)} %bitcast.17, bf16[15,128,128]{2,1,0:T(8,128)(2,1)S(1)} %bitcast.19, bf16[1536,2048]{1,0:T(8,128)(2,1)S(1)} %bitcast.12), custom_call_target="tpu_custom_call" | custom-call | flops 8000000000 | bytes 20000000 | tf_op jit(solution)/shard_map/subtree/pallas_call | solution.py:238
  79.9 2.6 %copy-done.2 = bf16[16,1536,128]{2,1,0:T(8,128)(2,1)} copy-done((bf16[16,1536,128]{2,1,0:T(8,128)(2,1)}, bf16[16,1536,128]{2,1,0:T(8,128)(2,1)S(1)}, u32[]{:S(2)}) %copy-start.2) | copy-done | bytes 6291480
  82.5 2.3 %copy-done.5 = bf16[15,384,384]{2,1,0:T(8,128)(2,1)S(1)} copy-done((bf16[15,384,384]{2,1,0:T(8,128)(2,1)S(1)}, bf16[15,384,384]{2,1,0:T(8,128)(2,1)}, u32[]{:S(2)}) %copy-start.5) | copy-done | bytes 4423704
  84.8 2.2 %copy-done.7 = bf16[14,384,384]{2,1,0:T(8,128)(2,1)S(1)} copy-done((bf16[14,384,384]{2,1,0:T(8,128)(2,1)S(1)}, bf16[14,384,384]{2,1,0:T(8,128)(2,1)}, u32[]{:S(2)}) %copy-start.7) | copy-done | bytes 4128792
  87.0 2.9 %tree.1 = f32[8,8,1536]{2,1,0:T(8,128)S(1)} custom-call(s32[2]{0:T(128)S(1)} %pad_add_fusion.place, f32[8,8,1536]{2,1,0:T(8,128)S(1)} %all-to-all-done.1.gathered, bf16[15,384,384]{2,1,0:T(8,128)(2,1)S(1)} %copy-done.5, bf16[14,384,384]{2,1,0:T(8,128)(2,1)S(1)} %copy-done.7), custom_call_target="tpu_custom_call" | custom-call | tf_op jit(solution)/shard_map/tree/pallas_call | solution.py:250
  89.9 11.2 %all_to_all.15 = f32[8,8,1536]{2,1,0:T(8,128)S(1)} all-to-all(f32[8,8,1536]{2,1,0:T(8,128)S(1)} %tree.1), channel_id=1, replica_groups=mesh['leaf'=16,'rep'=8] {'rep'}, dimensions={0} | all-to-all | bytes 786432 | tf_op jit(solution)/shard_map/all_to_all | solution.py:263
  101.1 2.7 %collective-permute-start.1 = (f32[64,1536]{1,0:T(8,128)S(1)}, f32[64,1536]{1,0:T(8,128)S(1)}, u32[]{:S(2)}, u32[]{:S(2)}) collective-permute-start(f32[64,1536]{1,0:T(8,128)S(1)} %bitcast.13), channel_id=1, source_target_pairs={{0,8},{8,0},{16,24},{24,16},{32,40},{40,32},{48,56},{56,48},{64,72... | collective-permute-start | bytes 1179656 | tf_op jit(solution)/shard_map/ppermute | solution.py:264
  103.9 1.3 %collective-permute-done.1.other = f32[64,1536]{1,0:T(8,128)S(1)} collective-permute-done((f32[64,1536]{1,0:T(8,128)S(1)}, f32[64,1536]{1,0:T(8,128)S(1)}, u32[]{:S(2)}, u32[]{:S(2)}) %collective-permute-start.1) | collective-permute-done | bytes 393248 | tf_op jit(solution)/shard_map/ppermute | solution.py:264
  105.2 3.0 %finish.1 = (f32[2048,128]{1,0:T(8,128)}, f32[1536,128]{1,0:T(8,128)}) custom-call(s32[2]{0:T(128)S(1)} %pad_add_fusion.place, f32[64,1536]{1,0:T(8,128)S(1)} %bitcast.14, f32[64,1536]{1,0:T(8,128)S(1)} %collective-permute-done.1.other, f32[16,128,128]{2,1,0:T(8,128)S(1)} %get-tuple-element.36.base, bf16[16,1536,128]{2,1,0:T(8,128)(2,1)S(1)} %copy-done.3), custom_call_target="tpu_custom_call" | custom-call | tf_op jit(solution)/shard_map/finish/pallas_call | solution.py:265
  (32 shorter events, 4.4 us)
Async XLA Ops:
  0.7 2.8 %copy-start = (bf16[1,1,4,384,2048]{4,3,2,1,0:T(8,128)(2,1)S(1)}, bf16[1,1,4,384,2048]{4,3,2,1,0:T(8,128)(2,1)}, u32[]{:S(2)}) copy-start(bf16[1,1,4,384,2048]{4,3,2,1,0:T(8,128)(2,1)} %param.13) | copy-start | bytes 18874372
  3.5 1.8 %copy-start.8 = (f32[15,384,128]{2,1,0:T(8,128)S(1)}, f32[15,384,128]{2,1,0:T(8,128)}, u32[]{:S(2)}) copy-start(f32[15,384,128]{2,1,0:T(8,128)} %sepright_hbm.1) | copy-start | bytes 8847364
  5.3 1.2 %copy-start.9 = (f32[1,1,2048,128]{3,2,1,0:T(8,128)S(1)}, f32[1,1,2048,128]{3,2,1,0:T(8,128)}, u32[]{:S(2)}) copy-start(f32[1,1,2048,128]{3,2,1,0:T(8,128)} %param.9) | copy-start | bytes 3145732
  6.6 1.0 copy-start.10
  7.6 1.0 copy-start.12
  8.6 0.7 copy-start.14
  17.7 2.9 %collective-permute-start = (f32[64,1536]{1,0:T(8,128)S(1)}, f32[64,1536]{1,0:T(8,128)S(1)}, u32[]{:S(2)}, u32[]{:S(2)}) collective-permute-start(f32[64,1536]{1,0:T(8,128)S(1)} %get-tuple-element.22), channel_id=1, source_target_pairs={{0,8},{8,0},{16,24},{24,16},{32,40},{40,32},{48,56},{56,48},{64,72... | collective-permute-start | bytes 1179656 | tf_op jit(solution)/shard_map/ppermute | solution.py:219
  21.3 23.4 %all-to-all-start = ((f32[8,8,1536]{2,1,0:T(8,128)}), f32[8,8,1536]{2,1,0:T(8,128)S(1)}, u32[]{:S(2)}, u32[]{:S(2)}) async-start(f32[8,8,1536]{2,1,0:T(8,128)} %bitcast.7), calls=%async_computation | async-start | bytes 786432 | tf_op jit(solution)/shard_map/all_to_all | solution.py:220
  27.4 2.3 %copy-start.16 = (bf16[15,384,384]{2,1,0:T(8,128)(2,1)S(1)}, bf16[15,384,384]{2,1,0:T(8,128)(2,1)}, u32[]{:S(2)}) copy-start(bf16[15,384,384]{2,1,0:T(8,128)(2,1)} %lowerpart) | copy-start | bytes 13271044
  29.7 2.2 %copy-start.17 = (bf16[14,384,384]{2,1,0:T(8,128)(2,1)S(1)}, bf16[14,384,384]{2,1,0:T(8,128)(2,1)}, u32[]{:S(2)}) copy-start(bf16[14,384,384]{2,1,0:T(8,128)(2,1)} %coupling) | copy-start | bytes 12386308
  31.8 1.4 %copy-start.18 = (bf16[15,3,128,128]{3,2,1,0:T(8,128)(2,1)S(1)}, bf16[15,3,128,128]{3,2,1,0:T(8,128)(2,1)}, u32[]{:S(2)}) copy-start(bf16[15,3,128,128]{3,2,1,0:T(8,128)(2,1)} %inverse) | copy-start | bytes 4423684
  33.2 18.7 %copy-start.11 = (bf16[1,1,16,128,128]{4,3,2,1,0:T(8,128)(2,1)S(1)}, bf16[1,1,16,128,128]{4,3,2,1,0:T(8,128)(2,1)}, u32[]{:S(2)}) copy-start(bf16[1,1,16,128,128]{4,3,2,1,0:T(8,128)(2,1)} %param.10) | copy-start | bytes 1572868
  33.2 18.7 %copy-start.13 = (bf16[1,1,15,128,128]{4,3,2,1,0:T(8,128)(2,1)S(1)}, bf16[1,1,15,128,128]{4,3,2,1,0:T(8,128)(2,1)}, u32[]{:S(2)}) copy-start(bf16[1,1,15,128,128]{4,3,2,1,0:T(8,128)(2,1)} %param.11) | copy-start | bytes 1474564
  33.2 18.7 %copy-start.15 = (s32[1,1,15]{2,1,0:T(1,128)S(1)}, s32[1,1,15]{2,1,0:T(1,128)}, u32[]{:S(2)}) copy-start(s32[1,1,15]{2,1,0:T(1,128)} %param.12) | copy-start | bytes 184
  40.5 2.1 %copy-start.4 = (bf16[15,384,384]{2,1,0:T(8,128)(2,1)}, bf16[15,384,384]{2,1,0:T(8,128)(2,1)S(1)}, u32[]{:S(2)}) copy-start(bf16[15,384,384]{2,1,0:T(8,128)(2,1)S(1)} %get-tuple-element.34.full) | copy-start | bytes 13271044
  42.7 2.0 %copy-start.6 = (bf16[14,384,384]{2,1,0:T(8,128)(2,1)}, bf16[14,384,384]{2,1,0:T(8,128)(2,1)S(1)}, u32[]{:S(2)}) copy-start(bf16[14,384,384]{2,1,0:T(8,128)(2,1)S(1)} %get-tuple-element.35.product) | copy-start | bytes 12386308
  45.5 37.0 %all-to-all-start.1 = ((f32[8,8,1536]{2,1,0:T(8,128)}), f32[8,8,1536]{2,1,0:T(8,128)S(1)}, u32[]{:S(2)}, u32[]{:S(2)}) async-start(f32[8,8,1536]{2,1,0:T(8,128)} %broadcast_in_dim.4), calls=%async_computation.1 | async-start | bytes 786432 | tf_op jit(solution)/shard_map/all_to_all | solution.py:236
  51.9 2.8 %copy-start.1 = (bf16[1,1,4,384,2048]{4,3,2,1,0:T(8,128)(2,1)S(1)}, bf16[1,1,4,384,2048]{4,3,2,1,0:T(8,128)(2,1)}, u32[]{:S(2)}) copy-start(bf16[1,1,4,384,2048]{4,3,2,1,0:T(8,128)(2,1)} %param.13) | copy-start | bytes 18874372
  79.9 2.7 %copy-start.2 = (bf16[16,1536,128]{2,1,0:T(8,128)(2,1)}, bf16[16,1536,128]{2,1,0:T(8,128)(2,1)S(1)}, u32[]{:S(2)}) copy-start(bf16[16,1536,128]{2,1,0:T(8,128)(2,1)S(1)} %get-tuple-element.37.weights) | copy-start | bytes 18874372
  82.5 2.3 %copy-start.5 = (bf16[15,384,384]{2,1,0:T(8,128)(2,1)S(1)}, bf16[15,384,384]{2,1,0:T(8,128)(2,1)}, u32[]{:S(2)}) copy-start(bf16[15,384,384]{2,1,0:T(8,128)(2,1)} %copy-done.4) | copy-start | bytes 13271044
  84.8 2.2 %copy-start.7 = (bf16[14,384,384]{2,1,0:T(8,128)(2,1)S(1)}, bf16[14,384,384]{2,1,0:T(8,128)(2,1)}, u32[]{:S(2)}) copy-start(bf16[14,384,384]{2,1,0:T(8,128)(2,1)} %copy-done.6) | copy-start | bytes 12386308
  87.0 18.3 %copy-start.3 = (bf16[16,1536,128]{2,1,0:T(8,128)(2,1)S(1)}, bf16[16,1536,128]{2,1,0:T(8,128)(2,1)}, u32[]{:S(2)}) copy-start(bf16[16,1536,128]{2,1,0:T(8,128)(2,1)} %copy-done.2) | copy-start | bytes 18874372
  101.1 4.1 %collective-permute-start.1 = (f32[64,1536]{1,0:T(8,128)S(1)}, f32[64,1536]{1,0:T(8,128)S(1)}, u32[]{:S(2)}, u32[]{:S(2)}) collective-permute-start(f32[64,1536]{1,0:T(8,128)S(1)} %bitcast.13), channel_id=1, source_target_pairs={{0,8},{8,0},{16,24},{24,16},{32,40},{40,32},{48,56},{56,48},{64,72... | collective-permute-start | bytes 1179656 | tf_op jit(solution)/shard_map/ppermute | solution.py:264

commit v2 on v1

v2 whole, which is shorter than its diff:
```python
import jax
import jax.numpy as jnp
from jax import lax
from jax.experimental import pallas as pl
from jax.experimental.pallas import tpu as pltpu
from jax.sharding import PartitionSpec as P

NB = 128
LB = 16
SB = 3
S = SB * NB
LEV = 4
CH = 8
F32 = jnp.float32
BF16 = jnp.bfloat16
VMEM = pl.BlockSpec(memory_space=pltpu.VMEM)
SMEM = pl.BlockSpec(memory_space=pltpu.SMEM)
HBM = pl.BlockSpec(memory_space=pltpu.HBM)


def in_hbm(*arrays):
    return [pltpu.with_memory_space_constraint(array, pltpu.HBM) for array in arrays]


def limit(mib):
    return pltpu.CompilerParams(vmem_limit_bytes=mib << 20)


def mm(a, b):
    return jnp.dot(a, b, preferred_element_type=F32)


def mm_nt(a, b):
    return lax.dot_general(a, b, (((1,), (1,)), ((), ())), preferred_element_type=F32)


def first_number(height):
    return (1 << (LEV - height)) - 1


def forward_kernel(
    place, parent_hbm, right_hbm, inverse_hbm, below_hbm, coupling_hbm, sepright_hbm,
    forward_hbm, weights_hbm, factors_hbm, keep, send,
    forward_t, weights, factors,
    parent, right, inverse, below, coupling, sepright, acc, rounded, sem, out_sem,
):
    leaf, rep = place[0], place[1]
    first = [
        pltpu.make_async_copy(parent_hbm, parent, sem.at[0]),
        pltpu.make_async_copy(inverse_hbm, inverse, sem.at[1]),
        pltpu.make_async_copy(below_hbm, below, sem.at[2]),
        pltpu.make_async_copy(right_hbm, right, sem.at[3]),
    ]
    quarters = []
    for q in range(4):
        columns = pl.ds((3 - q) * 4 * NB, 4 * NB)
        quarters.append(
            pltpu.make_async_copy(
                coupling_hbm.at[:, columns], coupling.at[:, columns], sem.at[4 + q]
            )
        )
    others = []
    for h in range(1, LEV + 1):
        number = first_number(h) + (leaf >> h)
        others.append(
            pltpu.make_async_copy(sepright_hbm.at[number], sepright.at[h - 1], sem.at[7 + h])
        )
    for copy in first + quarters + others:
        copy.start()
    acc[...] = jnp.zeros_like(acc)
    for copy in first:
        copy.wait()
    for k in range(LB):
        factors[k, :NB, :] = inverse[k]
        if k < LB - 1:
            factors[k, NB:, :] = (-mm(below[k], inverse[k])).astype(BF16)
        else:
            factors[k, NB:, :] = jnp.zeros((NB, NB), BF16)
    outward = [pltpu.make_async_copy(factors, factors_hbm, out_sem.at[LB])]
    outward[0].start()
    rows = coupling.shape[0] // 2
    for i in range(LB):
        k = i
        result = mm(inverse[k], (right[k] - acc[k]).astype(BF16))
        low = result.astype(BF16)
        rounded[k * NB : (k + 1) * NB, :] = low
        forward_t[k] = result.T
        if k < LB - 1:
            p = parent[0, 0, k]
            acc[p] = acc[p] + mm(below[k], low)
        k = LB - 1 - i
        if i % 4 == 0:
            quarters[i // 4].wait()
        own = coupling[:, k * NB : (k + 1) * NB]
        if k < LB - 1:
            p = parent[0, 0, k]
            above = [weights[p, :rows, :], weights[p, rows:, :]]
            factor = factors[k]
            for j in range(2):
                part = jnp.concatenate([own[j * rows : (j + 1) * rows], above[j]], axis=1)
                weights[k, j * rows : (j + 1) * rows, :] = mm(part, factor).astype(BF16)
        else:
            weights[k] = mm(own, inverse[k]).astype(BF16)
        outward.append(pltpu.make_async_copy(weights.at[k], weights_hbm.at[k], out_sem.at[k]))
        outward[-1].start()
    outward.append(pltpu.make_async_copy(forward_t, forward_hbm, out_sem.at[LB + 1]))
    outward[-1].start()
    for copy in others:
        copy.wait()
    values = rounded[...]
    first_core = lax.rem(leaf, 2) == 0
    for h in range(1, LEV + 1):
        owner = jnp.logical_and(rep == 0, lax.rem(leaf, 1 << h) == 0)
        flag = jnp.where(owner, 1.0, 0.0).astype(F32)
        for i in range(SB):
            at = (h - 1) * S + i * NB
            block = flag * sepright[h - 1, i * NB : (i + 1) * NB, :] - mm(
                coupling[at : at + NB, :], values
            )
            block = block.T
            upper, lower = block[: NB // 2], block[NB // 2 :]
            keep[:, at : at + NB] = jnp.where(first_core, upper, lower)
            send[:, at : at + NB] = jnp.where(first_core, lower, upper)
    for copy in outward:
        copy.wait()


def separator_kernel(
    place, inverse_hbm, lower_hbm, coupling_hbm, full_hbm, product,
    full, inverse, lowerpart, coupling, sem, out_sem,
):
    shared = first_number(1)
    number = shared + (place[0] >> 1)
    groups = []
    for at, size, source in ((shared, 1, number), (3, 4, 3), (0, 3, 0)):
        k = len(groups) * 3
        low = max(at, 1)
        count = size - (low - at)
        start = number - 1 if at == shared else low - 1
        groups.append([
            pltpu.make_async_copy(
                inverse_hbm.at[pl.ds(source, size)], inverse.at[pl.ds(at, size)], sem.at[k]
            ),
            pltpu.make_async_copy(
                lower_hbm.at[pl.ds(source, size)], lowerpart.at[pl.ds(at, size)], sem.at[k + 1]
            ),
            pltpu.make_async_copy(
                coupling_hbm.at[pl.ds(start, count)],
                coupling.at[pl.ds(low - 1, count)],
                sem.at[k + 2],
            ),
        ])
    for group in groups:
        for copy in group:
            copy.start()
    outward = []
    for group, members in zip(groups, ((shared,), range(3, shared), range(3))):
        for copy in group:
            copy.wait()
        for m in members:
            i0, i1, i2 = inverse[m, 0], inverse[m, 1], inverse[m, 2]
            l10 = lowerpart[m, NB : 2 * NB, :NB]
            l20 = lowerpart[m, 2 * NB :, :NB]
            l21 = lowerpart[m, 2 * NB :, NB : 2 * NB]
            x10 = (-mm(i1, mm(l10, i0).astype(BF16))).astype(BF16)
            x21 = (-mm(i2, mm(l21, i1).astype(BF16))).astype(BF16)
            x20 = (-mm(i2, (mm(l20, i0) + mm(l21, x10)).astype(BF16))).astype(BF16)
            zero = jnp.zeros((NB, NB), BF16)
            parts = (
                jnp.concatenate([i0, zero, zero], axis=1),
                jnp.concatenate([x10, i1, zero], axis=1),
                jnp.concatenate([x20, x21, i2], axis=1),
            )
            matrix = jnp.concatenate(parts, axis=0)
            full[m] = matrix
            outward.append(pltpu.make_async_copy(full.at[m], full_hbm.at[m], out_sem.at[m]))
            outward[-1].start()
            if m > 0:
                product[m - 1] = mm(coupling[m - 1], matrix).astype(BF16)
    for copy in outward:
        copy.wait()


def level_kernel(parts, product, out, residue):
    total = parts[0]
    for j in range(1, parts.shape[0]):
        total = total + parts[j]
    level = total[:, :S]
    residue[...] = level
    second = total[:, S : 2 * S] - mm_nt(level.astype(BF16), product[product.shape[0] - 1])
    for j in range(out.shape[0]):
        out[j, :, :S] = second
        out[j, :, S:] = total[:, 2 * S :]


def base_kernel(
    parent_hbm, forward_hbm, factors_hbm, base, parent, forward_t, factors, base_low, sem
):
    copies = [
        pltpu.make_async_copy(parent_hbm, parent, sem.at[0]),
        pltpu.make_async_copy(factors_hbm, factors, sem.at[1]),
        pltpu.make_async_copy(forward_hbm, forward_t, sem.at[2]),
    ]
    for copy in copies:
        copy.start()
    for copy in copies:
        copy.wait()
    for k in reversed(range(LB)):
        value = forward_t[k].astype(BF16)
        if k < LB - 1:
            value = jnp.concatenate([value, base_low[parent[0, 0, k]]], axis=1)
            value = mm(value, factors[k])
        else:
            value = mm(value, factors[k, :NB, :])
        base[k] = value
        base_low[k] = value.astype(BF16)


def tree_kernel(place, gathered, residue, full_hbm, product, out, res2, res3, full, sem):
    leaf = place[0]
    copies = []
    for h in range(1, LEV + 1):
        number = first_number(1) if h == 1 else first_number(h) + (leaf >> h)
        copies.append(pltpu.make_async_copy(full_hbm.at[number], full.at[h - 1], sem.at[h - 1]))
    for copy in copies:
        copy.start()
    span = [slice(h * S, (h + 1) * S) for h in range(LEV)]
    residues = []
    for h in range(2, LEV + 1):
        groups = 1 << (LEV - h)
        width = 8 // groups
        children = first_number(h - 1) - 1
        following = []
        for g in range(groups):
            r = gathered[g * width, :, span[h - 2]]
            for j in range(1, width):
                r = r + gathered[g * width + j, :, span[h - 2]]
            if h > 2:
                for c in (2 * g, 2 * g + 1):
                    r = r - mm_nt(residues[c], product[children + c])
            if h == 2:
                res2[g] = r
            if h == 3:
                res3[g] = r
            following.append(r if h == LEV else r.astype(BF16))
        residues = following
    own = [residue[...], res2[leaf >> 2], res3[leaf >> 3], residues[0]]
    above = None
    for copy in copies:
        copy.wait()
    for h in range(LEV, 0, -1):
        number = first_number(1) if h == 1 else first_number(h) + (leaf >> h)
        matrix = full[h - 1]
        value = mm(mm_nt(own[h - 1].astype(BF16), matrix).astype(BF16), matrix)
        if h < LEV:
            value = value - mm(above, product[number - 1])
        above = value.astype(BF16)
        for j in range(out.shape[0]):
            out[j, :, span[h - 1]] = value


def finish_kernel(
    place, mine, other, base, weights_hbm, local_hbm, separators_hbm,
    weights, local, separators, sem, out_sem,
):
    inward = [
        pltpu.make_async_copy(weights_hbm.at[k], weights.at[k], sem.at[k]) for k in range(LB)
    ]
    for copy in inward:
        copy.start()
    first_core = lax.rem(place[0], 2) == 0
    a, b = mine[...], other[...]
    rows = jnp.concatenate([jnp.where(first_core, a, b), jnp.where(first_core, b, a)], axis=0)
    low = rows.astype(BF16)
    for i in range(rows.shape[1] // NB):
        separators[i * NB : (i + 1) * NB, :] = rows[:, i * NB : (i + 1) * NB].T
    outward = [pltpu.make_async_copy(separators, separators_hbm, out_sem.at[0])]
    outward[0].start()
    for k in range(0, LB, 2):
        inward[k].wait()
        inward[k + 1].wait()
        terms = mm(low, jnp.concatenate([weights[k], weights[k + 1]], axis=1))
        for j in range(2):
            value = base[k + j] - terms[:, j * NB : (j + 1) * NB]
            local[(k + j) * NB : (k + j + 1) * NB, :] = value.T
        span = pl.ds(k * NB, 2 * NB)
        outward.append(
            pltpu.make_async_copy(local.at[span], local_hbm.at[span], out_sem.at[1 + k // 2])
        )
        outward[-1].start()
    for copy in outward:
        copy.wait()


def shape(dims, dtype=F32):
    return jax.ShapeDtypeStruct(dims, dtype)


def on_device(
    local_right,
    local_inverse,
    local_below,
    local_parent,
    local_coupling,
    separator_right,
    separator_inverse,
    separator_lower,
    parent_coupling,
):
    rows = local_right.shape[2]
    columns = local_right.shape[3]
    half = columns // 2
    height = LEV * S
    leaves = lax.axis_size("leaf")
    reps = lax.axis_size("rep")
    chips = [[2 * i + c for i in range(leaves // 2)] for c in range(2)]
    pairs = [(i, i ^ 1) for i in range(leaves)]
    place = jnp.stack([lax.axis_index("leaf"), lax.axis_index("rep")]).astype(jnp.int32)
    right = local_right.reshape(LB, NB, columns)
    coupling = local_coupling.reshape(height, rows)

    forward_t, weights, factors, keep, send = pl.pallas_call(
        forward_kernel,
        out_shape=(
            pltpu.HBM((LB, columns, NB), F32),
            pltpu.HBM((LB, height, NB), BF16),
            pltpu.HBM((LB, 2 * NB, NB), BF16),
            shape((half, height)),
            shape((half, height)),
        ),
        in_specs=[SMEM] + [HBM] * 6,
        out_specs=(HBM,) * 3 + (VMEM,) * 2,
        scratch_shapes=[
            pltpu.VMEM((LB, columns, NB), F32),
            pltpu.VMEM((LB, height, NB), BF16),
            pltpu.VMEM((LB, 2 * NB, NB), BF16),
            pltpu.SMEM((1, 1, LB - 1), jnp.int32),
            pltpu.VMEM((LB, NB, columns), F32),
            pltpu.VMEM((LB, NB, NB), BF16),
            pltpu.VMEM((LB - 1, NB, NB), BF16),
            pltpu.VMEM((height, rows), BF16),
            pltpu.VMEM((LEV, S, columns), F32),
            pltpu.VMEM((LB, NB, columns), F32),
            pltpu.VMEM((rows, columns), BF16),
            pltpu.SemaphoreType.DMA((12,)),
            pltpu.SemaphoreType.DMA((LB + 2,)),
        ],
        compiler_params=limit(30),
        name="forward",
    )(place, *in_hbm(local_parent, right, local_inverse[0, 0], local_below[0, 0], coupling, separator_right))

    total = keep + lax.ppermute(send, "leaf", pairs)
    parts = lax.all_to_all(total.reshape(reps, CH, height), "rep", 0, 0, tiled=True)
    place_after, _ = lax.optimization_barrier((place, total))
    full, product = pl.pallas_call(
        separator_kernel,
        out_shape=(pltpu.HBM((8, S, S), BF16), shape((7, S, S), BF16)),
        in_specs=[SMEM] + [HBM] * 3,
        out_specs=(HBM, VMEM),
        scratch_shapes=[
            pltpu.VMEM((8, S, S), BF16),
            pltpu.VMEM((8, SB, NB, NB), BF16),
            pltpu.VMEM((8, S, S), BF16),
            pltpu.VMEM((7, S, S), BF16),
            pltpu.SemaphoreType.DMA((9,)),
            pltpu.SemaphoreType.DMA((8,)),
        ],
        compiler_params=limit(16),
        cost_estimate=pl.CostEstimate(flops=6 * 10**9, transcendentals=0, bytes_accessed=2 * 10**7),
        name="separator",
    )(place_after, *in_hbm(separator_inverse, separator_lower, parent_coupling))

    parts, full, product = lax.optimization_barrier((parts, full, product))
    summed, residue = pl.pallas_call(
        level_kernel,
        out_shape=(shape((leaves // 2, CH, height - S)), shape((CH, S))),
        in_specs=[VMEM] * 2,
        out_specs=(VMEM, VMEM),
        compiler_params=limit(8),
        name="level",
    )(parts, product)
    gathered = lax.all_to_all(summed, "leaf", 0, 0, axis_index_groups=chips, tiled=True)
    forward_t, _ = lax.optimization_barrier((forward_t, residue))
    base = pl.pallas_call(
        base_kernel,
        out_shape=shape((LB, columns, NB)),
        in_specs=[HBM] * 3,
        out_specs=VMEM,
        scratch_shapes=[
            pltpu.SMEM((1, 1, LB - 1), jnp.int32),
            pltpu.VMEM((LB, columns, NB), F32),
            pltpu.VMEM((LB, 2 * NB, NB), BF16),
            pltpu.VMEM((LB, columns, NB), BF16),
            pltpu.SemaphoreType.DMA((3,)),
        ],
        compiler_params=limit(8),
        cost_estimate=pl.CostEstimate(flops=6 * 10**9, transcendentals=0, bytes_accessed=2 * 10**7),
        name="base",
    )(*in_hbm(local_parent, forward_t, factors))
    gathered, base = lax.optimization_barrier((gathered, base))

    solved = pl.pallas_call(
        tree_kernel,
        out_shape=shape((reps, CH, height)),
        in_specs=[SMEM, VMEM, VMEM, HBM, VMEM],
        out_specs=VMEM,
        scratch_shapes=[
            pltpu.VMEM((4, CH, S), F32),
            pltpu.VMEM((2, CH, S), F32),
            pltpu.VMEM((LEV, S, S), BF16),
            pltpu.SemaphoreType.DMA((LEV,)),
        ],
        compiler_params=limit(8),
        name="tree",
    )(place, gathered, residue, *in_hbm(full), product)
    mine = lax.all_to_all(solved, "rep", 0, 0, tiled=True).reshape(half, height)
    other = lax.ppermute(mine, "leaf", pairs)
    local, separators = pl.pallas_call(
        finish_kernel,
        out_shape=(pltpu.HBM((rows, columns), F32), pltpu.HBM((height, columns), F32)),
        in_specs=[SMEM] + [VMEM] * 3 + [HBM],
        out_specs=(HBM, HBM),
        scratch_shapes=[
            pltpu.VMEM((LB, height, NB), BF16),
            pltpu.VMEM((rows, columns), F32),
            pltpu.VMEM((height, columns), F32),
            pltpu.SemaphoreType.DMA((LB,)),
            pltpu.SemaphoreType.DMA((LB // 2 + 1,)),
        ],
        compiler_params=limit(16),
        name="finish",
    )(place, mine, other, base, *in_hbm(weights))
    return (local[None, None], separators.reshape(1, LEV, S, columns))


def solution(mesh):
    in_specs = (
        P("leaf", "rep", None, None),
        P("leaf", "rep", None, None, None),
        P("leaf", "rep", None, None, None),
        P("leaf", "rep", None),
        P("leaf", "rep", None, None, None),
        P(),
        P(),
        P(),
        P(),
    )
    out_specs = (P("leaf", "rep", None, None), P("leaf", None, None, None))
    return jax.shard_map(
        on_device, mesh=mesh, in_specs=in_specs, out_specs=out_specs, check_vma=False
    )
```

time: 109 us -> 70 us (0.64)
  local copies, waits for them, and re-layouts: 29.1 us -> 0 us
  Pallas kernels: 46.7 us -> 32.4 us
  waiting for transfers between devices: 2.7 us -> 6.61 us
    unnamed x38 -> x0, local copies, waits for them, and re-layouts: 28.4 us -> none
    pallas_call x5 -> x6, Pallas kernels: 46.7 us -> 32.4 us  [the longest x1 11 us: on_device(): pl.pallas_call(forward_kernel, out_shape=(pltpu.HBM((LB, columns, NB), F3...]
    all_to_all x1, waiting for transfers between devices: 0.01 us -> 3.91 us  [on_device(): lax.all_to_all(summed, 'leaf', 0, 0, axis_index_groups=chips, tiled=True)]
  transfers between devices with their start and end apart: 4 -> 4, of which waited for: 2 -> 3; matrix products, arithmetic and copies ran while one was open for 0% -> 0% of each run, Pallas kernels for 30% -> 16%
where the time goes in v2:
time: 70 us; the launch traced here: 69.6 us
  Pallas kernels  32.4 us (46%)
  starting transfers between devices  17.4 us (25%)
  blocking collectives  11.5 us (16%)
  waiting for transfers between devices  6.61 us (9%)
  other arithmetic  0.86 us (1%)
  between operations  0.84 us (1%)
    all_to_all x1, blocking collectives, on_device(): mine = lax.all_to_all(solved, 'rep', 0, 0, tiled=True).reshape(half, height)  11.5 us
    pallas_call x1, Pallas kernels, on_device(): pl.pallas_call(forward_kernel, out_shape=(pltpu.HBM((LB, columns, NB), F3...  11 us
    pallas_call x1, Pallas kernels, on_device(): pl.pallas_call(separator_kernel, out_shape=(pltpu.HBM((8, S, S), BF16), s...  7.1 us
    all_to_all x1, starting transfers between devices, on_device(): lax.all_to_all(summed, 'leaf', 0, 0, axis_index_groups=chips, tiled=True)  6.36 us
    pallas_call x1, Pallas kernels, on_device(): pl.pallas_call(finish_kernel, out_shape=(pltpu.HBM((rows, columns), F32),...  6.21 us
    all_to_all x1, starting transfers between devices, on_device(): lax.all_to_all(total.reshape(reps, CH, height), 'rep', 0, 0, tiled=True)  6.13 us
    pallas_call x1, Pallas kernels, on_device(): pl.pallas_call(base_kernel, out_shape=shape((LB, columns, NB)), in_specs=...  3.98 us
    all_to_all x1, waiting for transfers between devices, on_device(): lax.all_to_all(summed, 'leaf', 0, 0, axis_index_groups=chips, tiled=True)  3.91 us
  transfers between devices with their start and end apart: 4, of which 3 were waited for; matrix products, arithmetic and copies ran while one was open for 0% of the time, Pallas kernels for 16%

profile of v2, /device:TPU:1, one launch (start us, length us, event | category | flops | bytes accessed | tf_op | source)
XLA Modules:
  0.0 69.6 jit_solution(9921574726770380077)
XLA Ops:
  0.6 0.1 pad_add_fusion.place
  0.7 11.0 %forward.1 = (f32[16,128,128]{2,1,0:T(8,128)}, bf16[16,1536,128]{2,1,0:T(8,128)(2,1)}, bf16[16,256,128]{2,1,0:T(8,128)(2,1)}, f32[64,1536]{1,0:T(8,128)S(1)}, f32[64,1536]{1,0:T(8,128)S(1)}) custom-call(s32[2]{0:T(128)S(1)} %pad_add_fusion.place, s32[1,1,15]{2,1,0:T(1,128)} %parent_hbm.3, f32[16,128,128]{2,1,0:T(8,128)} %bitcast.13, ...), custom_call_target="tpu_custom_call" | custom-call | tf_op jit(solution)/shard_map/forward/pallas_call | solution.py:322
  11.7 1.5 %collective-permute-start = (f32[64,1536]{1,0:T(8,128)S(1)}, f32[64,1536]{1,0:T(8,128)S(1)}, u32[]{:S(2)}, u32[]{:S(2)}) collective-permute-start(f32[64,1536]{1,0:T(8,128)S(1)} %get-tuple-element.21), channel_id=1, source_target_pairs={{0,8},{8,0},{16,24},{24,16},{32,40},{40,32},{48,56},{56,48},{64,72... | collective-permute-start | bytes 1179656 | tf_op jit(solution)/shard_map/ppermute | solution.py:352
  13.2 1.3 %collective-permute-done = f32[64,1536]{1,0:T(8,128)S(1)} collective-permute-done((f32[64,1536]{1,0:T(8,128)S(1)}, f32[64,1536]{1,0:T(8,128)S(1)}, u32[]{:S(2)}, u32[]{:S(2)}) %collective-permute-start) | collective-permute-done | bytes 393248 | tf_op jit(solution)/shard_map/ppermute | solution.py:352
  14.5 0.8 %add.3 = f32[64,1536]{1,0:T(8,128)} add(f32[64,1536]{1,0:T(8,128)S(1)} %get-tuple-element.20, f32[64,1536]{1,0:T(8,128)S(1)} %collective-permute-done) | non-fusion elementwise | flops 98304 | bytes 1179648 | tf_op jit(solution)/shard_map/add | solution.py:352
  15.3 6.1 %all-to-all-start = ((f32[8,8,1536]{2,1,0:T(8,128)}), f32[8,8,1536]{2,1,0:T(8,128)S(1)}, u32[]{:S(2)}, u32[]{:S(2)}) async-start(f32[8,8,1536]{2,1,0:T(8,128)} %bitcast.6), calls=%async_computation | async-start | bytes 786432 | tf_op jit(solution)/shard_map/all_to_all | solution.py:353
  21.5 7.1 %separator.1 = (bf16[8,384,384]{2,1,0:T(8,128)(2,1)}, bf16[7,384,384]{2,1,0:T(8,128)(2,1)S(1)}) custom-call(s32[2]{0:T(128)S(1)} %pad_add_fusion.place, bf16[15,3,128,128]{3,2,1,0:T(8,128)(2,1)} %inverse_hbm.1, bf16[15,384,384]{2,1,0:T(8,128)(2,1)} %lower_hbm.1, bf16[14,384,384]{2,1,0:T(8,128)(2,1)} %coupling_hbm.1), custom_call_target="tpu_custom_call" | custom-call | flops 6000000000 | bytes 20000000 | tf_op jit(solution)/shard_map/separator/pallas_call | solution.py:355
  28.6 0.0 all-to-all-done.parts
  28.6 0.9 %level.1 = (f32[8,8,1152]{2,1,0:T(8,128)}, f32[8,384]{1,0:T(8,128)S(1)}) custom-call(f32[8,8,1536]{2,1,0:T(8,128)S(1)} %all-to-all-done.parts, bf16[7,384,384]{2,1,0:T(8,128)(2,1)S(1)} %get-tuple-element.26.product), custom_call_target="tpu_custom_call" | custom-call | tf_op jit(solution)/shard_map/level/pallas_call | solution.py:374
  29.5 6.4 %all-to-all-start.1 = ((f32[8,8,1152]{2,1,0:T(8,128)}), f32[8,8,1152]{2,1,0:T(8,128)S(1)}, u32[]{:S(2)}, u32[]{:S(2)}) async-start(f32[8,8,1152]{2,1,0:T(8,128)} %get-tuple-element.27), calls=%async_computation.1 | async-start | bytes 589824 | tf_op jit(solution)/shard_map/all_to_all | solution.py:382
  35.9 4.0 %base.1 = f32[16,128,128]{2,1,0:T(8,128)S(1)} custom-call(s32[1,1,15]{2,1,0:T(1,128)} %parent_hbm.3, f32[16,128,128]{2,1,0:T(8,128)} %get-tuple-element.30.forward_hbm, bf16[16,256,128]{2,1,0:T(8,128)(2,1)} %get-tuple-element.31.factors_hbm), custom_call_target="tpu_custom_call" | custom-call | flops 6000000000 | bytes 20000000 | tf_op jit(solution)/shard_map/base/pallas_call | solution.py:384
  39.9 3.9 %all-to-all-done.1.gathered = f32[8,8,1152]{2,1,0:T(8,128)S(1)} async-done(((f32[8,8,1152]{2,1,0:T(8,128)}), f32[8,8,1152]{2,1,0:T(8,128)S(1)}, u32[]{:S(2)}, u32[]{:S(2)}) %all-to-all-start.1) | async-done | bytes 294944 | tf_op jit(solution)/shard_map/all_to_all | solution.py:382
  43.8 3.2 %tree.1 = f32[8,8,1536]{2,1,0:T(8,128)S(1)} custom-call(s32[2]{0:T(128)S(1)} %pad_add_fusion.place, f32[8,8,1152]{2,1,0:T(8,128)S(1)} %all-to-all-done.1.gathered, f32[8,384]{1,0:T(8,128)S(1)} %get-tuple-element.29.residue, bf16[8,384,384]{2,1,0:T(8,128)(2,1)} %get-tuple-element.33.full_hbm, bf16[7,384,384]{2,1,0:T(8,128)(2,1)S(1)} %get-tuple-element.26.product), custom_call_target="tpu_custom_call" | custom-call | tf_op jit(solution)/shard_map/tree/pallas_call | solution.py:402
  47.0 11.5 %all_to_all.15 = f32[8,8,1536]{2,1,0:T(8,128)S(1)} all-to-all(f32[8,8,1536]{2,1,0:T(8,128)S(1)} %tree.1), channel_id=1, replica_groups=mesh['leaf'=16,'rep'=8] {'rep'}, dimensions={0} | all-to-all | bytes 786432 | tf_op jit(solution)/shard_map/all_to_all | solution.py:416
  58.5 3.4 %collective-permute-start.1 = (f32[64,1536]{1,0:T(8,128)S(1)}, f32[64,1536]{1,0:T(8,128)S(1)}, u32[]{:S(2)}, u32[]{:S(2)}) collective-permute-start(f32[64,1536]{1,0:T(8,128)S(1)} %bitcast.10), channel_id=1, source_target_pairs={{0,8},{8,0},{16,24},{24,16},{32,40},{40,32},{48,56},{56,48},{64,72... | collective-permute-start | bytes 1179656 | tf_op jit(solution)/shard_map/ppermute | solution.py:417
  61.9 1.3 %collective-permute-done.1.other = f32[64,1536]{1,0:T(8,128)S(1)} collective-permute-done((f32[64,1536]{1,0:T(8,128)S(1)}, f32[64,1536]{1,0:T(8,128)S(1)}, u32[]{:S(2)}, u32[]{:S(2)}) %collective-permute-start.1) | collective-permute-done | bytes 393248 | tf_op jit(solution)/shard_map/ppermute | solution.py:417
  63.3 6.2 %finish.1 = (f32[2048,128]{1,0:T(8,128)}, f32[1536,128]{1,0:T(8,128)}) custom-call(s32[2]{0:T(128)S(1)} %pad_add_fusion.place, f32[64,1536]{1,0:T(8,128)S(1)} %bitcast.11, f32[64,1536]{1,0:T(8,128)S(1)} %collective-permute-done.1.other, f32[16,128,128]{2,1,0:T(8,128)S(1)} %base.1, bf16[16,1536,128]{2,1,0:T(8,128)(2,1)} %get-tuple-element.35.weights_hbm), custom_call_target="tpu_custom_call" | custom-call | tf_op jit(solution)/shard_map/finish/pallas_call | solution.py:418
Async XLA Ops:
  11.7 2.8 %collective-permute-start = (f32[64,1536]{1,0:T(8,128)S(1)}, f32[64,1536]{1,0:T(8,128)S(1)}, u32[]{:S(2)}, u32[]{:S(2)}) collective-permute-start(f32[64,1536]{1,0:T(8,128)S(1)} %get-tuple-element.21), channel_id=1, source_target_pairs={{0,8},{8,0},{16,24},{24,16},{32,40},{40,32},{48,56},{56,48},{64,72... | collective-permute-start | bytes 1179656 | tf_op jit(solution)/shard_map/ppermute | solution.py:352
  15.3 13.2 %all-to-all-start = ((f32[8,8,1536]{2,1,0:T(8,128)}), f32[8,8,1536]{2,1,0:T(8,128)S(1)}, u32[]{:S(2)}, u32[]{:S(2)}) async-start(f32[8,8,1536]{2,1,0:T(8,128)} %bitcast.6), calls=%async_computation | async-start | bytes 786432 | tf_op jit(solution)/shard_map/all_to_all | solution.py:353
  29.5 14.3 %all-to-all-start.1 = ((f32[8,8,1152]{2,1,0:T(8,128)}), f32[8,8,1152]{2,1,0:T(8,128)S(1)}, u32[]{:S(2)}, u32[]{:S(2)}) async-start(f32[8,8,1152]{2,1,0:T(8,128)} %get-tuple-element.27), calls=%async_computation.1 | async-start | bytes 589824 | tf_op jit(solution)/shard_map/all_to_all | solution.py:382
  58.5 4.7 %collective-permute-start.1 = (f32[64,1536]{1,0:T(8,128)S(1)}, f32[64,1536]{1,0:T(8,128)S(1)}, u32[]{:S(2)}, u32[]{:S(2)}) collective-permute-start(f32[64,1536]{1,0:T(8,128)S(1)} %bitcast.10), channel_id=1, source_target_pairs={{0,8},{8,0},{16,24},{24,16},{32,40},{40,32},{48,56},{56,48},{64,72... | collective-permute-start | bytes 1179656 | tf_op jit(solution)/shard_map/ppermute | solution.py:417

commit v3 on v2

--- a/solution.py
+++ b/solution.py
@@ -40,8 +40,8 @@
 
 def forward_kernel(
     place, parent_hbm, right_hbm, inverse_hbm, below_hbm, coupling_hbm, sepright_hbm,
-    forward_hbm, weights_hbm, factors_hbm, keep, send,
-    forward_t, weights, factors,
+    weights_hbm, base_hbm, keep, send,
+    forward_t, weights, factors, base, base_low,
     parent, right, inverse, below, coupling, sepright, acc, rounded, sem, out_sem,
 ):
     leaf, rep = place[0], place[1]
@@ -76,15 +76,14 @@
             factors[k, NB:, :] = (-mm(below[k], inverse[k])).astype(BF16)
         else:
             factors[k, NB:, :] = jnp.zeros((NB, NB), BF16)
-    outward = [pltpu.make_async_copy(factors, factors_hbm, out_sem.at[LB])]
-    outward[0].start()
+    outward = []
     rows = coupling.shape[0] // 2
     for i in range(LB):
         k = i
         result = mm(inverse[k], (right[k] - acc[k]).astype(BF16))
         low = result.astype(BF16)
         rounded[k * NB : (k + 1) * NB, :] = low
-        forward_t[k] = result.T
+        forward_t[k] = result.T.astype(BF16)
         if k < LB - 1:
             p = parent[0, 0, k]
             acc[p] = acc[p] + mm(below[k], low)
@@ -103,16 +102,25 @@
             weights[k] = mm(own, inverse[k]).astype(BF16)
         outward.append(pltpu.make_async_copy(weights.at[k], weights_hbm.at[k], out_sem.at[k]))
         outward[-1].start()
-    outward.append(pltpu.make_async_copy(forward_t, forward_hbm, out_sem.at[LB + 1]))
-    outward[-1].start()
     for copy in others:
         copy.wait()
     values = rounded[...]
     first_core = lax.rem(leaf, 2) == 0
+    remaining = list(reversed(range(LB)))
     for h in range(1, LEV + 1):
         owner = jnp.logical_and(rep == 0, lax.rem(leaf, 1 << h) == 0)
         flag = jnp.where(owner, 1.0, 0.0).astype(F32)
         for i in range(SB):
+            for k in remaining[:2]:
+                value = forward_t[k]
+                if k < LB - 1:
+                    value = jnp.concatenate([value, base_low[parent[0, 0, k]]], axis=1)
+                    value = mm(value, factors[k])
+                else:
+                    value = mm(value, inverse[k])
+                base[k] = value
+                base_low[k] = value.astype(BF16)
+            remaining = remaining[2:]
             at = (h - 1) * S + i * NB
             block = flag * sepright[h - 1, i * NB : (i + 1) * NB, :] - mm(
                 coupling[at : at + NB, :], values
@@ -121,6 +129,8 @@
             upper, lower = block[: NB // 2], block[NB // 2 :]
             keep[:, at : at + NB] = jnp.where(first_core, upper, lower)
             send[:, at : at + NB] = jnp.where(first_core, lower, upper)
+    outward.append(pltpu.make_async_copy(base, base_hbm, out_sem.at[LB]))
+    outward[-1].start()
     for copy in outward:
         copy.wait()
 
@@ -193,36 +203,20 @@
         out[j, :, S:] = total[:, 2 * S :]
 
 
-def base_kernel(
-    parent_hbm, forward_hbm, factors_hbm, base, parent, forward_t, factors, base_low, sem
+def tree_kernel(
+    place, gathered, residue, full_hbm, product, weights_hbm, base_hbm,
+    out, weights, base, res2, res3, full, sem,
 ):
-    copies = [
-        pltpu.make_async_copy(parent_hbm, parent, sem.at[0]),
-        pltpu.make_async_copy(factors_hbm, factors, sem.at[1]),
-        pltpu.make_async_copy(forward_hbm, forward_t, sem.at[2]),
-    ]
-    for copy in copies:
-        copy.start()
-    for copy in copies:
-        copy.wait()
-    for k in reversed(range(LB)):
-        value = forward_t[k].astype(BF16)
-        if k < LB - 1:
-            value = jnp.concatenate([value, base_low[parent[0, 0, k]]], axis=1)
-            value = mm(value, factors[k])
-        else:
-            value = mm(value, factors[k, :NB, :])
-        base[k] = value
-        base_low[k] = value.astype(BF16)
-
-
-def tree_kernel(place, gathered, residue, full_hbm, product, out, res2, res3, full, sem):
     leaf = place[0]
     copies = []
     for h in range(1, LEV + 1):
         number = first_number(1) if h == 1 else first_number(h) + (leaf >> h)
         copies.append(pltpu.make_async_copy(full_hbm.at[number], full.at[h - 1], sem.at[h - 1]))
-    for copy in copies:
+    fetched = [
+        pltpu.make_async_copy(weights_hbm, weights, sem.at[LEV]),
+        pltpu.make_async_copy(base_hbm, base, sem.at[LEV + 1]),
+    ]
+    for copy in copies + fetched:
         copy.start()
     span = [slice(h * S, (h + 1) * S) for h in range(LEV)]
     residues = []
@@ -257,17 +251,13 @@
         above = value.astype(BF16)
         for j in range(out.shape[0]):
             out[j, :, span[h - 1]] = value
+    for copy in fetched:
+        copy.wait()
 
 
 def finish_kernel(
-    place, mine, other, base, weights_hbm, local_hbm, separators_hbm,
-    weights, local, separators, sem, out_sem,
+    place, mine, other, base, weights, local_hbm, separators_hbm, local, separators, out_sem
 ):
-    inward = [
-        pltpu.make_async_copy(weights_hbm.at[k], weights.at[k], sem.at[k]) for k in range(LB)
-    ]
-    for copy in inward:
-        copy.start()
     first_core = lax.rem(place[0], 2) == 0
     a, b = mine[...], other[...]
     rows = jnp.concatenate([jnp.where(first_core, a, b), jnp.where(first_core, b, a)], axis=0)
@@ -277,8 +267,6 @@
     outward = [pltpu.make_async_copy(separators, separators_hbm, out_sem.at[0])]
     outward[0].start()
     for k in range(0, LB, 2):
-        inward[k].wait()
-        inward[k + 1].wait()
         terms = mm(low, jnp.concatenate([weights[k], weights[k + 1]], axis=1))
         for j in range(2):
             value = base[k + j] - terms[:, j * NB : (j + 1) * NB]
@@ -319,21 +307,22 @@
     right = local_right.reshape(LB, NB, columns)
     coupling = local_coupling.reshape(height, rows)
 
-    forward_t, weights, factors, keep, send = pl.pallas_call(
+    weights, base, keep, send = pl.pallas_call(
         forward_kernel,
         out_shape=(
+            pltpu.HBM((LB, height, NB), BF16),
             pltpu.HBM((LB, columns, NB), F32),
-            pltpu.HBM((LB, height, NB), BF16),
-            pltpu.HBM((LB, 2 * NB, NB), BF16),
             shape((half, height)),
             shape((half, height)),
         ),
         in_specs=[SMEM] + [HBM] * 6,
-        out_specs=(HBM,) * 3 + (VMEM,) * 2,
+        out_specs=(HBM,) * 2 + (VMEM,) * 2,
         scratch_shapes=[
-            pltpu.VMEM((LB, columns, NB), F32),
+            pltpu.VMEM((LB, columns, NB), BF16),
             pltpu.VMEM((LB, height, NB), BF16),
             pltpu.VMEM((LB, 2 * NB, NB), BF16),
+            pltpu.VMEM((LB, columns, NB), F32),
+            pltpu.VMEM((LB, columns, NB), BF16),
             pltpu.SMEM((1, 1, LB - 1), jnp.int32),
             pltpu.VMEM((LB, NB, columns), F32),
             pltpu.VMEM((LB, NB, NB), BF16),
@@ -343,7 +332,7 @@
             pltpu.VMEM((LB, NB, columns), F32),
             pltpu.VMEM((rows, columns), BF16),
             pltpu.SemaphoreType.DMA((12,)),
-            pltpu.SemaphoreType.DMA((LB + 2,)),
+            pltpu.SemaphoreType.DMA((LB + 1,)),
         ],
         compiler_params=limit(30),
         name="forward",
@@ -380,56 +369,39 @@
         name="level",
     )(parts, product)
     gathered = lax.all_to_all(summed, "leaf", 0, 0, axis_index_groups=chips, tiled=True)
-    forward_t, _ = lax.optimization_barrier((forward_t, residue))
-    base = pl.pallas_call(
-        base_kernel,
-        out_shape=shape((LB, columns, NB)),
-        in_specs=[HBM] * 3,
-        out_specs=VMEM,
-        scratch_shapes=[
-            pltpu.SMEM((1, 1, LB - 1), jnp.int32),
+    solved, weights, base = pl.pallas_call(
+        tree_kernel,
+        out_shape=(
+            shape((reps, CH, height)),
+            pltpu.VMEM((LB, height, NB), BF16),
             pltpu.VMEM((LB, columns, NB), F32),
-            pltpu.VMEM((LB, 2 * NB, NB), BF16),
-            pltpu.VMEM((LB, columns, NB), BF16),
-            pltpu.SemaphoreType.DMA((3,)),
-        ],
-        compiler_params=limit(8),
-        cost_estimate=pl.CostEstimate(flops=6 * 10**9, transcendentals=0, bytes_accessed=2 * 10**7),
-        name="base",
-    )(*in_hbm(local_parent, forward_t, factors))
-    gathered, base = lax.optimization_barrier((gathered, base))
-
-    solved = pl.pallas_call(
-        tree_kernel,
-        out_shape=shape((reps, CH, height)),
-        in_specs=[SMEM, VMEM, VMEM, HBM, VMEM],
-        out_specs=VMEM,
+        ),
+        in_specs=[SMEM, VMEM, VMEM, HBM, VMEM, HBM, HBM],
+        out_specs=(VMEM,) * 3,
         scratch_shapes=[
             pltpu.VMEM((4, CH, S), F32),
             pltpu.VMEM((2, CH, S), F32),
             pltpu.VMEM((LEV, S, S), BF16),
-            pltpu.SemaphoreType.DMA((LEV,)),
+            pltpu.SemaphoreType.DMA((LEV + 2,)),
         ],
         compiler_params=limit(8),
         name="tree",
-    )(place, gathered, residue, *in_hbm(full), product)
+    )(place, gathered, residue, *in_hbm(full), product, *in_hbm(weights, base))
     mine = lax.all_to_all(solved, "rep", 0, 0, tiled=True).reshape(half, height)
     other = lax.ppermute(mine, "leaf", pairs)
     local, separators = pl.pallas_call(
         finish_kernel,
         out_shape=(pltpu.HBM((rows, columns), F32), pltpu.HBM((height, columns), F32)),
-        in_specs=[SMEM] + [VMEM] * 3 + [HBM],
+        in_specs=[SMEM] + [VMEM] * 4,
         out_specs=(HBM, HBM),
         scratch_shapes=[
-            pltpu.VMEM((LB, height, NB), BF16),
             pltpu.VMEM((rows, columns), F32),
             pltpu.VMEM((height, columns), F32),
-            pltpu.SemaphoreType.DMA((LB,)),
             pltpu.SemaphoreType.DMA((LB // 2 + 1,)),
         ],
         compiler_params=limit(16),
         name="finish",
-    )(place, mine, other, base, *in_hbm(weights))
+    )(place, mine, other, base, weights)
     return (local[None, None], separators.reshape(1, LEV, S, columns))
 
 

time: 70 us -> 67.8 us (0.969)
  blocking collectives: 11.5 us -> 25.4 us
  starting transfers between devices: 17.4 us -> 11.4 us
  Pallas kernels: 32.4 us -> 26.5 us
  waiting for transfers between devices: 6.61 us -> 2.7 us
    all_to_all x0 -> x1, blocking collectives: none -> 14.2 us  [on_device(): lax.all_to_all(summed, 'leaf', 0, 0, axis_index_groups=chips, tiled=True)]
    all_to_all x1 -> x0, starting transfers between devices: 6.36 us -> none  [on_device(): lax.all_to_all(summed, 'leaf', 0, 0, axis_index_groups=chips, tiled=True)]
    all_to_all x1 -> x0, waiting for transfers between devices: 3.91 us -> none  [on_device(): lax.all_to_all(summed, 'leaf', 0, 0, axis_index_groups=chips, tiled=True)]
    pallas_call x1, Pallas kernels: 6.21 us -> 2.44 us  [on_device(): pl.pallas_call(finish_kernel, out_shape=(pltpu.HBM((rows, columns), F32),...]
    pallas_call x3 -> x2, Pallas kernels: 18.2 us -> 16.8 us  [the longest x1 12.5 us: on_device(): pl.pallas_call(forward_kernel, out_shape=(pltpu.HBM((LB, height, NB), BF1...]
    pallas_call x1, Pallas kernels: 0.93 us -> 0.19 us  [on_device(): pl.pallas_call(level_kernel, out_shape=(shape((leaves // 2, CH, height -...]
  transfers between devices with their start and end apart: 4 -> 3, of which waited for: 3 -> 2; matrix products, arithmetic and copies ran while one was open for 0% -> 0% of each run, Pallas kernels for 16% -> 11%
where the time goes in v3:
time: 67.8 us; the launch traced here: 67.5 us
  Pallas kernels  26.5 us (39%)
  blocking collectives  25.4 us (37%)
  starting transfers between devices  11.4 us (17%)
  waiting for transfers between devices  2.7 us (4%)
  other arithmetic  0.86 us (1%)
    all_to_all x1, blocking collectives, on_device(): lax.all_to_all(summed, 'leaf', 0, 0, axis_index_groups=chips, tiled=True)  14.2 us
    pallas_call x1, Pallas kernels, on_device(): pl.pallas_call(forward_kernel, out_shape=(pltpu.HBM((LB, height, NB), BF1...  12.5 us
    all_to_all x1, blocking collectives, on_device(): mine = lax.all_to_all(solved, 'rep', 0, 0, tiled=True).reshape(half, height)  11.2 us
    pallas_call x1, Pallas kernels, on_device(): pl.pallas_call(separator_kernel, out_shape=(pltpu.HBM((8, S, S), BF16), s...  7.11 us
    all_to_all x1, starting transfers between devices, on_device(): lax.all_to_all(total.reshape(reps, CH, height), 'rep', 0, 0, tiled=True)  6.13 us
    pallas_call x1, Pallas kernels, on_device(): pl.pallas_call(tree_kernel, out_shape=(shape((reps, CH, height)), pltpu.V...  4.29 us
    ppermute x1, starting transfers between devices, on_device(): other = lax.ppermute(mine, 'leaf', pairs)  3.74 us
    pallas_call x1, Pallas kernels, on_device(): pl.pallas_call(finish_kernel, out_shape=(pltpu.HBM((rows, columns), F32),...  2.44 us
  transfers between devices with their start and end apart: 3, of which 2 were waited for; matrix products, arithmetic and copies ran while one was open for 0% of the time, Pallas kernels for 11%

profile of v3, /device:TPU:1, one launch (start us, length us, event | category | flops | bytes accessed | tf_op | source)
XLA Modules:
  0.0 67.5 jit_solution(1760618883849365162)
XLA Ops:
  0.6 0.1 pad_add_fusion.place
  0.7 12.5 %forward.1 = (bf16[16,1536,128]{2,1,0:T(8,128)(2,1)}, f32[16,128,128]{2,1,0:T(8,128)}, f32[64,1536]{1,0:T(8,128)S(1)}, f32[64,1536]{1,0:T(8,128)S(1)}) custom-call(s32[2]{0:T(128)S(1)} %pad_add_fusion.place, s32[1,1,15]{2,1,0:T(1,128)} %parent_hbm.1, f32[16,128,128]{2,1,0:T(8,128)} %bitcast.13, bf16[16,128,128]{2,1,0:T(8,128)(2,1)} %bitcast.14, ...), custom_call_target="tpu_custom_call" | custom-call | tf_op jit(solution)/shard_map/forward/pallas_call | solution.py:310
  13.2 1.5 %collective-permute-start = (f32[64,1536]{1,0:T(8,128)S(1)}, f32[64,1536]{1,0:T(8,128)S(1)}, u32[]{:S(2)}, u32[]{:S(2)}) collective-permute-start(f32[64,1536]{1,0:T(8,128)S(1)} %get-tuple-element.20), channel_id=1, source_target_pairs={{0,8},{8,0},{16,24},{24,16},{32,40},{40,32},{48,56},{56,48},{64,72... | collective-permute-start | bytes 1179656 | tf_op jit(solution)/shard_map/ppermute | solution.py:341
  14.7 1.3 %collective-permute-done = f32[64,1536]{1,0:T(8,128)S(1)} collective-permute-done((f32[64,1536]{1,0:T(8,128)S(1)}, f32[64,1536]{1,0:T(8,128)S(1)}, u32[]{:S(2)}, u32[]{:S(2)}) %collective-permute-start) | collective-permute-done | bytes 393248 | tf_op jit(solution)/shard_map/ppermute | solution.py:341
  16.1 0.8 %add.3 = f32[64,1536]{1,0:T(8,128)} add(f32[64,1536]{1,0:T(8,128)S(1)} %get-tuple-element.19, f32[64,1536]{1,0:T(8,128)S(1)} %collective-permute-done) | non-fusion elementwise | flops 98304 | bytes 1179648 | tf_op jit(solution)/shard_map/add | solution.py:341
  16.9 6.1 %all-to-all-start = ((f32[8,8,1536]{2,1,0:T(8,128)}), f32[8,8,1536]{2,1,0:T(8,128)S(1)}, u32[]{:S(2)}, u32[]{:S(2)}) async-start(f32[8,8,1536]{2,1,0:T(8,128)} %bitcast.6), calls=%async_computation | async-start | bytes 786432 | tf_op jit(solution)/shard_map/all_to_all | solution.py:342
  23.0 7.1 %separator.1 = (bf16[8,384,384]{2,1,0:T(8,128)(2,1)}, bf16[7,384,384]{2,1,0:T(8,128)(2,1)S(1)}) custom-call(s32[2]{0:T(128)S(1)} %pad_add_fusion.place, bf16[15,3,128,128]{3,2,1,0:T(8,128)(2,1)} %inverse_hbm.1, bf16[15,384,384]{2,1,0:T(8,128)(2,1)} %lower_hbm.1, bf16[14,384,384]{2,1,0:T(8,128)(2,1)} %coupling_hbm.1), custom_call_target="tpu_custom_call" | custom-call | flops 6000000000 | bytes 20000000 | tf_op jit(solution)/shard_map/separator/pallas_call | solution.py:344
  30.1 0.0 all-to-all-done.parts
  30.1 0.2 level.1
  30.3 14.2 %all_to_all.15.gathered = f32[8,8,1152]{2,1,0:T(8,128)S(1)} all-to-all(f32[8,8,1152]{2,1,0:T(8,128)S(1)} %get-tuple-element.26), channel_id=1, replica_groups={{0,16,32,48,64,80,96,112},{8,24,40,56,72,88,104,120},{1,17,33,49,65,81,..., dimensions={0} | all-to-all | bytes 589824 | tf_op jit(solution)/shard_map/all_to_all | solution.py:371
  44.5 4.3 %tree.1 = (f32[8,8,1536]{2,1,0:T(8,128)S(1)}, bf16[16,1536,128]{2,1,0:T(8,128)(2,1)S(1)}, f32[16,128,128]{2,1,0:T(8,128)S(1)}) custom-call(s32[2]{0:T(128)S(1)} %pad_add_fusion.place, f32[8,8,1152]{2,1,0:T(8,128)S(1)} %all_to_all.15.gathered, f32[8,384]{1,0:T(8,128)S(1)} %get-tuple-element.27.residue, bf16[8,384,384]{2,1,0:T(8,128)(2,1)} %get-tuple-element.28.full_hbm, ...), custom_call_target="tpu_custom_call" | custom-call | tf_op jit(solution)/shard_map/tree/pallas_call | solution.py:372
  48.8 11.2 %all_to_all.16 = f32[8,8,1536]{2,1,0:T(8,128)S(1)} all-to-all(f32[8,8,1536]{2,1,0:T(8,128)S(1)} %get-tuple-element.31), channel_id=1, replica_groups=mesh['leaf'=16,'rep'=8] {'rep'}, dimensions={0} | all-to-all | bytes 786432 | tf_op jit(solution)/shard_map/all_to_all | solution.py:390
  60.0 3.7 %collective-permute-start.1 = (f32[64,1536]{1,0:T(8,128)S(1)}, f32[64,1536]{1,0:T(8,128)S(1)}, u32[]{:S(2)}, u32[]{:S(2)}) collective-permute-start(f32[64,1536]{1,0:T(8,128)S(1)} %bitcast.10), channel_id=1, source_target_pairs={{0,8},{8,0},{16,24},{24,16},{32,40},{40,32},{48,56},{56,48},{64,72... | collective-permute-start | bytes 1179656 | tf_op jit(solution)/shard_map/ppermute | solution.py:391
  63.8 1.3 %collective-permute-done.1.other = f32[64,1536]{1,0:T(8,128)S(1)} collective-permute-done((f32[64,1536]{1,0:T(8,128)S(1)}, f32[64,1536]{1,0:T(8,128)S(1)}, u32[]{:S(2)}, u32[]{:S(2)}) %collective-permute-start.1) | collective-permute-done | bytes 393248 | tf_op jit(solution)/shard_map/ppermute | solution.py:391
  65.1 2.4 %finish.1 = (f32[2048,128]{1,0:T(8,128)}, f32[1536,128]{1,0:T(8,128)}) custom-call(s32[2]{0:T(128)S(1)} %pad_add_fusion.place, f32[64,1536]{1,0:T(8,128)S(1)} %bitcast.11, f32[64,1536]{1,0:T(8,128)S(1)} %collective-permute-done.1.other, f32[16,128,128]{2,1,0:T(8,128)S(1)} %get-tuple-element.32.base, bf16[16,1536,128]{2,1,0:T(8,128)(2,1)S(1)} %get-tuple-element.33.weights), custom_call_target="tpu_custom_call" | custom-call | tf_op jit(solution)/shard_map/finish/pallas_call | solution.py:392
Async XLA Ops:
  13.2 2.9 %collective-permute-start = (f32[64,1536]{1,0:T(8,128)S(1)}, f32[64,1536]{1,0:T(8,128)S(1)}, u32[]{:S(2)}, u32[]{:S(2)}) collective-permute-start(f32[64,1536]{1,0:T(8,128)S(1)} %get-tuple-element.20), channel_id=1, source_target_pairs={{0,8},{8,0},{16,24},{24,16},{32,40},{40,32},{48,56},{56,48},{64,72... | collective-permute-start | bytes 1179656 | tf_op jit(solution)/shard_map/ppermute | solution.py:341
  16.9 13.2 %all-to-all-start = ((f32[8,8,1536]{2,1,0:T(8,128)}), f32[8,8,1536]{2,1,0:T(8,128)S(1)}, u32[]{:S(2)}, u32[]{:S(2)}) async-start(f32[8,8,1536]{2,1,0:T(8,128)} %bitcast.6), calls=%async_computation | async-start | bytes 786432 | tf_op jit(solution)/shard_map/all_to_all | solution.py:342
  60.0 5.1 %collective-permute-start.1 = (f32[64,1536]{1,0:T(8,128)S(1)}, f32[64,1536]{1,0:T(8,128)S(1)}, u32[]{:S(2)}, u32[]{:S(2)}) collective-permute-start(f32[64,1536]{1,0:T(8,128)S(1)} %bitcast.10), channel_id=1, source_target_pairs={{0,8},{8,0},{16,24},{24,16},{32,40},{40,32},{48,56},{56,48},{64,72... | collective-permute-start | bytes 1179656 | tf_op jit(solution)/shard_map/ppermute | solution.py:391

commit v4 on v3

v4 whole, which is shorter than its diff:
```python
import jax
import jax.numpy as jnp
from jax import lax
from jax.experimental import pallas as pl
from jax.experimental.pallas import tpu as pltpu
from jax.sharding import PartitionSpec as P

NB = 128
LB = 16
SB = 3
S = SB * NB
LEV = 4
CH = 8
F32 = jnp.float32
BF16 = jnp.bfloat16
VMEM = pl.BlockSpec(memory_space=pltpu.VMEM)
SMEM = pl.BlockSpec(memory_space=pltpu.SMEM)
HBM = pl.BlockSpec(memory_space=pltpu.HBM)


def in_hbm(*arrays):
    return [pltpu.with_memory_space_constraint(array, pltpu.HBM) for array in arrays]


def limit(mib):
    return pltpu.CompilerParams(vmem_limit_bytes=mib << 20)


def mm(a, b):
    return jnp.dot(a, b, preferred_element_type=F32)


def mm_nt(a, b):
    return lax.dot_general(a, b, (((1,), (1,)), ((), ())), preferred_element_type=F32)


def first_number(height):
    return (1 << (LEV - height)) - 1


def forward_kernel(
    place, parent_hbm, right_hbm, inverse_hbm, below_hbm, coupling_hbm, sepright_hbm,
    weights_hbm, forward_hbm, factors_hbm, keep, send,
    forward_t, weights_a, weights_b, factors,
    parent, right, inverse, below, coupling, sepright, acc, rounded, sem, out_sem,
):
    leaf, rep = place[0], place[1]
    first = [
        pltpu.make_async_copy(parent_hbm, parent, sem.at[0]),
        pltpu.make_async_copy(inverse_hbm, inverse, sem.at[1]),
        pltpu.make_async_copy(below_hbm, below, sem.at[2]),
        pltpu.make_async_copy(right_hbm, right, sem.at[3]),
    ]
    quarters = []
    for q in range(4):
        columns = pl.ds((3 - q) * 4 * NB, 4 * NB)
        quarters.append(
            pltpu.make_async_copy(
                coupling_hbm.at[:, columns], coupling.at[:, columns], sem.at[4 + q]
            )
        )
    others = []
    for h in range(1, LEV + 1):
        number = first_number(h) + (leaf >> h)
        others.append(
            pltpu.make_async_copy(sepright_hbm.at[number], sepright.at[h - 1], sem.at[7 + h])
        )
    for copy in first + quarters + others:
        copy.start()
    acc[...] = jnp.zeros_like(acc)
    for copy in first:
        copy.wait()

    factors[LB - 1, :NB, :] = inverse[LB - 1]
    factors[LB - 1, NB:, :] = jnp.zeros((NB, NB), BF16)

    def factor_step(k):
        factors[k, :NB, :] = inverse[k]
        factors[k, NB:, :] = (-mm(below[k], inverse[k])).astype(BF16)

    def forward_step(k):
        result = mm(inverse[k], (right[k] - acc[k]).astype(BF16))
        low = result.astype(BF16)
        rounded[k * NB : (k + 1) * NB, :] = low
        forward_t[k] = result.T.astype(BF16)
        if k < LB - 1:
            p = parent[0, 0, k]
            acc[p] = acc[p] + mm(below[k], low)

    outward = []
    rows = coupling.shape[0] // 2

    def weights_step(k, j):
        own = coupling[j * rows : (j + 1) * rows, k * NB : (k + 1) * NB]
        half = (weights_a, weights_b)[j]
        if k < LB - 1:
            part = jnp.concatenate([own, half[parent[0, 0, k]]], axis=1)
            half[k] = mm(part, factors[k]).astype(BF16)
        else:
            half[k] = mm(own, inverse[k]).astype(BF16)
        target = weights_hbm.at[k, pl.ds(j * rows, rows), :]
        outward.append(pltpu.make_async_copy(half.at[k], target, out_sem.at[2 * k + j]))
        outward[-1].start()

    for k in reversed(range(LB - 1)):
        factor_step(k)
    outward.append(pltpu.make_async_copy(factors, factors_hbm, out_sem.at[2 * LB]))
    outward[-1].start()
    for i in range(LB):
        if i % 4 == 0:
            quarters[i // 4].wait()
        weights_step(LB - 1 - i, 0)
        forward_step(i)
        weights_step(LB - 1 - i, 1)
    outward.append(pltpu.make_async_copy(forward_t, forward_hbm, out_sem.at[2 * LB + 1]))
    outward[-1].start()
    for copy in others:
        copy.wait()
    values = rounded[...]
    first_core = lax.rem(leaf, 2) == 0
    for h in range(1, LEV + 1):
        owner = jnp.logical_and(rep == 0, lax.rem(leaf, 1 << h) == 0)
        flag = jnp.where(owner, 1.0, 0.0).astype(F32)
        for i in range(SB):
            at = (h - 1) * S + i * NB
            block = flag * sepright[h - 1, i * NB : (i + 1) * NB, :] - mm(
                coupling[at : at + NB, :], values
            )
            block = block.T
            upper, lower = block[: NB // 2], block[NB // 2 :]
            keep[:, at : at + NB] = jnp.where(first_core, upper, lower)
            send[:, at : at + NB] = jnp.where(first_core, lower, upper)
    for copy in outward:
        copy.wait()


def separator_kernel(
    place, inverse_hbm, lower_hbm, coupling_hbm, full_hbm, product,
    full, inverse, lowerpart, coupling, sem, out_sem,
):
    shared = first_number(1)
    number = shared + (place[0] >> 1)
    low_rows, low_columns = pl.ds(NB, 2 * NB), pl.ds(0, 2 * NB)
    triangles, couplings = [], []
    for at, size, source in ((0, shared, 0), (shared, 1, number)):
        k = 3 * len(couplings)
        entries = pl.ds(source, size)
        triangles.append(
            pltpu.make_async_copy(inverse_hbm.at[entries], inverse.at[pl.ds(at, size)], sem.at[k])
        )
        triangles.append(
            pltpu.make_async_copy(
                lower_hbm.at[entries, low_rows, low_columns],
                lowerpart.at[pl.ds(at, size)],
                sem.at[k + 1],
            )
        )
        skip = 1 if at == 0 else 0
        couplings.append(
            pltpu.make_async_copy(
                coupling_hbm.at[pl.ds(source - 1 + skip, size - skip)],
                coupling.at[pl.ds(at - 1 + skip, size - skip)],
                sem.at[k + 2],
            )
        )
    for copy in triangles + couplings:
        copy.start()
    for copy in triangles:
        copy.wait()
    outward = []
    zero = jnp.zeros((NB, NB), BF16)
    one, two, three = slice(0, NB), slice(NB, 2 * NB), slice(2 * NB, 3 * NB)
    members = range(shared + 1)
    inv = {m: [inverse[m, i] for i in range(SB)] for m in members}
    t10 = {m: mm(lowerpart[m, one, one], inv[m][0]).astype(BF16) for m in members}
    t21 = {m: mm(lowerpart[m, two, two], inv[m][1]).astype(BF16) for m in members}
    x10 = {m: (-mm(inv[m][1], t10[m])).astype(BF16) for m in members}
    x21 = {m: (-mm(inv[m][2], t21[m])).astype(BF16) for m in members}
    t20 = {
        m: mm(lowerpart[m, two, :], jnp.concatenate([inv[m][0], x10[m]], axis=0)).astype(BF16)
        for m in members
    }
    x20 = {m: (-mm(inv[m][2], t20[m])).astype(BF16) for m in members}
    for m in members:
        full[m, one, :] = jnp.concatenate([inv[m][0], zero, zero], axis=1)
        full[m, two, :] = jnp.concatenate([x10[m], inv[m][1], zero], axis=1)
        full[m, three, :] = jnp.concatenate([x20[m], x21[m], inv[m][2]], axis=1)
        outward.append(pltpu.make_async_copy(full.at[m], full_hbm.at[m], out_sem.at[m]))
        outward[-1].start()
    for copy in couplings:
        copy.wait()
    for m in members[1:]:
        product[m - 1] = mm(coupling[m - 1], full[m]).astype(BF16)
    for copy in outward:
        copy.wait()


def level_kernel(parts, product, out, residue):
    total = parts[0]
    for j in range(1, parts.shape[0]):
        total = total + parts[j]
    level = total[:, :S]
    residue[...] = level
    second = total[:, S : 2 * S] - mm_nt(level.astype(BF16), product[product.shape[0] - 1])
    for j in range(out.shape[0]):
        out[j, :, :S] = second
        out[j, :, S:] = total[:, 2 * S :]


def tree_kernel(
    place, gathered, residue, full_hbm, product, weights_hbm, parent_hbm, forward_hbm, factors_hbm,
    out, weights, base,
    res2, res3, full, parent, forward_t, factors, base_low, sem,
):
    leaf = place[0]
    early = [
        pltpu.make_async_copy(parent_hbm, parent, sem.at[0]),
        pltpu.make_async_copy(factors_hbm, factors, sem.at[1]),
        pltpu.make_async_copy(forward_hbm, forward_t, sem.at[2]),
    ]
    for h in range(1, LEV + 1):
        number = first_number(1) if h == 1 else first_number(h) + (leaf >> h)
        early.append(pltpu.make_async_copy(full_hbm.at[number], full.at[h - 1], sem.at[2 + h]))
    fetched = pltpu.make_async_copy(weights_hbm.at[pl.ds(0, LB // 2)], weights, sem.at[3 + LEV])
    for copy in early + [fetched]:
        copy.start()
    remaining = list(reversed(range(LB)))

    def base_steps(count):
        for _ in range(min(count, len(remaining))):
            k = remaining.pop(0)
            value = forward_t[k]
            if k < LB - 1:
                value = jnp.concatenate([value, base_low[parent[0, 0, k]]], axis=1)
                value = mm(value, factors[k])
            else:
                value = mm(value, factors[k, :NB, :])
            base[k] = value
            base_low[k] = value.astype(BF16)

    span = [slice(h * S, (h + 1) * S) for h in range(LEV)]
    residues = []
    for h in range(2, LEV + 1):
        groups = 1 << (LEV - h)
        width = 8 // groups
        children = first_number(h - 1) - 1
        following = []
        for g in range(groups):
            r = gathered[g * width, :, span[h - 2]]
            for j in range(1, width):
                r = r + gathered[g * width + j, :, span[h - 2]]
            if h > 2:
                for c in (2 * g, 2 * g + 1):
                    r = r - mm_nt(residues[c], product[children + c])
                base_steps(2)
            if h == 2:
                res2[g] = r
            if h == 3:
                res3[g] = r
            following.append(r if h == LEV else r.astype(BF16))
        residues = following
        if h == 2:
            for copy in early:
                copy.wait()
    own = [residue[...], res2[leaf >> 2], res3[leaf >> 3], residues[0]]
    scaled = [None] * LEV
    for h in range(LEV, 0, -1):
        matrix = full[h - 1]
        scaled[h - 1] = mm(mm_nt(own[h - 1].astype(BF16), matrix).astype(BF16), matrix)
        base_steps(1)
    above = None
    for h in range(LEV, 0, -1):
        number = first_number(1) if h == 1 else first_number(h) + (leaf >> h)
        value = scaled[h - 1]
        if h < LEV:
            value = value - mm(above, product[number - 1])
        above = value.astype(BF16)
        base_steps(2)
        for j in range(out.shape[0]):
            out[j, :, span[h - 1]] = value
    base_steps(LB)
    fetched.wait()


def finish_kernel(
    place, mine, other, base, weights_first, weights_hbm, local_hbm, separators_hbm,
    weights_last, local, separators, sem, out_sem,
):
    inward = []
    for j in range(2):
        source = weights_hbm.at[pl.ds(LB // 2 + j * LB // 4, LB // 4)]
        target = weights_last.at[pl.ds(j * LB // 4, LB // 4)]
        inward.append(pltpu.make_async_copy(source, target, sem.at[j]))
        inward[-1].start()
    first_core = lax.rem(place[0], 2) == 0
    a, b = mine[...], other[...]
    rows = jnp.concatenate([jnp.where(first_core, a, b), jnp.where(first_core, b, a)], axis=0)
    low = rows.astype(BF16)
    for i in range(rows.shape[1] // NB):
        separators[i * NB : (i + 1) * NB, :] = rows[:, i * NB : (i + 1) * NB].T
    outward = [pltpu.make_async_copy(separators, separators_hbm, out_sem.at[0])]
    outward[0].start()
    for k in range(0, LB, 2):
        if k >= LB // 2 and k % (LB // 4) == 0:
            inward[(k - LB // 2) // (LB // 4)].wait()
        weights, at = (weights_first, k) if k < LB // 2 else (weights_last, k - LB // 2)
        terms = mm(low, jnp.concatenate([weights[at], weights[at + 1]], axis=1))
        for j in range(2):
            value = base[k + j] - terms[:, j * NB : (j + 1) * NB]
            local[(k + j) * NB : (k + j + 1) * NB, :] = value.T
        span = pl.ds(k * NB, 2 * NB)
        outward.append(
            pltpu.make_async_copy(local.at[span], local_hbm.at[span], out_sem.at[1 + k // 2])
        )
        outward[-1].start()
    for copy in outward:
        copy.wait()


def shape(dims, dtype=F32):
    return jax.ShapeDtypeStruct(dims, dtype)


def run_forward(place, parent, right, inverse, below, coupling, separator_right):
    height, rows = coupling.shape
    columns = right.shape[2]
    half = columns // 2
    return pl.pallas_call(
        forward_kernel,
        out_shape=(
            pltpu.HBM((LB, height, NB), BF16),
            pltpu.HBM((LB, columns, NB), BF16),
            pltpu.HBM((LB, 2 * NB, NB), BF16),
            shape((half, height)),
            shape((half, height)),
        ),
        in_specs=[SMEM] + [HBM] * 6,
        out_specs=(HBM,) * 3 + (VMEM,) * 2,
        scratch_shapes=[
            pltpu.VMEM((LB, columns, NB), BF16),
            pltpu.VMEM((LB, height // 2, NB), BF16),
            pltpu.VMEM((LB, height // 2, NB), BF16),
            pltpu.VMEM((LB, 2 * NB, NB), BF16),
            pltpu.SMEM((1, 1, LB - 1), jnp.int32),
            pltpu.VMEM((LB, NB, columns), F32),
            pltpu.VMEM((LB, NB, NB), BF16),
            pltpu.VMEM((LB - 1, NB, NB), BF16),
            pltpu.VMEM((height, rows), BF16),
            pltpu.VMEM((LEV, S, columns), F32),
            pltpu.VMEM((LB, NB, columns), F32),
            pltpu.VMEM((rows, columns), BF16),
            pltpu.SemaphoreType.DMA((12,)),
            pltpu.SemaphoreType.DMA((2 * LB + 2,)),
        ],
        compiler_params=limit(30),
        name="forward",
    )(place, *in_hbm(parent, right, inverse, below, coupling, separator_right))


def run_separator(place, inverse, lowerpart, coupling):
    return pl.pallas_call(
        separator_kernel,
        out_shape=(pltpu.HBM((8, S, S), BF16), shape((7, S, S), BF16)),
        in_specs=[SMEM] + [HBM] * 3,
        out_specs=(HBM, VMEM),
        scratch_shapes=[
            pltpu.VMEM((8, S, S), BF16),
            pltpu.VMEM((8, SB, NB, NB), BF16),
            pltpu.VMEM((8, 2 * NB, 2 * NB), BF16),
            pltpu.VMEM((7, S, S), BF16),
            pltpu.SemaphoreType.DMA((6,)),
            pltpu.SemaphoreType.DMA((8,)),
        ],
        compiler_params=limit(16),
        cost_estimate=pl.CostEstimate(flops=6 * 10**9, transcendentals=0, bytes_accessed=2 * 10**7),
        name="separator",
    )(place, *in_hbm(inverse, lowerpart, coupling))


def on_device(
    local_right,
    local_inverse,
    local_below,
    local_parent,
    local_coupling,
    separator_right,
    separator_inverse,
    separator_lower,
    parent_coupling,
):
    rows = local_right.shape[2]
    columns = local_right.shape[3]
    half = columns // 2
    height = LEV * S
    leaves = lax.axis_size("leaf")
    reps = lax.axis_size("rep")
    chips = [[2 * i + c for i in range(leaves // 2)] for c in range(2)]
    pairs = [(i, i ^ 1) for i in range(leaves)]
    place = jnp.stack([lax.axis_index("leaf"), lax.axis_index("rep")]).astype(jnp.int32)
    right = local_right.reshape(LB, NB, columns)
    coupling = local_coupling.reshape(height, rows)

    weights, forward_t, factors, keep, send = run_forward(
        place, local_parent, right, local_inverse[0, 0], local_below[0, 0], coupling, separator_right
    )
    total = keep + lax.ppermute(send, "leaf", pairs)
    parts = lax.all_to_all(total.reshape(reps, CH, height), "rep", 0, 0, tiled=True)
    place_after, _ = lax.optimization_barrier((place, total))
    full, product = run_separator(
        place_after, separator_inverse, separator_lower, parent_coupling
    )
    parts, full, product = lax.optimization_barrier((parts, full, product))
    summed, residue = pl.pallas_call(
        level_kernel,
        out_shape=(shape((leaves // 2, CH, height - S)), shape((CH, S))),
        in_specs=[VMEM] * 2,
        out_specs=(VMEM, VMEM),
        compiler_params=limit(8),
        name="level",
    )(parts, product)
    gathered = lax.all_to_all(summed, "leaf", 0, 0, axis_index_groups=chips, tiled=True)
    solved, weights_first, base = pl.pallas_call(
        tree_kernel,
        out_shape=(
            shape((reps, CH, height)),
            pltpu.VMEM((LB // 2, height, NB), BF16),
            pltpu.VMEM((LB, columns, NB), F32),
        ),
        in_specs=[SMEM, VMEM, VMEM, HBM, VMEM] + [HBM] * 4,
        out_specs=(VMEM,) * 3,
        scratch_shapes=[
            pltpu.VMEM((4, CH, S), F32),
            pltpu.VMEM((2, CH, S), F32),
            pltpu.VMEM((LEV, S, S), BF16),
            pltpu.SMEM((1, 1, LB - 1), jnp.int32),
            pltpu.VMEM((LB, columns, NB), BF16),
            pltpu.VMEM((LB, 2 * NB, NB), BF16),
            pltpu.VMEM((LB, columns, NB), BF16),
            pltpu.SemaphoreType.DMA((LEV + 4,)),
        ],
        compiler_params=limit(12),
        name="tree",
    )(
        place, gathered, residue, *in_hbm(full), product,
        *in_hbm(weights, local_parent, forward_t, factors),
    )
    mine = lax.all_to_all(solved, "rep", 0, 0, tiled=True).reshape(half, height)
    other = lax.ppermute(mine, "leaf", pairs)
    local, separators = pl.pallas_call(
        finish_kernel,
        out_shape=(pltpu.HBM((rows, columns), F32), pltpu.HBM((height, columns), F32)),
        in_specs=[SMEM] + [VMEM] * 4 + [HBM],
        out_specs=(HBM, HBM),
        scratch_shapes=[
            pltpu.VMEM((LB // 2, height, NB), BF16),
            pltpu.VMEM((rows, columns), F32),
            pltpu.VMEM((height, columns), F32),
            pltpu.SemaphoreType.DMA((2,)),
            pltpu.SemaphoreType.DMA((LB // 2 + 1,)),
        ],
        compiler_params=limit(16),
        name="finish",
    )(place, mine, other, base, weights_first, *in_hbm(weights))
    return (local[None, None], separators.reshape(1, LEV, S, columns))


def solution(mesh):
    in_specs = (
        P("leaf", "rep", None, None),
        P("leaf", "rep", None, None, None),
        P("leaf", "rep", None, None, None),
        P("leaf", "rep", None),
        P("leaf", "rep", None, None, None),
        P(),
        P(),
        P(),
        P(),
    )
    out_specs = (P("leaf", "rep", None, None), P("leaf", None, None, None))
    return jax.shard_map(
        on_device, mesh=mesh, in_specs=in_specs, out_specs=out_specs, check_vma=False
    )
```

time: 67.8 us -> 68.9 us (1.016)
  waiting for transfers between devices: 2.7 us -> 5.17 us
  Pallas kernels: 26.5 us -> 25.5 us
    pallas_call x2, Pallas kernels: 19.6 us -> 15.4 us  [the longest x1 11 us: run_forward(): pl.pallas_call(forward_kernel, out_shape=(pltpu.HBM((LB, height, NB), BF1...]
    all_to_all x1, waiting for transfers between devices: 0.01 us -> 2.47 us  [on_device(): lax.all_to_all(total.reshape(reps, CH, height), 'rep', 0, 0, tiled=True)]
    pallas_call x1, Pallas kernels: 2.44 us -> 4.61 us  [on_device(): pl.pallas_call(finish_kernel, out_shape=(pltpu.HBM((rows, columns), F32),...]
    pallas_call x1, Pallas kernels: 4.29 us -> 5.25 us  [on_device(): pl.pallas_call(tree_kernel, out_shape=(shape((reps, CH, height)), pltpu.V...]
  transfers between devices with their start and end apart: 3 -> 3, of which waited for: 2 -> 3; matrix products, arithmetic and copies ran while one was open for 0% -> 0% of each run, Pallas kernels for 11% -> 6%
where the time goes in v4:
time: 68.9 us; the launch traced here: 68.6 us
  Pallas kernels  25.5 us (37%)
  blocking collectives  25.2 us (37%)
  starting transfers between devices  11.1 us (16%)
  waiting for transfers between devices  5.17 us (8%)
  other arithmetic  0.9 us (1%)
  between operations  0.82 us (1%)
    all_to_all x1, blocking collectives, on_device(): lax.all_to_all(summed, 'leaf', 0, 0, axis_index_groups=chips, tiled=True)  14.2 us
    pallas_call x1, Pallas kernels, run_forward(): pl.pallas_call(forward_kernel, out_shape=(pltpu.HBM((LB, height, NB), BF1...  11 us
    all_to_all x1, blocking collectives, on_device(): mine = lax.all_to_all(solved, 'rep', 0, 0, tiled=True).reshape(half, height)  11 us
    all_to_all x1, starting transfers between devices, on_device(): lax.all_to_all(total.reshape(reps, CH, height), 'rep', 0, 0, tiled=True)  6.13 us
    pallas_call x1, Pallas kernels, on_device(): pl.pallas_call(tree_kernel, out_shape=(shape((reps, CH, height)), pltpu.V...  5.25 us
    pallas_call x1, Pallas kernels, on_device(): pl.pallas_call(finish_kernel, out_shape=(pltpu.HBM((rows, columns), F32),...  4.61 us
    pallas_call x1, Pallas kernels, run_separator(): pl.pallas_call(separator_kernel, out_shape=(pltpu.HBM((8, S, S), BF16), s...  4.39 us
    ppermute x1, starting transfers between devices, on_device(): other = lax.ppermute(mine, 'leaf', pairs)  3.43 us
  transfers between devices with their start and end apart: 3, of which 3 were waited for; matrix products, arithmetic and copies ran while one was open for 0% of the time, Pallas kernels for 6%

profile of v4, /device:TPU:1, one launch (start us, length us, event | category | flops | bytes accessed | tf_op | source)
XLA Modules:
  0.0 68.6 jit_solution(5984335457621701583)
XLA Ops:
  0.6 0.1 pad_add_fusion.place
  0.7 11.0 %forward.1 = (bf16[16,1536,128]{2,1,0:T(8,128)(2,1)}, bf16[16,128,128]{2,1,0:T(8,128)(2,1)}, bf16[16,256,128]{2,1,0:T(8,128)(2,1)}, f32[64,1536]{1,0:T(8,128)S(1)}, f32[64,1536]{1,0:T(8,128)S(1)}) custom-call(s32[2]{0:T(128)S(1)} %pad_add_fusion.place, s32[1,1,15]{2,1,0:T(1,128)} %parent_hbm.3, f32[16,128,128]{2,1,0:T(8,128)} %bitcast.13, ...), custom_call_target="tpu_custom_call" | custom-call | tf_op jit(solution)/shard_map/forward/pallas_call | solution.py:328
  11.8 1.5 %collective-permute-start = (f32[64,1536]{1,0:T(8,128)S(1)}, f32[64,1536]{1,0:T(8,128)S(1)}, u32[]{:S(2)}, u32[]{:S(2)}) collective-permute-start(f32[64,1536]{1,0:T(8,128)S(1)} %get-tuple-element.21), channel_id=1, source_target_pairs={{0,8},{8,0},{16,24},{24,16},{32,40},{40,32},{48,56},{56,48},{64,72... | collective-permute-start | bytes 1179656 | tf_op jit(solution)/shard_map/ppermute | solution.py:406
  13.3 1.3 %collective-permute-done = f32[64,1536]{1,0:T(8,128)S(1)} collective-permute-done((f32[64,1536]{1,0:T(8,128)S(1)}, f32[64,1536]{1,0:T(8,128)S(1)}, u32[]{:S(2)}, u32[]{:S(2)}) %collective-permute-start) | collective-permute-done | bytes 393248 | tf_op jit(solution)/shard_map/ppermute | solution.py:406
  14.6 0.8 %add.3 = f32[64,1536]{1,0:T(8,128)} add(f32[64,1536]{1,0:T(8,128)S(1)} %get-tuple-element.20, f32[64,1536]{1,0:T(8,128)S(1)} %collective-permute-done) | non-fusion elementwise | flops 98304 | bytes 1179648 | tf_op jit(solution)/shard_map/add | solution.py:406
  15.4 6.1 %all-to-all-start = ((f32[8,8,1536]{2,1,0:T(8,128)}), f32[8,8,1536]{2,1,0:T(8,128)S(1)}, u32[]{:S(2)}, u32[]{:S(2)}) async-start(f32[8,8,1536]{2,1,0:T(8,128)} %bitcast.6), calls=%async_computation | async-start | bytes 786432 | tf_op jit(solution)/shard_map/all_to_all | solution.py:407
  21.6 4.4 %separator.1 = (bf16[8,384,384]{2,1,0:T(8,128)(2,1)}, bf16[7,384,384]{2,1,0:T(8,128)(2,1)S(1)}) custom-call(s32[2]{0:T(128)S(1)} %pad_add_fusion.place, bf16[15,3,128,128]{3,2,1,0:T(8,128)(2,1)} %inverse_hbm.1, bf16[15,384,384]{2,1,0:T(8,128)(2,1)} %lower_hbm.1, bf16[14,384,384]{2,1,0:T(8,128)(2,1)} %coupling_hbm.1), custom_call_target="tpu_custom_call" | custom-call | flops 6000000000 | bytes 20000000 | tf_op jit(solution)/shard_map/separator/pallas_call | solution.py:361
  26.0 2.5 %all-to-all-done.parts = f32[8,8,1536]{2,1,0:T(8,128)S(1)} async-done(((f32[8,8,1536]{2,1,0:T(8,128)}), f32[8,8,1536]{2,1,0:T(8,128)S(1)}, u32[]{:S(2)}, u32[]{:S(2)}) %all-to-all-start) | async-done | bytes 393248 | tf_op jit(solution)/shard_map/all_to_all | solution.py:407
  28.4 0.2 level.1
  28.6 14.2 %all_to_all.15.gathered = f32[8,8,1152]{2,1,0:T(8,128)S(1)} all-to-all(f32[8,8,1152]{2,1,0:T(8,128)S(1)} %get-tuple-element.27), channel_id=1, replica_groups={{0,16,32,48,64,80,96,112},{8,24,40,56,72,88,104,120},{1,17,33,49,65,81,..., dimensions={0} | all-to-all | bytes 589824 | tf_op jit(solution)/shard_map/all_to_all | solution.py:421
  42.8 5.2 %tree.1 = (f32[8,8,1536]{2,1,0:T(8,128)S(1)}, bf16[8,1536,128]{2,1,0:T(8,128)(2,1)S(1)}, f32[16,128,128]{2,1,0:T(8,128)S(1)}) custom-call(s32[2]{0:T(128)S(1)} %pad_add_fusion.place, f32[8,8,1152]{2,1,0:T(8,128)S(1)} %all_to_all.15.gathered, f32[8,384]{1,0:T(8,128)S(1)} %get-tuple-element.28.residue, bf16[8,384,384]{2,1,0:T(8,128)(2,1)} %get-tuple-element.29.full_hbm, ...), custom_call_target="tpu_custom_call" | custom-call | tf_op jit(solution)/shard_map/tree/pallas_call | solution.py:422
  48.1 11.0 %all_to_all.16 = f32[8,8,1536]{2,1,0:T(8,128)S(1)} all-to-all(f32[8,8,1536]{2,1,0:T(8,128)S(1)} %get-tuple-element.33), channel_id=1, replica_groups=mesh['leaf'=16,'rep'=8] {'rep'}, dimensions={0} | all-to-all | bytes 786432 | tf_op jit(solution)/shard_map/all_to_all | solution.py:447
  59.1 3.4 %collective-permute-start.1 = (f32[64,1536]{1,0:T(8,128)S(1)}, f32[64,1536]{1,0:T(8,128)S(1)}, u32[]{:S(2)}, u32[]{:S(2)}) collective-permute-start(f32[64,1536]{1,0:T(8,128)S(1)} %bitcast.10), channel_id=1, source_target_pairs={{0,8},{8,0},{16,24},{24,16},{32,40},{40,32},{48,56},{56,48},{64,72... | collective-permute-start | bytes 1179656 | tf_op jit(solution)/shard_map/ppermute | solution.py:448
  62.5 1.3 %collective-permute-done.1.other = f32[64,1536]{1,0:T(8,128)S(1)} collective-permute-done((f32[64,1536]{1,0:T(8,128)S(1)}, f32[64,1536]{1,0:T(8,128)S(1)}, u32[]{:S(2)}, u32[]{:S(2)}) %collective-permute-start.1) | collective-permute-done | bytes 393248 | tf_op jit(solution)/shard_map/ppermute | solution.py:448
  63.9 4.6 %finish.1 = (f32[2048,128]{1,0:T(8,128)}, f32[1536,128]{1,0:T(8,128)}) custom-call(s32[2]{0:T(128)S(1)} %pad_add_fusion.place, f32[64,1536]{1,0:T(8,128)S(1)} %bitcast.11, f32[64,1536]{1,0:T(8,128)S(1)} %collective-permute-done.1.other, f32[16,128,128]{2,1,0:T(8,128)S(1)} %get-tuple-element.34.base, ...), custom_call_target="tpu_custom_call" | custom-call | tf_op jit(solution)/shard_map/finish/pallas_call | solution.py:449
Async XLA Ops:
  11.8 2.9 %collective-permute-start = (f32[64,1536]{1,0:T(8,128)S(1)}, f32[64,1536]{1,0:T(8,128)S(1)}, u32[]{:S(2)}, u32[]{:S(2)}) collective-permute-start(f32[64,1536]{1,0:T(8,128)S(1)} %get-tuple-element.21), channel_id=1, source_target_pairs={{0,8},{8,0},{16,24},{24,16},{32,40},{40,32},{48,56},{56,48},{64,72... | collective-permute-start | bytes 1179656 | tf_op jit(solution)/shard_map/ppermute | solution.py:406
  15.4 13.0 %all-to-all-start = ((f32[8,8,1536]{2,1,0:T(8,128)}), f32[8,8,1536]{2,1,0:T(8,128)S(1)}, u32[]{:S(2)}, u32[]{:S(2)}) async-start(f32[8,8,1536]{2,1,0:T(8,128)} %bitcast.6), calls=%async_computation | async-start | bytes 786432 | tf_op jit(solution)/shard_map/all_to_all | solution.py:407
  59.1 4.8 %collective-permute-start.1 = (f32[64,1536]{1,0:T(8,128)S(1)}, f32[64,1536]{1,0:T(8,128)S(1)}, u32[]{:S(2)}, u32[]{:S(2)}) collective-permute-start(f32[64,1536]{1,0:T(8,128)S(1)} %bitcast.10), channel_id=1, source_target_pairs={{0,8},{8,0},{16,24},{24,16},{32,40},{40,32},{48,56},{56,48},{64,72... | collective-permute-start | bytes 1179656 | tf_op jit(solution)/shard_map/ppermute | solution.py:448

commit v5 on v4

--- a/solution.py
+++ b/solution.py
@@ -208,8 +208,7 @@
 
 
 def tree_kernel(
-    place, gathered, residue, full_hbm, product, weights_hbm, parent_hbm, forward_hbm, factors_hbm,
-    out, weights, base,
+    place, gathered, residue, full_hbm, product, parent_hbm, forward_hbm, factors_hbm, out, base,
     res2, res3, full, parent, forward_t, factors, base_low, sem,
 ):
     leaf = place[0]
@@ -221,8 +220,7 @@
     for h in range(1, LEV + 1):
         number = first_number(1) if h == 1 else first_number(h) + (leaf >> h)
         early.append(pltpu.make_async_copy(full_hbm.at[number], full.at[h - 1], sem.at[2 + h]))
-    fetched = pltpu.make_async_copy(weights_hbm.at[pl.ds(0, LB // 2)], weights, sem.at[3 + LEV])
-    for copy in early + [fetched]:
+    for copy in early:
         copy.start()
     remaining = list(reversed(range(LB)))
 
@@ -279,19 +277,11 @@
         for j in range(out.shape[0]):
             out[j, :, span[h - 1]] = value
     base_steps(LB)
-    fetched.wait()
 
 
 def finish_kernel(
-    place, mine, other, base, weights_first, weights_hbm, local_hbm, separators_hbm,
-    weights_last, local, separators, sem, out_sem,
+    place, mine, other, base, weights, local_hbm, separators_hbm, local, separators, out_sem
 ):
-    inward = []
-    for j in range(2):
-        source = weights_hbm.at[pl.ds(LB // 2 + j * LB // 4, LB // 4)]
-        target = weights_last.at[pl.ds(j * LB // 4, LB // 4)]
-        inward.append(pltpu.make_async_copy(source, target, sem.at[j]))
-        inward[-1].start()
     first_core = lax.rem(place[0], 2) == 0
     a, b = mine[...], other[...]
     rows = jnp.concatenate([jnp.where(first_core, a, b), jnp.where(first_core, b, a)], axis=0)
@@ -301,10 +291,7 @@
     outward = [pltpu.make_async_copy(separators, separators_hbm, out_sem.at[0])]
     outward[0].start()
     for k in range(0, LB, 2):
-        if k >= LB // 2 and k % (LB // 4) == 0:
-            inward[(k - LB // 2) // (LB // 4)].wait()
-        weights, at = (weights_first, k) if k < LB // 2 else (weights_last, k - LB // 2)
-        terms = mm(low, jnp.concatenate([weights[at], weights[at + 1]], axis=1))
+        terms = mm(low, jnp.concatenate([weights[k], weights[k + 1]], axis=1))
         for j in range(2):
             value = base[k + j] - terms[:, j * NB : (j + 1) * NB]
             local[(k + j) * NB : (k + j + 1) * NB, :] = value.T
@@ -419,15 +406,14 @@
         name="level",
     )(parts, product)
     gathered = lax.all_to_all(summed, "leaf", 0, 0, axis_index_groups=chips, tiled=True)
-    solved, weights_first, base = pl.pallas_call(
+    solved, base = pl.pallas_call(
         tree_kernel,
         out_shape=(
             shape((reps, CH, height)),
-            pltpu.VMEM((LB // 2, height, NB), BF16),
             pltpu.VMEM((LB, columns, NB), F32),
         ),
-        in_specs=[SMEM, VMEM, VMEM, HBM, VMEM] + [HBM] * 4,
-        out_specs=(VMEM,) * 3,
+        in_specs=[SMEM, VMEM, VMEM, HBM, VMEM] + [HBM] * 3,
+        out_specs=(VMEM,) * 2,
         scratch_shapes=[
             pltpu.VMEM((4, CH, S), F32),
             pltpu.VMEM((2, CH, S), F32),
@@ -436,31 +422,30 @@
             pltpu.VMEM((LB, columns, NB), BF16),
             pltpu.VMEM((LB, 2 * NB, NB), BF16),
             pltpu.VMEM((LB, columns, NB), BF16),
-            pltpu.SemaphoreType.DMA((LEV + 4,)),
+            pltpu.SemaphoreType.DMA((LEV + 3,)),
         ],
         compiler_params=limit(12),
+        cost_estimate=pl.CostEstimate(flops=6 * 10**9, transcendentals=0, bytes_accessed=4 * 10**7),
         name="tree",
     )(
         place, gathered, residue, *in_hbm(full), product,
-        *in_hbm(weights, local_parent, forward_t, factors),
+        *in_hbm(local_parent, forward_t, factors),
     )
     mine = lax.all_to_all(solved, "rep", 0, 0, tiled=True).reshape(half, height)
     other = lax.ppermute(mine, "leaf", pairs)
     local, separators = pl.pallas_call(
         finish_kernel,
         out_shape=(pltpu.HBM((rows, columns), F32), pltpu.HBM((height, columns), F32)),
-        in_specs=[SMEM] + [VMEM] * 4 + [HBM],
+        in_specs=[SMEM] + [VMEM] * 4,
         out_specs=(HBM, HBM),
         scratch_shapes=[
-            pltpu.VMEM((LB // 2, height, NB), BF16),
             pltpu.VMEM((rows, columns), F32),
             pltpu.VMEM((height, columns), F32),
-            pltpu.SemaphoreType.DMA((2,)),
             pltpu.SemaphoreType.DMA((LB // 2 + 1,)),
         ],
         compiler_params=limit(16),
         name="finish",
-    )(place, mine, other, base, weights_first, *in_hbm(weights))
+    )(place, mine, other, base, weights)
     return (local[None, None], separators.reshape(1, LEV, S, columns))
 
 

time: 68.9 us -> 67 us (0.972)
  Pallas kernels: 25.5 us -> 23.6 us
    pallas_call x1, Pallas kernels: 4.61 us -> 2.45 us  [on_device(): pl.pallas_call(finish_kernel, out_shape=(pltpu.HBM((rows, columns), F32),...]
  transfers between devices with their start and end apart: 3 -> 3, of which waited for: 3 -> 3; matrix products, arithmetic and copies ran while one was open for 0% -> 0% of each run, Pallas kernels for 6% -> 7%
where the time goes in v5:
time: 67 us; the launch traced here: 66.8 us
  blocking collectives  25.2 us (38%)
  Pallas kernels  23.6 us (35%)
  starting transfers between devices  11.1 us (17%)
  waiting for transfers between devices  5.17 us (8%)
  other arithmetic  0.93 us (1%)
  between operations  0.83 us (1%)
    all_to_all x1, blocking collectives, on_device(): lax.all_to_all(summed, 'leaf', 0, 0, axis_index_groups=chips, tiled=True)  14.2 us
    pallas_call x1, Pallas kernels, run_forward(): pl.pallas_call(forward_kernel, out_shape=(pltpu.HBM((LB, height, NB), BF1...  11.1 us
    all_to_all x1, blocking collectives, on_device(): mine = lax.all_to_all(solved, 'rep', 0, 0, tiled=True).reshape(half, height)  11 us
    all_to_all x1, starting transfers between devices, on_device(): lax.all_to_all(total.reshape(reps, CH, height), 'rep', 0, 0, tiled=True)  6.13 us
    pallas_call x1, Pallas kernels, on_device(): pl.pallas_call(tree_kernel, out_shape=(shape((reps, CH, height)), pltpu.V...  5.5 us
    pallas_call x1, Pallas kernels, run_separator(): pl.pallas_call(separator_kernel, out_shape=(pltpu.HBM((8, S, S), BF16), s...  4.39 us
    ppermute x1, starting transfers between devices, on_device(): other = lax.ppermute(mine, 'leaf', pairs)  3.42 us
    all_to_all x1, waiting for transfers between devices, on_device(): lax.all_to_all(total.reshape(reps, CH, height), 'rep', 0, 0, tiled=True)  2.47 us
  transfers between devices with their start and end apart: 3, of which 3 were waited for; matrix products, arithmetic and copies ran while one was open for 0% of the time, Pallas kernels for 7%

profile of v5, /device:TPU:1, one launch (start us, length us, event | category | flops | bytes accessed | tf_op | source)
XLA Modules:
  0.0 66.8 jit_solution(11872408060620622112)
XLA Ops:
  0.6 0.1 pad_add_fusion.place
  0.7 11.1 %forward.1 = (bf16[16,1536,128]{2,1,0:T(8,128)(2,1)}, bf16[16,128,128]{2,1,0:T(8,128)(2,1)}, bf16[16,256,128]{2,1,0:T(8,128)(2,1)}, f32[64,1536]{1,0:T(8,128)S(1)}, f32[64,1536]{1,0:T(8,128)S(1)}) custom-call(s32[2]{0:T(128)S(1)} %pad_add_fusion.place, s32[1,1,15]{2,1,0:T(1,128)} %parent_hbm.3, f32[16,128,128]{2,1,0:T(8,128)} %bitcast.15, ...), custom_call_target="tpu_custom_call" | custom-call | tf_op jit(solution)/shard_map/forward/pallas_call | solution.py:315
  11.8 1.5 %collective-permute-start = (f32[64,1536]{1,0:T(8,128)S(1)}, f32[64,1536]{1,0:T(8,128)S(1)}, u32[]{:S(2)}, u32[]{:S(2)}) collective-permute-start(f32[64,1536]{1,0:T(8,128)S(1)} %get-tuple-element.20), channel_id=1, source_target_pairs={{0,8},{8,0},{16,24},{24,16},{32,40},{40,32},{48,56},{56,48},{64,72... | collective-permute-start | bytes 1179656 | tf_op jit(solution)/shard_map/ppermute | solution.py:393
  13.3 1.3 %collective-permute-done = f32[64,1536]{1,0:T(8,128)S(1)} collective-permute-done((f32[64,1536]{1,0:T(8,128)S(1)}, f32[64,1536]{1,0:T(8,128)S(1)}, u32[]{:S(2)}, u32[]{:S(2)}) %collective-permute-start) | collective-permute-done | bytes 393248 | tf_op jit(solution)/shard_map/ppermute | solution.py:393
  14.6 0.9 %add.3 = f32[64,1536]{1,0:T(8,128)} add(f32[64,1536]{1,0:T(8,128)S(1)} %get-tuple-element.19, f32[64,1536]{1,0:T(8,128)S(1)} %collective-permute-done) | non-fusion elementwise | flops 98304 | bytes 1179648 | tf_op jit(solution)/shard_map/add | solution.py:393
  15.5 6.1 %all-to-all-start = ((f32[8,8,1536]{2,1,0:T(8,128)}), f32[8,8,1536]{2,1,0:T(8,128)S(1)}, u32[]{:S(2)}, u32[]{:S(2)}) async-start(f32[8,8,1536]{2,1,0:T(8,128)} %bitcast.6), calls=%async_computation | async-start | bytes 786432 | tf_op jit(solution)/shard_map/all_to_all | solution.py:394
  21.6 4.4 %separator.1 = (bf16[8,384,384]{2,1,0:T(8,128)(2,1)}, bf16[7,384,384]{2,1,0:T(8,128)(2,1)S(1)}) custom-call(s32[2]{0:T(128)S(1)} %pad_add_fusion.place, bf16[15,3,128,128]{3,2,1,0:T(8,128)(2,1)} %inverse_hbm.1, bf16[15,384,384]{2,1,0:T(8,128)(2,1)} %lower_hbm.1, bf16[14,384,384]{2,1,0:T(8,128)(2,1)} %coupling_hbm.1), custom_call_target="tpu_custom_call" | custom-call | flops 6000000000 | bytes 20000000 | tf_op jit(solution)/shard_map/separator/pallas_call | solution.py:348
  26.0 2.5 %all-to-all-done.parts = f32[8,8,1536]{2,1,0:T(8,128)S(1)} async-done(((f32[8,8,1536]{2,1,0:T(8,128)}), f32[8,8,1536]{2,1,0:T(8,128)S(1)}, u32[]{:S(2)}, u32[]{:S(2)}) %all-to-all-start) | async-done | bytes 393248 | tf_op jit(solution)/shard_map/all_to_all | solution.py:394
  28.5 0.2 level.1
  28.7 14.2 %all_to_all.15.gathered = f32[8,8,1152]{2,1,0:T(8,128)S(1)} all-to-all(f32[8,8,1152]{2,1,0:T(8,128)S(1)} %get-tuple-element.26), channel_id=1, replica_groups={{0,16,32,48,64,80,96,112},{8,24,40,56,72,88,104,120},{1,17,33,49,65,81,..., dimensions={0} | all-to-all | bytes 589824 | tf_op jit(solution)/shard_map/all_to_all | solution.py:408
  42.9 0.0 slice-start
  42.9 0.0 slice-start.1
  42.9 5.5 %tree.1 = (f32[8,8,1536]{2,1,0:T(8,128)S(1)}, f32[16,128,128]{2,1,0:T(8,128)S(1)}) custom-call(s32[2]{0:T(128)S(1)} %pad_add_fusion.place, f32[8,8,1152]{2,1,0:T(8,128)S(1)} %all_to_all.15.gathered, f32[8,384]{1,0:T(8,128)S(1)} %get-tuple-element.27.residue, bf16[8,384,384]{2,1,0:T(8,128)(2,1)} %get-tuple-element.28.full_hbm, ...), custom_call_target="tpu_custom_call" | custom-call | flops 6000000000 | bytes 40000000 | tf_op jit(solution)/shard_map/tree/pallas_call | solution.py:409
  48.4 11.0 %all_to_all.16 = f32[8,8,1536]{2,1,0:T(8,128)S(1)} all-to-all(f32[8,8,1536]{2,1,0:T(8,128)S(1)} %get-tuple-element.31), channel_id=1, replica_groups=mesh['leaf'=16,'rep'=8] {'rep'}, dimensions={0} | all-to-all | bytes 786432 | tf_op jit(solution)/shard_map/all_to_all | solution.py:434
  59.4 3.4 %collective-permute-start.1 = (f32[64,1536]{1,0:T(8,128)S(1)}, f32[64,1536]{1,0:T(8,128)S(1)}, u32[]{:S(2)}, u32[]{:S(2)}) collective-permute-start(f32[64,1536]{1,0:T(8,128)S(1)} %bitcast.12), channel_id=1, source_target_pairs={{0,8},{8,0},{16,24},{24,16},{32,40},{40,32},{48,56},{56,48},{64,72... | collective-permute-start | bytes 1179656 | tf_op jit(solution)/shard_map/ppermute | solution.py:435
  62.8 1.3 %collective-permute-done.1.other = f32[64,1536]{1,0:T(8,128)S(1)} collective-permute-done((f32[64,1536]{1,0:T(8,128)S(1)}, f32[64,1536]{1,0:T(8,128)S(1)}, u32[]{:S(2)}, u32[]{:S(2)}) %collective-permute-start.1) | collective-permute-done | bytes 393248 | tf_op jit(solution)/shard_map/ppermute | solution.py:435
  64.2 0.0 slice-done
  64.2 0.0 slice-done.1
  64.2 2.5 %finish.1 = (f32[2048,128]{1,0:T(8,128)}, f32[1536,128]{1,0:T(8,128)}) custom-call(s32[2]{0:T(128)S(1)} %pad_add_fusion.place, f32[64,1536]{1,0:T(8,128)S(1)} %bitcast.13, f32[64,1536]{1,0:T(8,128)S(1)} %collective-permute-done.1.other, f32[16,128,128]{2,1,0:T(8,128)S(1)} %get-tuple-element.32.base, bf16[16,1536,128]{2,1,0:T(8,128)(2,1)S(1)} %bitcast.11), custom_call_target="tpu_custom_call" | custom-call | tf_op jit(solution)/shard_map/finish/pallas_call | solution.py:436
  (1 shorter events, 0.0 us)
Async XLA Ops:
  11.8 2.9 %collective-permute-start = (f32[64,1536]{1,0:T(8,128)S(1)}, f32[64,1536]{1,0:T(8,128)S(1)}, u32[]{:S(2)}, u32[]{:S(2)}) collective-permute-start(f32[64,1536]{1,0:T(8,128)S(1)} %get-tuple-element.20), channel_id=1, source_target_pairs={{0,8},{8,0},{16,24},{24,16},{32,40},{40,32},{48,56},{56,48},{64,72... | collective-permute-start | bytes 1179656 | tf_op jit(solution)/shard_map/ppermute | solution.py:393
  15.5 13.0 %all-to-all-start = ((f32[8,8,1536]{2,1,0:T(8,128)}), f32[8,8,1536]{2,1,0:T(8,128)S(1)}, u32[]{:S(2)}, u32[]{:S(2)}) async-start(f32[8,8,1536]{2,1,0:T(8,128)} %bitcast.6), calls=%async_computation | async-start | bytes 786432 | tf_op jit(solution)/shard_map/all_to_all | solution.py:394
  42.9 21.3 %slice-start = ((s8[6291456]{0:T(1024)(128)(4,1)}), s8[4194304]{0:T(1024)(128)(4,1)S(1)}, s32[]{:S(2)}) async-start(s8[6291456]{0:T(1024)(128)(4,1)} %bitcast.10), calls=%async_computation.3 | async-start | bytes 8388608
  42.9 21.3 %slice-start.1 = ((s8[6291456]{0:T(1024)(128)(4,1)}), s8[2097152]{0:T(1024)(128)(4,1)S(1)}, s32[]{:S(2)}) async-start(s8[6291456]{0:T(1024)(128)(4,1)} %bitcast.10), calls=%async_computation.4 | async-start | bytes 4194304
  59.4 4.8 %collective-permute-start.1 = (f32[64,1536]{1,0:T(8,128)S(1)}, f32[64,1536]{1,0:T(8,128)S(1)}, u32[]{:S(2)}, u32[]{:S(2)}) collective-permute-start(f32[64,1536]{1,0:T(8,128)S(1)} %bitcast.12), channel_id=1, source_target_pairs={{0,8},{8,0},{16,24},{24,16},{32,40},{40,32},{48,56},{56,48},{64,72... | collective-permute-start | bytes 1179656 | tf_op jit(solution)/shard_map/ppermute | solution.py:435

commit v6 on v5

--- a/solution.py
+++ b/solution.py
@@ -40,8 +40,8 @@
 
 def forward_kernel(
     place, parent_hbm, right_hbm, inverse_hbm, below_hbm, coupling_hbm, sepright_hbm,
-    weights_hbm, forward_hbm, factors_hbm, keep, send,
-    forward_t, weights_a, weights_b, factors,
+    weights_hbm, forward_t, factors, keep, send,
+    weights_a, weights_b,
     parent, right, inverse, below, coupling, sepright, acc, rounded, sem, out_sem,
 ):
     leaf, rep = place[0], place[1]
@@ -104,16 +104,12 @@
 
     for k in reversed(range(LB - 1)):
         factor_step(k)
-    outward.append(pltpu.make_async_copy(factors, factors_hbm, out_sem.at[2 * LB]))
-    outward[-1].start()
     for i in range(LB):
         if i % 4 == 0:
             quarters[i // 4].wait()
         weights_step(LB - 1 - i, 0)
         forward_step(i)
         weights_step(LB - 1 - i, 1)
-    outward.append(pltpu.make_async_copy(forward_t, forward_hbm, out_sem.at[2 * LB + 1]))
-    outward[-1].start()
     for copy in others:
         copy.wait()
     values = rounded[...]
@@ -135,8 +131,9 @@
 
 
 def separator_kernel(
-    place, inverse_hbm, lower_hbm, coupling_hbm, full_hbm, product,
-    full, inverse, lowerpart, coupling, sem, out_sem,
+    place, inverse_hbm, lower_hbm, coupling_hbm, parent_hbm, forward_t, factors,
+    full_hbm, base_hbm, product,
+    full, inverse, lowerpart, coupling, parent, base, base_low, sem, out_sem,
 ):
     shared = first_number(1)
     number = shared + (place[0] >> 1)
@@ -163,64 +160,8 @@
                 sem.at[k + 2],
             )
         )
-    for copy in triangles + couplings:
-        copy.start()
-    for copy in triangles:
-        copy.wait()
-    outward = []
-    zero = jnp.zeros((NB, NB), BF16)
-    one, two, three = slice(0, NB), slice(NB, 2 * NB), slice(2 * NB, 3 * NB)
-    members = range(shared + 1)
-    inv = {m: [inverse[m, i] for i in range(SB)] for m in members}
-    t10 = {m: mm(lowerpart[m, one, one], inv[m][0]).astype(BF16) for m in members}
-    t21 = {m: mm(lowerpart[m, two, two], inv[m][1]).astype(BF16) for m in members}
-    x10 = {m: (-mm(inv[m][1], t10[m])).astype(BF16) for m in members}
-    x21 = {m: (-mm(inv[m][2], t21[m])).astype(BF16) for m in members}
-    t20 = {
-        m: mm(lowerpart[m, two, :], jnp.concatenate([inv[m][0], x10[m]], axis=0)).astype(BF16)
-        for m in members
-    }
-    x20 = {m: (-mm(inv[m][2], t20[m])).astype(BF16) for m in members}
-    for m in members:
-        full[m, one, :] = jnp.concatenate([inv[m][0], zero, zero], axis=1)
-        full[m, two, :] = jnp.concatenate([x10[m], inv[m][1], zero], axis=1)
-        full[m, three, :] = jnp.concatenate([x20[m], x21[m], inv[m][2]], axis=1)
-        outward.append(pltpu.make_async_copy(full.at[m], full_hbm.at[m], out_sem.at[m]))
-        outward[-1].start()
-    for copy in couplings:
-        copy.wait()
-    for m in members[1:]:
-        product[m - 1] = mm(coupling[m - 1], full[m]).astype(BF16)
-    for copy in outward:
-        copy.wait()
-
-
-def level_kernel(parts, product, out, residue):
-    total = parts[0]
-    for j in range(1, parts.shape[0]):
-        total = total + parts[j]
-    level = total[:, :S]
-    residue[...] = level
-    second = total[:, S : 2 * S] - mm_nt(level.astype(BF16), product[product.shape[0] - 1])
-    for j in range(out.shape[0]):
-        out[j, :, :S] = second
-        out[j, :, S:] = total[:, 2 * S :]
-
-
-def tree_kernel(
-    place, gathered, residue, full_hbm, product, parent_hbm, forward_hbm, factors_hbm, out, base,
-    res2, res3, full, parent, forward_t, factors, base_low, sem,
-):
-    leaf = place[0]
-    early = [
-        pltpu.make_async_copy(parent_hbm, parent, sem.at[0]),
-        pltpu.make_async_copy(factors_hbm, factors, sem.at[1]),
-        pltpu.make_async_copy(forward_hbm, forward_t, sem.at[2]),
-    ]
-    for h in range(1, LEV + 1):
-        number = first_number(1) if h == 1 else first_number(h) + (leaf >> h)
-        early.append(pltpu.make_async_copy(full_hbm.at[number], full.at[h - 1], sem.at[2 + h]))
-    for copy in early:
+    fetched = pltpu.make_async_copy(parent_hbm, parent, sem.at[6])
+    for copy in [fetched] + triangles + couplings:
         copy.start()
     remaining = list(reversed(range(LB)))
 
@@ -236,6 +177,69 @@
             base[k] = value
             base_low[k] = value.astype(BF16)
 
+    fetched.wait()
+    base_steps(3)
+    for copy in triangles:
+        copy.wait()
+    outward = []
+    zero = jnp.zeros((NB, NB), BF16)
+    one, two, three = slice(0, NB), slice(NB, 2 * NB), slice(2 * NB, 3 * NB)
+    members = range(shared + 1)
+    inv = {m: [inverse[m, i] for i in range(SB)] for m in members}
+    t10 = {m: mm(lowerpart[m, one, one], inv[m][0]).astype(BF16) for m in members}
+    base_steps(1)
+    t21 = {m: mm(lowerpart[m, two, two], inv[m][1]).astype(BF16) for m in members}
+    base_steps(1)
+    x10 = {m: (-mm(inv[m][1], t10[m])).astype(BF16) for m in members}
+    base_steps(1)
+    x21 = {m: (-mm(inv[m][2], t21[m])).astype(BF16) for m in members}
+    base_steps(1)
+    t20 = {
+        m: mm(lowerpart[m, two, :], jnp.concatenate([inv[m][0], x10[m]], axis=0)).astype(BF16)
+        for m in members
+    }
+    base_steps(1)
+    x20 = {m: (-mm(inv[m][2], t20[m])).astype(BF16) for m in members}
+    for m in members:
+        full[m, one, :] = jnp.concatenate([inv[m][0], zero, zero], axis=1)
+        full[m, two, :] = jnp.concatenate([x10[m], inv[m][1], zero], axis=1)
+        full[m, three, :] = jnp.concatenate([x20[m], x21[m], inv[m][2]], axis=1)
+        outward.append(pltpu.make_async_copy(full.at[m], full_hbm.at[m], out_sem.at[m]))
+        outward[-1].start()
+    for copy in couplings:
+        copy.wait()
+    for m in members[1:]:
+        base_steps(2)
+        product[m - 1] = mm(coupling[m - 1], full[m]).astype(BF16)
+        if not remaining and len(outward) == len(members):
+            outward.append(pltpu.make_async_copy(base, base_hbm, out_sem.at[len(members)]))
+            outward[-1].start()
+    for copy in outward:
+        copy.wait()
+
+
+def level_kernel(parts, product, out, residue):
+    total = parts[0]
+    for j in range(1, parts.shape[0]):
+        total = total + parts[j]
+    level = total[:, :S]
+    residue[...] = level
+    second = total[:, S : 2 * S] - mm_nt(level.astype(BF16), product[product.shape[0] - 1])
+    for j in range(out.shape[0]):
+        out[j, :, :S] = second
+        out[j, :, S:] = total[:, 2 * S :]
+
+
+def tree_kernel(
+    place, gathered, residue, full_hbm, product, out, res2, res3, full, sem,
+):
+    leaf = place[0]
+    early = []
+    for h in range(1, LEV + 1):
+        number = first_number(1) if h == 1 else first_number(h) + (leaf >> h)
+        early.append(pltpu.make_async_copy(full_hbm.at[number], full.at[h - 1], sem.at[h - 1]))
+    for copy in early:
+        copy.start()
     span = [slice(h * S, (h + 1) * S) for h in range(LEV)]
     residues = []
     for h in range(2, LEV + 1):
@@ -250,7 +254,6 @@
             if h > 2:
                 for c in (2 * g, 2 * g + 1):
                     r = r - mm_nt(residues[c], product[children + c])
-                base_steps(2)
             if h == 2:
                 res2[g] = r
             if h == 3:
@@ -265,7 +268,6 @@
     for h in range(LEV, 0, -1):
         matrix = full[h - 1]
         scaled[h - 1] = mm(mm_nt(own[h - 1].astype(BF16), matrix).astype(BF16), matrix)
-        base_steps(1)
     above = None
     for h in range(LEV, 0, -1):
         number = first_number(1) if h == 1 else first_number(h) + (leaf >> h)
@@ -273,10 +275,8 @@
         if h < LEV:
             value = value - mm(above, product[number - 1])
         above = value.astype(BF16)
-        base_steps(2)
         for j in range(out.shape[0]):
             out[j, :, span[h - 1]] = value
-    base_steps(LB)
 
 
 def finish_kernel(
@@ -316,18 +316,16 @@
         forward_kernel,
         out_shape=(
             pltpu.HBM((LB, height, NB), BF16),
-            pltpu.HBM((LB, columns, NB), BF16),
-            pltpu.HBM((LB, 2 * NB, NB), BF16),
+            shape((LB, columns, NB), BF16),
+            shape((LB, 2 * NB, NB), BF16),
             shape((half, height)),
             shape((half, height)),
         ),
         in_specs=[SMEM] + [HBM] * 6,
-        out_specs=(HBM,) * 3 + (VMEM,) * 2,
+        out_specs=(HBM,) + (VMEM,) * 4,
         scratch_shapes=[
-            pltpu.VMEM((LB, columns, NB), BF16),
             pltpu.VMEM((LB, height // 2, NB), BF16),
             pltpu.VMEM((LB, height // 2, NB), BF16),
-            pltpu.VMEM((LB, 2 * NB, NB), BF16),
             pltpu.SMEM((1, 1, LB - 1), jnp.int32),
             pltpu.VMEM((LB, NB, columns), F32),
             pltpu.VMEM((LB, NB, NB), BF16),
@@ -337,31 +335,38 @@
             pltpu.VMEM((LB, NB, columns), F32),
             pltpu.VMEM((rows, columns), BF16),
             pltpu.SemaphoreType.DMA((12,)),
-            pltpu.SemaphoreType.DMA((2 * LB + 2,)),
+            pltpu.SemaphoreType.DMA((2 * LB,)),
         ],
         compiler_params=limit(30),
         name="forward",
     )(place, *in_hbm(parent, right, inverse, below, coupling, separator_right))
 
 
-def run_separator(place, inverse, lowerpart, coupling):
+def run_separator(place, inverse, lowerpart, coupling, parent, forward_t, factors):
     return pl.pallas_call(
         separator_kernel,
-        out_shape=(pltpu.HBM((8, S, S), BF16), shape((7, S, S), BF16)),
-        in_specs=[SMEM] + [HBM] * 3,
-        out_specs=(HBM, VMEM),
+        out_shape=(
+            pltpu.HBM((8, S, S), BF16),
+            pltpu.HBM(forward_t.shape, F32),
+            shape((7, S, S), BF16),
+        ),
+        in_specs=[SMEM] + [HBM] * 4 + [VMEM] * 2,
+        out_specs=(HBM, HBM, VMEM),
         scratch_shapes=[
             pltpu.VMEM((8, S, S), BF16),
             pltpu.VMEM((8, SB, NB, NB), BF16),
             pltpu.VMEM((8, 2 * NB, 2 * NB), BF16),
             pltpu.VMEM((7, S, S), BF16),
-            pltpu.SemaphoreType.DMA((6,)),
-            pltpu.SemaphoreType.DMA((8,)),
+            pltpu.SMEM((1, 1, LB - 1), jnp.int32),
+            pltpu.VMEM(forward_t.shape, F32),
+            pltpu.VMEM(forward_t.shape, BF16),
+            pltpu.SemaphoreType.DMA((7,)),
+            pltpu.SemaphoreType.DMA((9,)),
         ],
         compiler_params=limit(16),
         cost_estimate=pl.CostEstimate(flops=6 * 10**9, transcendentals=0, bytes_accessed=2 * 10**7),
         name="separator",
-    )(place, *in_hbm(inverse, lowerpart, coupling))
+    )(place, *in_hbm(inverse, lowerpart, coupling, parent), forward_t, factors)
 
 
 def on_device(
@@ -393,10 +398,10 @@
     total = keep + lax.ppermute(send, "leaf", pairs)
     parts = lax.all_to_all(total.reshape(reps, CH, height), "rep", 0, 0, tiled=True)
     place_after, _ = lax.optimization_barrier((place, total))
-    full, product = run_separator(
-        place_after, separator_inverse, separator_lower, parent_coupling
+    full, base, product = run_separator(
+        place_after, separator_inverse, separator_lower, parent_coupling, local_parent, forward_t, factors
     )
-    parts, full, product = lax.optimization_barrier((parts, full, product))
+    parts, full, base, product = lax.optimization_barrier((parts, full, base, product))
     summed, residue = pl.pallas_call(
         level_kernel,
         out_shape=(shape((leaves // 2, CH, height - S)), shape((CH, S))),
@@ -406,31 +411,21 @@
         name="level",
     )(parts, product)
     gathered = lax.all_to_all(summed, "leaf", 0, 0, axis_index_groups=chips, tiled=True)
-    solved, base = pl.pallas_call(
+    solved = pl.pallas_call(
         tree_kernel,
-        out_shape=(
-            shape((reps, CH, height)),
-            pltpu.VMEM((LB, columns, NB), F32),
-        ),
-        in_specs=[SMEM, VMEM, VMEM, HBM, VMEM] + [HBM] * 3,
-        out_specs=(VMEM,) * 2,
+        out_shape=shape((reps, CH, height)),
+        in_specs=[SMEM, VMEM, VMEM, HBM, VMEM],
+        out_specs=VMEM,
         scratch_shapes=[
             pltpu.VMEM((4, CH, S), F32),
             pltpu.VMEM((2, CH, S), F32),
             pltpu.VMEM((LEV, S, S), BF16),
-            pltpu.SMEM((1, 1, LB - 1), jnp.int32),
-            pltpu.VMEM((LB, columns, NB), BF16),
-            pltpu.VMEM((LB, 2 * NB, NB), BF16),
-            pltpu.VMEM((LB, columns, NB), BF16),
-            pltpu.SemaphoreType.DMA((LEV + 3,)),
+            pltpu.SemaphoreType.DMA((LEV,)),
         ],
         compiler_params=limit(12),
         cost_estimate=pl.CostEstimate(flops=6 * 10**9, transcendentals=0, bytes_accessed=4 * 10**7),
         name="tree",
-    )(
-        place, gathered, residue, *in_hbm(full), product,
-        *in_hbm(local_parent, forward_t, factors),
-    )
+    )(place, gathered, residue, *in_hbm(full), product)
     mine = lax.all_to_all(solved, "rep", 0, 0, tiled=True).reshape(half, height)
     other = lax.ppermute(mine, "leaf", pairs)
     local, separators = pl.pallas_call(

time: 67 us -> 65.7 us (0.981)
  waiting for transfers between devices: 5.17 us -> 2.95 us
  local copies, waits for them, and re-layouts: 0.01 us -> 1.06 us
    all_to_all x1, waiting for transfers between devices: 2.47 us -> 0.25 us  [on_device(): lax.all_to_all(total.reshape(reps, CH, height), 'rep', 0, 0, tiled=True)]
    unnamed x4 -> x10, local copies, waits for them, and re-layouts: 0.01 us -> 1.06 us
  transfers between devices with their start and end apart: 3 -> 3, of which waited for: 3 -> 3; matrix products, arithmetic and copies ran while one was open for 0% -> 0% of each run, Pallas kernels for 7% -> 9%
where the time goes in v6:
time: 65.7 us; the launch traced here: 65.4 us
  blocking collectives  25.2 us (38%)
  Pallas kernels  23.3 us (35%)
  starting transfers between devices  11.4 us (17%)
  waiting for transfers between devices  2.95 us (4%)
  local copies, waits for them, and re-layouts  1.06 us (2%)
  other arithmetic  0.94 us (1%)
  between operations  0.68 us (1%)
    all_to_all x1, blocking collectives, on_device(): lax.all_to_all(summed, 'leaf', 0, 0, axis_index_groups=chips, tiled=True)  14.2 us
    pallas_call x1, Pallas kernels, run_forward(): pl.pallas_call(forward_kernel, out_shape=(pltpu.HBM((LB, height, NB), BF1...  11 us
    all_to_all x1, blocking collectives, on_device(): mine = lax.all_to_all(solved, 'rep', 0, 0, tiled=True).reshape(half, height)  11 us
    all_to_all x1, starting transfers between devices, on_device(): lax.all_to_all(total.reshape(reps, CH, height), 'rep', 0, 0, tiled=True)  6.13 us
    pallas_call x1, Pallas kernels, run_separator(): pl.pallas_call(separator_kernel, out_shape=(pltpu.HBM((8, S, S), BF16), p...  5.57 us
    pallas_call x1, Pallas kernels, on_device(): pl.pallas_call(tree_kernel, out_shape=shape((reps, CH, height)), in_specs...  4.01 us
    ppermute x1, starting transfers between devices, on_device(): other = lax.ppermute(mine, 'leaf', pairs)  3.73 us
    pallas_call x1, Pallas kernels, on_device(): pl.pallas_call(finish_kernel, out_shape=(pltpu.HBM((rows, columns), F32),...  2.45 us
  transfers between devices with their start and end apart: 3, of which 3 were waited for; matrix products, arithmetic and copies ran while one was open for 0% of the time, Pallas kernels for 9%

profile of v6, /device:TPU:1, one launch (start us, length us, event | category | flops | bytes accessed | tf_op | source)
XLA Modules:
  0.0 65.4 jit_solution(14019948265497582971)
XLA Ops:
  0.6 0.1 pad_add_fusion.place
  0.7 11.0 %forward.1 = (bf16[16,1536,128]{2,1,0:T(8,128)(2,1)}, bf16[16,128,128]{2,1,0:T(8,128)(2,1)S(1)}, bf16[16,256,128]{2,1,0:T(8,128)(2,1)S(1)}, f32[64,1536]{1,0:T(8,128)S(1)}, f32[64,1536]{1,0:T(8,128)S(1)}) custom-call(s32[2]{0:T(128)S(1)} %pad_add_fusion.place, s32[1,1,15]{2,1,0:T(1,128)} %parent_hbm.3, f32[16,128,128]{2,1,0:T(8,128)} %bitcast.15, ...), custom_call_target="tpu_custom_call" | custom-call | tf_op jit(solution)/shard_map/forward/pallas_call | solution.py:315
  11.8 0.0 copy-start.1
  11.8 1.5 %collective-permute-start = (f32[64,1536]{1,0:T(8,128)S(1)}, f32[64,1536]{1,0:T(8,128)S(1)}, u32[]{:S(2)}, u32[]{:S(2)}) collective-permute-start(f32[64,1536]{1,0:T(8,128)S(1)} %get-tuple-element.20), channel_id=1, source_target_pairs={{0,8},{8,0},{16,24},{24,16},{32,40},{40,32},{48,56},{56,48},{64,72... | collective-permute-start | bytes 1179656 | tf_op jit(solution)/shard_map/ppermute | solution.py:398
  13.3 1.3 %collective-permute-done = f32[64,1536]{1,0:T(8,128)S(1)} collective-permute-done((f32[64,1536]{1,0:T(8,128)S(1)}, f32[64,1536]{1,0:T(8,128)S(1)}, u32[]{:S(2)}, u32[]{:S(2)}) %collective-permute-start) | collective-permute-done | bytes 393248 | tf_op jit(solution)/shard_map/ppermute | solution.py:398
  14.6 0.9 %add.3 = f32[64,1536]{1,0:T(8,128)} add(f32[64,1536]{1,0:T(8,128)S(1)} %get-tuple-element.19, f32[64,1536]{1,0:T(8,128)S(1)} %collective-permute-done) | non-fusion elementwise | flops 98304 | bytes 1179648 | tf_op jit(solution)/shard_map/add | solution.py:398
  15.5 0.0 copy-done.1
  15.5 6.1 %all-to-all-start = ((f32[8,8,1536]{2,1,0:T(8,128)}), f32[8,8,1536]{2,1,0:T(8,128)S(1)}, u32[]{:S(2)}, u32[]{:S(2)}) async-start(f32[8,8,1536]{2,1,0:T(8,128)} %bitcast.6), calls=%async_computation | async-start | bytes 786432 | tf_op jit(solution)/shard_map/all_to_all | solution.py:399
  21.6 0.0 copy-start.2
  21.6 1.0 %copy-done.2 = bf16[16,128,128]{2,1,0:T(8,128)(2,1)S(1)} copy-done((bf16[16,128,128]{2,1,0:T(8,128)(2,1)S(1)}, bf16[16,128,128]{2,1,0:T(8,128)(2,1)}, u32[]{:S(2)}) %copy-start.2) | copy-done | bytes 524312
  22.7 5.6 %separator.1 = (bf16[8,384,384]{2,1,0:T(8,128)(2,1)}, f32[16,128,128]{2,1,0:T(8,128)}, bf16[7,384,384]{2,1,0:T(8,128)(2,1)S(1)}) custom-call(s32[2]{0:T(128)S(1)} %pad_add_fusion.place, bf16[15,3,128,128]{3,2,1,0:T(8,128)(2,1)} %inverse_hbm.1, bf16[15,384,384]{2,1,0:T(8,128)(2,1)} %lower_hbm.1, bf16[14,384,384]{2,1,0:T(8,128)(2,1)} %coupling_hbm.1, ...), custom_call_target="tpu_custom_call" | custom-call | flops 6000000000 | bytes 20000000 | tf_op jit(solution)/shard_map/separator/pallas_call | solution.py:346
  28.2 0.2 all-to-all-done.parts
  28.5 0.2 level.1
  28.7 14.2 %all_to_all.15.gathered = f32[8,8,1152]{2,1,0:T(8,128)S(1)} all-to-all(f32[8,8,1152]{2,1,0:T(8,128)S(1)} %get-tuple-element.29), channel_id=1, replica_groups={{0,16,32,48,64,80,96,112},{8,24,40,56,72,88,104,120},{1,17,33,49,65,81,..., dimensions={0} | all-to-all | bytes 589824 | tf_op jit(solution)/shard_map/all_to_all | solution.py:413
  42.9 0.0 slice-start
  42.9 0.0 slice-start.1
  42.9 4.0 %tree.1 = f32[8,8,1536]{2,1,0:T(8,128)S(1)} custom-call(s32[2]{0:T(128)S(1)} %pad_add_fusion.place, f32[8,8,1152]{2,1,0:T(8,128)S(1)} %all_to_all.15.gathered, f32[8,384]{1,0:T(8,128)S(1)} %get-tuple-element.30.residue, bf16[8,384,384]{2,1,0:T(8,128)(2,1)} %get-tuple-element.31.full_hbm, bf16[7,384,384]{2,1,0:T(8,128)(2,1)S(1)} %get-tuple-element.28.product), custom_call_target="tpu_custom_call" | custom-call | flops 6000000000 | bytes 40000000 | tf_op jit(solution)/shard_map/tree/pallas_call | solution.py:414
  46.9 11.0 %all_to_all.16 = f32[8,8,1536]{2,1,0:T(8,128)S(1)} all-to-all(f32[8,8,1536]{2,1,0:T(8,128)S(1)} %tree.1), channel_id=1, replica_groups=mesh['leaf'=16,'rep'=8] {'rep'}, dimensions={0} | all-to-all | bytes 786432 | tf_op jit(solution)/shard_map/all_to_all | solution.py:429
  57.9 3.7 %collective-permute-start.1 = (f32[64,1536]{1,0:T(8,128)S(1)}, f32[64,1536]{1,0:T(8,128)S(1)}, u32[]{:S(2)}, u32[]{:S(2)}) collective-permute-start(f32[64,1536]{1,0:T(8,128)S(1)} %bitcast.12), channel_id=1, source_target_pairs={{0,8},{8,0},{16,24},{24,16},{32,40},{40,32},{48,56},{56,48},{64,72... | collective-permute-start | bytes 1179656 | tf_op jit(solution)/shard_map/ppermute | solution.py:430
  61.6 1.3 %collective-permute-done.1.other = f32[64,1536]{1,0:T(8,128)S(1)} collective-permute-done((f32[64,1536]{1,0:T(8,128)S(1)}, f32[64,1536]{1,0:T(8,128)S(1)}, u32[]{:S(2)}, u32[]{:S(2)}) %collective-permute-start.1) | collective-permute-done | bytes 393248 | tf_op jit(solution)/shard_map/ppermute | solution.py:430
  63.0 0.0 slice-done
  63.0 0.0 slice-done.1
  63.0 0.0 copy-done
  63.0 2.4 %finish.1 = (f32[2048,128]{1,0:T(8,128)}, f32[1536,128]{1,0:T(8,128)}) custom-call(s32[2]{0:T(128)S(1)} %pad_add_fusion.place, f32[64,1536]{1,0:T(8,128)S(1)} %bitcast.13, f32[64,1536]{1,0:T(8,128)S(1)} %collective-permute-done.1.other, f32[16,128,128]{2,1,0:T(8,128)S(1)} %copy-done, bf16[16,1536,128]{2,1,0:T(8,128)(2,1)S(1)} %bitcast.11), custom_call_target="tpu_custom_call" | custom-call | tf_op jit(solution)/shard_map/finish/pallas_call | solution.py:431
  (2 shorter events, 0.0 us)
Async XLA Ops:
  11.8 3.7 %copy-start.1 = (bf16[16,128,128]{2,1,0:T(8,128)(2,1)}, bf16[16,128,128]{2,1,0:T(8,128)(2,1)S(1)}, u32[]{:S(2)}) copy-start(bf16[16,128,128]{2,1,0:T(8,128)(2,1)S(1)} %get-tuple-element.22.forward_t) | copy-start | bytes 1572868
  11.8 2.9 %collective-permute-start = (f32[64,1536]{1,0:T(8,128)S(1)}, f32[64,1536]{1,0:T(8,128)S(1)}, u32[]{:S(2)}, u32[]{:S(2)}) collective-permute-start(f32[64,1536]{1,0:T(8,128)S(1)} %get-tuple-element.20), channel_id=1, source_target_pairs={{0,8},{8,0},{16,24},{24,16},{32,40},{40,32},{48,56},{56,48},{64,72... | collective-permute-start | bytes 1179656 | tf_op jit(solution)/shard_map/ppermute | solution.py:398
  15.5 13.0 %all-to-all-start = ((f32[8,8,1536]{2,1,0:T(8,128)}), f32[8,8,1536]{2,1,0:T(8,128)S(1)}, u32[]{:S(2)}, u32[]{:S(2)}) async-start(f32[8,8,1536]{2,1,0:T(8,128)} %bitcast.6), calls=%async_computation | async-start | bytes 786432 | tf_op jit(solution)/shard_map/all_to_all | solution.py:399
  21.6 1.0 %copy-start.2 = (bf16[16,128,128]{2,1,0:T(8,128)(2,1)S(1)}, bf16[16,128,128]{2,1,0:T(8,128)(2,1)}, u32[]{:S(2)}) copy-start(bf16[16,128,128]{2,1,0:T(8,128)(2,1)} %copy-done.1) | copy-start | bytes 1572868
  42.9 20.1 %slice-start = ((s8[6291456]{0:T(1024)(128)(4,1)}), s8[4194304]{0:T(1024)(128)(4,1)S(1)}, s32[]{:S(2)}) async-start(s8[6291456]{0:T(1024)(128)(4,1)} %bitcast.10), calls=%async_computation.3 | async-start | bytes 8388608
  42.9 20.1 %slice-start.1 = ((s8[6291456]{0:T(1024)(128)(4,1)}), s8[2097152]{0:T(1024)(128)(4,1)S(1)}, s32[]{:S(2)}) async-start(s8[6291456]{0:T(1024)(128)(4,1)} %bitcast.10), calls=%async_computation.4 | async-start | bytes 4194304
  42.9 20.1 %copy-start = (f32[16,128,128]{2,1,0:T(8,128)S(1)}, f32[16,128,128]{2,1,0:T(8,128)}, u32[]{:S(2)}) copy-start(f32[16,128,128]{2,1,0:T(8,128)} %get-tuple-element.32.base) | copy-start | bytes 3145732
  57.9 5.1 %collective-permute-start.1 = (f32[64,1536]{1,0:T(8,128)S(1)}, f32[64,1536]{1,0:T(8,128)S(1)}, u32[]{:S(2)}, u32[]{:S(2)}) collective-permute-start(f32[64,1536]{1,0:T(8,128)S(1)} %bitcast.12), channel_id=1, source_target_pairs={{0,8},{8,0},{16,24},{24,16},{32,40},{40,32},{48,56},{56,48},{64,72... | collective-permute-start | bytes 1179656 | tf_op jit(solution)/shard_map/ppermute | solution.py:430

commit v7 on v6

--- a/solution.py
+++ b/solution.py
@@ -40,8 +40,8 @@
 
 def forward_kernel(
     place, parent_hbm, right_hbm, inverse_hbm, below_hbm, coupling_hbm, sepright_hbm,
-    weights_hbm, forward_t, factors, keep, send,
-    weights_a, weights_b,
+    weights_hbm, forward_hbm, factors_hbm, keep, send,
+    forward_t, factors, weights_a, weights_b,
     parent, right, inverse, below, coupling, sepright, acc, rounded, sem, out_sem,
 ):
     leaf, rep = place[0], place[1]
@@ -104,12 +104,16 @@
 
     for k in reversed(range(LB - 1)):
         factor_step(k)
+    outward.append(pltpu.make_async_copy(factors, factors_hbm, out_sem.at[2 * LB + 1]))
+    outward[-1].start()
     for i in range(LB):
         if i % 4 == 0:
             quarters[i // 4].wait()
         weights_step(LB - 1 - i, 0)
         forward_step(i)
         weights_step(LB - 1 - i, 1)
+    outward.append(pltpu.make_async_copy(forward_t, forward_hbm, out_sem.at[2 * LB]))
+    outward[-1].start()
     for copy in others:
         copy.wait()
     values = rounded[...]
@@ -130,10 +134,19 @@
         copy.wait()
 
 
+def triangle(parts, zero):
+    rows = (
+        jnp.concatenate([parts[0], zero, zero], axis=1),
+        jnp.concatenate([parts[1], parts[2], zero], axis=1),
+        jnp.concatenate([parts[3], parts[4], parts[5]], axis=1),
+    )
+    return jnp.concatenate(rows, axis=0)
+
+
 def separator_kernel(
-    place, inverse_hbm, lower_hbm, coupling_hbm, parent_hbm, forward_t, factors,
-    full_hbm, base_hbm, product,
-    full, inverse, lowerpart, coupling, parent, base, base_low, sem, out_sem,
+    place, inverse_hbm, lower_hbm, coupling_hbm, parent_hbm, forward_hbm, factors_hbm,
+    base_hbm, full, product,
+    blocks, inverse, lowerpart, coupling, parent, forward_t, factors, base, base_low, sem,
 ):
     shared = first_number(1)
     number = shared + (place[0] >> 1)
@@ -160,8 +173,12 @@
                 sem.at[k + 2],
             )
         )
-    fetched = pltpu.make_async_copy(parent_hbm, parent, sem.at[6])
-    for copy in [fetched] + triangles + couplings:
+    fetched = [
+        pltpu.make_async_copy(parent_hbm, parent, sem.at[6]),
+        pltpu.make_async_copy(forward_hbm, forward_t, sem.at[7]),
+        pltpu.make_async_copy(factors_hbm, factors, sem.at[9]),
+    ]
+    for copy in fetched + triangles + couplings:
         copy.start()
     remaining = list(reversed(range(LB)))
 
@@ -177,11 +194,11 @@
             base[k] = value
             base_low[k] = value.astype(BF16)
 
-    fetched.wait()
+    for copy in fetched:
+        copy.wait()
     base_steps(3)
     for copy in triangles:
         copy.wait()
-    outward = []
     zero = jnp.zeros((NB, NB), BF16)
     one, two, three = slice(0, NB), slice(NB, 2 * NB), slice(2 * NB, 3 * NB)
     members = range(shared + 1)
@@ -201,24 +218,24 @@
     base_steps(1)
     x20 = {m: (-mm(inv[m][2], t20[m])).astype(BF16) for m in members}
     for m in members:
-        full[m, one, :] = jnp.concatenate([inv[m][0], zero, zero], axis=1)
-        full[m, two, :] = jnp.concatenate([x10[m], inv[m][1], zero], axis=1)
-        full[m, three, :] = jnp.concatenate([x20[m], x21[m], inv[m][2]], axis=1)
-        outward.append(pltpu.make_async_copy(full.at[m], full_hbm.at[m], out_sem.at[m]))
-        outward[-1].start()
+        for j, block in enumerate((inv[m][0], x10[m], inv[m][1], x20[m], x21[m], inv[m][2])):
+            blocks[m, j] = block
+    for h in range(1, LEV + 1):
+        full[h - 1] = blocks[shared if h == 1 else first_number(h) + (place[0] >> h)]
     for copy in couplings:
         copy.wait()
+    outward = pltpu.make_async_copy(base, base_hbm, sem.at[8])
     for m in members[1:]:
         base_steps(2)
-        product[m - 1] = mm(coupling[m - 1], full[m]).astype(BF16)
-        if not remaining and len(outward) == len(members):
-            outward.append(pltpu.make_async_copy(base, base_hbm, out_sem.at[len(members)]))
-            outward[-1].start()
-    for copy in outward:
-        copy.wait()
-
-
-def level_kernel(parts, product, out, residue):
+        if m == 4:
+            base_steps(LB)
+            outward.start()
+        matrix = triangle((inv[m][0], x10[m], inv[m][1], x20[m], x21[m], inv[m][2]), zero)
+        product[m - 1] = mm(coupling[m - 1], matrix).astype(BF16)
+    outward.wait()
+
+
+def level_kernel(parts, product, _full, out, residue):
     total = parts[0]
     for j in range(1, parts.shape[0]):
         total = total + parts[j]
@@ -231,15 +248,9 @@
 
 
 def tree_kernel(
-    place, gathered, residue, full_hbm, product, out, res2, res3, full, sem,
+    place, gathered, residue, full, product, out, res2, res3,
 ):
     leaf = place[0]
-    early = []
-    for h in range(1, LEV + 1):
-        number = first_number(1) if h == 1 else first_number(h) + (leaf >> h)
-        early.append(pltpu.make_async_copy(full_hbm.at[number], full.at[h - 1], sem.at[h - 1]))
-    for copy in early:
-        copy.start()
     span = [slice(h * S, (h + 1) * S) for h in range(LEV)]
     residues = []
     for h in range(2, LEV + 1):
@@ -260,13 +271,11 @@
                 res3[g] = r
             following.append(r if h == LEV else r.astype(BF16))
         residues = following
-        if h == 2:
-            for copy in early:
-                copy.wait()
     own = [residue[...], res2[leaf >> 2], res3[leaf >> 3], residues[0]]
     scaled = [None] * LEV
+    zero = jnp.zeros((NB, NB), BF16)
     for h in range(LEV, 0, -1):
-        matrix = full[h - 1]
+        matrix = triangle([full[h - 1, j] for j in range(6)], zero)
         scaled[h - 1] = mm(mm_nt(own[h - 1].astype(BF16), matrix).astype(BF16), matrix)
     above = None
     for h in range(LEV, 0, -1):
@@ -316,14 +325,16 @@
         forward_kernel,
         out_shape=(
             pltpu.HBM((LB, height, NB), BF16),
-            shape((LB, columns, NB), BF16),
-            shape((LB, 2 * NB, NB), BF16),
+            pltpu.HBM((LB, columns, NB), BF16),
+            pltpu.HBM((LB, 2 * NB, NB), BF16),
             shape((half, height)),
             shape((half, height)),
         ),
         in_specs=[SMEM] + [HBM] * 6,
-        out_specs=(HBM,) + (VMEM,) * 4,
+        out_specs=(HBM,) * 3 + (VMEM,) * 2,
         scratch_shapes=[
+            pltpu.VMEM((LB, columns, NB), BF16),
+            pltpu.VMEM((LB, 2 * NB, NB), BF16),
             pltpu.VMEM((LB, height // 2, NB), BF16),
             pltpu.VMEM((LB, height // 2, NB), BF16),
             pltpu.SMEM((1, 1, LB - 1), jnp.int32),
@@ -335,7 +346,7 @@
             pltpu.VMEM((LB, NB, columns), F32),
             pltpu.VMEM((rows, columns), BF16),
             pltpu.SemaphoreType.DMA((12,)),
-            pltpu.SemaphoreType.DMA((2 * LB,)),
+            pltpu.SemaphoreType.DMA((2 * LB + 2,)),
         ],
         compiler_params=limit(30),
         name="forward",
@@ -346,27 +357,28 @@
     return pl.pallas_call(
         separator_kernel,
         out_shape=(
-            pltpu.HBM((8, S, S), BF16),
             pltpu.HBM(forward_t.shape, F32),
+            shape((LEV, 6, NB, NB), BF16),
             shape((7, S, S), BF16),
         ),
-        in_specs=[SMEM] + [HBM] * 4 + [VMEM] * 2,
-        out_specs=(HBM, HBM, VMEM),
+        in_specs=[SMEM] + [HBM] * 6,
+        out_specs=(HBM, VMEM, VMEM),
         scratch_shapes=[
-            pltpu.VMEM((8, S, S), BF16),
+            pltpu.VMEM((8, 6, NB, NB), BF16),
             pltpu.VMEM((8, SB, NB, NB), BF16),
             pltpu.VMEM((8, 2 * NB, 2 * NB), BF16),
             pltpu.VMEM((7, S, S), BF16),
             pltpu.SMEM((1, 1, LB - 1), jnp.int32),
+            pltpu.VMEM(forward_t.shape, BF16),
+            pltpu.VMEM(factors.shape, BF16),
             pltpu.VMEM(forward_t.shape, F32),
             pltpu.VMEM(forward_t.shape, BF16),
-            pltpu.SemaphoreType.DMA((7,)),
-            pltpu.SemaphoreType.DMA((9,)),
+            pltpu.SemaphoreType.DMA((10,)),
         ],
         compiler_params=limit(16),
         cost_estimate=pl.CostEstimate(flops=6 * 10**9, transcendentals=0, bytes_accessed=2 * 10**7),
         name="separator",
-    )(place, *in_hbm(inverse, lowerpart, coupling, parent), forward_t, factors)
+    )(place, *in_hbm(inverse, lowerpart, coupling, parent, forward_t, factors))
 
 
 def on_device(
@@ -398,34 +410,32 @@
     total = keep + lax.ppermute(send, "leaf", pairs)
     parts = lax.all_to_all(total.reshape(reps, CH, height), "rep", 0, 0, tiled=True)
     place_after, _ = lax.optimization_barrier((place, total))
-    full, base, product = run_separator(
+    base, full, product = run_separator(
         place_after, separator_inverse, separator_lower, parent_coupling, local_parent, forward_t, factors
     )
     parts, full, base, product = lax.optimization_barrier((parts, full, base, product))
     summed, residue = pl.pallas_call(
         level_kernel,
         out_shape=(shape((leaves // 2, CH, height - S)), shape((CH, S))),
-        in_specs=[VMEM] * 2,
+        in_specs=[VMEM] * 2 + [pl.BlockSpec(memory_space=pl.ANY)],
         out_specs=(VMEM, VMEM),
         compiler_params=limit(8),
         name="level",
-    )(parts, product)
+    )(parts, product, full)
     gathered = lax.all_to_all(summed, "leaf", 0, 0, axis_index_groups=chips, tiled=True)
     solved = pl.pallas_call(
         tree_kernel,
         out_shape=shape((reps, CH, height)),
-        in_specs=[SMEM, VMEM, VMEM, HBM, VMEM],
+        in_specs=[SMEM] + [VMEM] * 4,
         out_specs=VMEM,
         scratch_shapes=[
             pltpu.VMEM((4, CH, S), F32),
             pltpu.VMEM((2, CH, S), F32),
-            pltpu.VMEM((LEV, S, S), BF16),
-            pltpu.SemaphoreType.DMA((LEV,)),
         ],
         compiler_params=limit(12),
         cost_estimate=pl.CostEstimate(flops=6 * 10**9, transcendentals=0, bytes_accessed=4 * 10**7),
         name="tree",
-    )(place, gathered, residue, *in_hbm(full), product)
+    )(place, gathered, residue, full, product)
     mine = lax.all_to_all(solved, "rep", 0, 0, tiled=True).reshape(half, height)
     other = lax.ppermute(mine, "leaf", pairs)
     local, separators = pl.pallas_call(

time: 65.7 us -> 63.7 us (0.970)
  Pallas kernels: 23.3 us -> 22.1 us
  local copies, waits for them, and re-layouts: 1.06 us -> 0.01 us
    pallas_call x1, Pallas kernels: 4.01 us -> 2.36 us  [on_device(): pl.pallas_call(tree_kernel, out_shape=shape((reps, CH, height)), in_specs...]
    unnamed x10 -> x6, local copies, waits for them, and re-layouts: 1.06 us -> 0.01 us
where the time goes in v7:
time: 63.7 us; the launch traced here: 63.4 us
  blocking collectives  25.2 us (40%)
  Pallas kernels  22.1 us (35%)
  starting transfers between devices  11.1 us (17%)
  waiting for transfers between devices  3.55 us (6%)
  other arithmetic  0.85 us (1%)
  between operations  0.66 us (1%)
    all_to_all x1, blocking collectives, on_device(): lax.all_to_all(summed, 'leaf', 0, 0, axis_index_groups=chips, tiled=True)  14.2 us
    pallas_call x1, Pallas kernels, run_forward(): pl.pallas_call(forward_kernel, out_shape=(pltpu.HBM((LB, height, NB), BF1...  11 us
    all_to_all x1, blocking collectives, on_device(): mine = lax.all_to_all(solved, 'rep', 0, 0, tiled=True).reshape(half, height)  11 us
    all_to_all x1, starting transfers between devices, on_device(): lax.all_to_all(total.reshape(reps, CH, height), 'rep', 0, 0, tiled=True)  6.13 us
    pallas_call x1, Pallas kernels, run_separator(): pl.pallas_call(separator_kernel, out_shape=(pltpu.HBM(forward_t.shape, F3...  6.02 us
    ppermute x1, starting transfers between devices, on_device(): other = lax.ppermute(mine, 'leaf', pairs)  3.43 us
    pallas_call x1, Pallas kernels, on_device(): pl.pallas_call(finish_kernel, out_shape=(pltpu.HBM((rows, columns), F32),...  2.44 us
    pallas_call x1, Pallas kernels, on_device(): pl.pallas_call(tree_kernel, out_shape=shape((reps, CH, height)), in_specs...  2.36 us
  transfers between devices with their start and end apart: 3, of which 3 were waited for; matrix products, arithmetic and copies ran while one was open for 0% of the time, Pallas kernels for 9%

profile of v7, /device:TPU:1, one launch (start us, length us, event | category | flops | bytes accessed | tf_op | source)
XLA Modules:
  0.0 63.4 jit_solution(9166500802552175895)
XLA Ops:
  0.6 0.1 pad_add_fusion.place
  0.7 11.0 %forward.1 = (bf16[16,1536,128]{2,1,0:T(8,128)(2,1)}, bf16[16,128,128]{2,1,0:T(8,128)(2,1)}, bf16[16,256,128]{2,1,0:T(8,128)(2,1)}, f32[64,1536]{1,0:T(8,128)S(1)}, f32[64,1536]{1,0:T(8,128)S(1)}) custom-call(s32[2]{0:T(128)S(1)} %pad_add_fusion.place, s32[1,1,15]{2,1,0:T(1,128)} %parent_hbm.3, f32[16,128,128]{2,1,0:T(8,128)} %bitcast.15, ...), custom_call_target="tpu_custom_call" | custom-call | tf_op jit(solution)/shard_map/forward/pallas_call | solution.py:324
  11.8 1.5 %collective-permute-start = (f32[64,1536]{1,0:T(8,128)S(1)}, f32[64,1536]{1,0:T(8,128)S(1)}, u32[]{:S(2)}, u32[]{:S(2)}) collective-permute-start(f32[64,1536]{1,0:T(8,128)S(1)} %get-tuple-element.20), channel_id=1, source_target_pairs={{0,8},{8,0},{16,24},{24,16},{32,40},{40,32},{48,56},{56,48},{64,72... | collective-permute-start | bytes 1179656 | tf_op jit(solution)/shard_map/ppermute | solution.py:410
  13.3 1.3 %collective-permute-done = f32[64,1536]{1,0:T(8,128)S(1)} collective-permute-done((f32[64,1536]{1,0:T(8,128)S(1)}, f32[64,1536]{1,0:T(8,128)S(1)}, u32[]{:S(2)}, u32[]{:S(2)}) %collective-permute-start) | collective-permute-done | bytes 393248 | tf_op jit(solution)/shard_map/ppermute | solution.py:410
  14.6 0.8 %add.3 = f32[64,1536]{1,0:T(8,128)} add(f32[64,1536]{1,0:T(8,128)S(1)} %get-tuple-element.19, f32[64,1536]{1,0:T(8,128)S(1)} %collective-permute-done) | non-fusion elementwise | flops 98304 | bytes 1179648 | tf_op jit(solution)/shard_map/add | solution.py:410
  15.4 6.1 %all-to-all-start = ((f32[8,8,1536]{2,1,0:T(8,128)}), f32[8,8,1536]{2,1,0:T(8,128)S(1)}, u32[]{:S(2)}, u32[]{:S(2)}) async-start(f32[8,8,1536]{2,1,0:T(8,128)} %bitcast.6), calls=%async_computation | async-start | bytes 786432 | tf_op jit(solution)/shard_map/all_to_all | solution.py:411
  21.5 6.0 %separator.1 = (f32[16,128,128]{2,1,0:T(8,128)}, bf16[4,6,128,128]{3,2,1,0:T(8,128)(2,1)S(1)}, bf16[7,384,384]{2,1,0:T(8,128)(2,1)S(1)}) custom-call(s32[2]{0:T(128)S(1)} %pad_add_fusion.place, bf16[15,3,128,128]{3,2,1,0:T(8,128)(2,1)} %inverse_hbm.1, bf16[15,384,384]{2,1,0:T(8,128)(2,1)} %lower_hbm.1, bf16[14,384,384]{2,1,0:T(8,128)(2,1)} %coupling_hbm.1, ...), custom_call_target="tpu_custom_call" | custom-call | flops 6000000000 | bytes 20000000 | tf_op jit(solution)/shard_map/separator/pallas_call | solution.py:357
  27.6 0.8 %all-to-all-done.parts = f32[8,8,1536]{2,1,0:T(8,128)S(1)} async-done(((f32[8,8,1536]{2,1,0:T(8,128)}), f32[8,8,1536]{2,1,0:T(8,128)S(1)}, u32[]{:S(2)}, u32[]{:S(2)}) %all-to-all-start) | async-done | bytes 393248 | tf_op jit(solution)/shard_map/all_to_all | solution.py:411
  28.4 0.2 level.1
  28.6 14.2 %all_to_all.15.gathered = f32[8,8,1152]{2,1,0:T(8,128)S(1)} all-to-all(f32[8,8,1152]{2,1,0:T(8,128)S(1)} %get-tuple-element.30), channel_id=1, replica_groups={{0,16,32,48,64,80,96,112},{8,24,40,56,72,88,104,120},{1,17,33,49,65,81,..., dimensions={0} | all-to-all | bytes 589824 | tf_op jit(solution)/shard_map/all_to_all | solution.py:425
  42.8 0.0 slice-start
  42.8 0.0 slice-start.1
  42.8 0.0 copy-start
  42.8 2.4 %tree.1 = f32[8,8,1536]{2,1,0:T(8,128)S(1)} custom-call(s32[2]{0:T(128)S(1)} %pad_add_fusion.place, f32[8,8,1152]{2,1,0:T(8,128)S(1)} %all_to_all.15.gathered, f32[8,384]{1,0:T(8,128)S(1)} %get-tuple-element.31.residue, bf16[4,6,128,128]{3,2,1,0:T(8,128)(2,1)S(1)} %get-tuple-element.29._full.full, bf16[7,384,384]{2,1,0:T(8,128)(2,1)S(1)} %get-tuple-element.28.product), custom_call_target="tpu_custom_call" | custom-call | flops 6000000000 | bytes 40000000 | tf_op jit(solution)/shard_map/tree/pallas_call | solution.py:426
  45.2 11.0 %all_to_all.16 = f32[8,8,1536]{2,1,0:T(8,128)S(1)} all-to-all(f32[8,8,1536]{2,1,0:T(8,128)S(1)} %tree.1), channel_id=1, replica_groups=mesh['leaf'=16,'rep'=8] {'rep'}, dimensions={0} | all-to-all | bytes 786432 | tf_op jit(solution)/shard_map/all_to_all | solution.py:439
  56.2 3.4 %collective-permute-start.1 = (f32[64,1536]{1,0:T(8,128)S(1)}, f32[64,1536]{1,0:T(8,128)S(1)}, u32[]{:S(2)}, u32[]{:S(2)}) collective-permute-start(f32[64,1536]{1,0:T(8,128)S(1)} %bitcast.12), channel_id=1, source_target_pairs={{0,8},{8,0},{16,24},{24,16},{32,40},{40,32},{48,56},{56,48},{64,72... | collective-permute-start | bytes 1179656 | tf_op jit(solution)/shard_map/ppermute | solution.py:440
  59.6 1.3 %collective-permute-done.1.other = f32[64,1536]{1,0:T(8,128)S(1)} collective-permute-done((f32[64,1536]{1,0:T(8,128)S(1)}, f32[64,1536]{1,0:T(8,128)S(1)}, u32[]{:S(2)}, u32[]{:S(2)}) %collective-permute-start.1) | collective-permute-done | bytes 393248 | tf_op jit(solution)/shard_map/ppermute | solution.py:440
  61.0 0.0 slice-done
  61.0 0.0 slice-done.1
  61.0 0.0 copy-done
  61.0 2.4 %finish.1 = (f32[2048,128]{1,0:T(8,128)}, f32[1536,128]{1,0:T(8,128)}) custom-call(s32[2]{0:T(128)S(1)} %pad_add_fusion.place, f32[64,1536]{1,0:T(8,128)S(1)} %bitcast.13, f32[64,1536]{1,0:T(8,128)S(1)} %collective-permute-done.1.other, f32[16,128,128]{2,1,0:T(8,128)S(1)} %copy-done, bf16[16,1536,128]{2,1,0:T(8,128)(2,1)S(1)} %bitcast.11), custom_call_target="tpu_custom_call" | custom-call | tf_op jit(solution)/shard_map/finish/pallas_call | solution.py:441
  (1 shorter events, 0.0 us)
Async XLA Ops:
  11.8 2.9 %collective-permute-start = (f32[64,1536]{1,0:T(8,128)S(1)}, f32[64,1536]{1,0:T(8,128)S(1)}, u32[]{:S(2)}, u32[]{:S(2)}) collective-permute-start(f32[64,1536]{1,0:T(8,128)S(1)} %get-tuple-element.20), channel_id=1, source_target_pairs={{0,8},{8,0},{16,24},{24,16},{32,40},{40,32},{48,56},{56,48},{64,72... | collective-permute-start | bytes 1179656 | tf_op jit(solution)/shard_map/ppermute | solution.py:410
  15.4 13.0 %all-to-all-start = ((f32[8,8,1536]{2,1,0:T(8,128)}), f32[8,8,1536]{2,1,0:T(8,128)S(1)}, u32[]{:S(2)}, u32[]{:S(2)}) async-start(f32[8,8,1536]{2,1,0:T(8,128)} %bitcast.6), calls=%async_computation | async-start | bytes 786432 | tf_op jit(solution)/shard_map/all_to_all | solution.py:411
  42.8 18.2 %slice-start = ((s8[6291456]{0:T(1024)(128)(4,1)}), s8[4194304]{0:T(1024)(128)(4,1)S(1)}, s32[]{:S(2)}) async-start(s8[6291456]{0:T(1024)(128)(4,1)} %bitcast.10), calls=%async_computation.3 | async-start | bytes 8388608
  42.8 18.2 %slice-start.1 = ((s8[6291456]{0:T(1024)(128)(4,1)}), s8[2097152]{0:T(1024)(128)(4,1)S(1)}, s32[]{:S(2)}) async-start(s8[6291456]{0:T(1024)(128)(4,1)} %bitcast.10), calls=%async_computation.4 | async-start | bytes 4194304
  42.8 18.2 %copy-start = (f32[16,128,128]{2,1,0:T(8,128)S(1)}, f32[16,128,128]{2,1,0:T(8,128)}, u32[]{:S(2)}) copy-start(f32[16,128,128]{2,1,0:T(8,128)} %get-tuple-element.32.base) | copy-start | bytes 3145732
  56.2 4.8 %collective-permute-start.1 = (f32[64,1536]{1,0:T(8,128)S(1)}, f32[64,1536]{1,0:T(8,128)S(1)}, u32[]{:S(2)}, u32[]{:S(2)}) collective-permute-start(f32[64,1536]{1,0:T(8,128)S(1)} %bitcast.12), channel_id=1, source_target_pairs={{0,8},{8,0},{16,24},{24,16},{32,40},{40,32},{48,56},{56,48},{64,72... | collective-permute-start | bytes 1179656 | tf_op jit(solution)/shard_map/ppermute | solution.py:440

commit v8 on v7

--- a/solution.py
+++ b/solution.py
@@ -233,6 +233,10 @@
         matrix = triangle((inv[m][0], x10[m], inv[m][1], x20[m], x21[m], inv[m][2]), zero)
         product[m - 1] = mm(coupling[m - 1], matrix).astype(BF16)
     outward.wait()
+
+
+def sum_kernel(first, second, out):
+    out[...] = first[...] + second[...]
 
 
 def level_kernel(parts, product, _full, out, residue):
@@ -407,7 +411,14 @@
     weights, forward_t, factors, keep, send = run_forward(
         place, local_parent, right, local_inverse[0, 0], local_below[0, 0], coupling, separator_right
     )
-    total = keep + lax.ppermute(send, "leaf", pairs)
+    total = pl.pallas_call(
+        sum_kernel,
+        out_shape=shape((half, height)),
+        in_specs=[VMEM] * 2,
+        out_specs=VMEM,
+        compiler_params=limit(8),
+        name="sum",
+    )(keep, lax.ppermute(send, "leaf", pairs))
     parts = lax.all_to_all(total.reshape(reps, CH, height), "rep", 0, 0, tiled=True)
     place_after, _ = lax.optimization_barrier((place, total))
     base, full, product = run_separator(

time: 63.7 us -> 63.7 us (level)
  other arithmetic: 0.85 us -> 0.08 us
  Pallas kernels: 22.1 us -> 22.8 us
    add x1 -> x0, other arithmetic: 0.78 us -> none  [on_device(): total = keep + lax.ppermute(send, 'leaf', pairs)]
    pallas_call x0 -> x1, Pallas kernels: none -> 0.77 us  [on_device(): pl.pallas_call(sum_kernel, out_shape=shape((half, height)), in_specs=[VME...]
where the time goes in v8:
time: 63.7 us; the launch traced here: 63.4 us
  blocking collectives  25.2 us (40%)
  Pallas kernels  22.8 us (36%)
  starting transfers between devices  11.1 us (17%)
  waiting for transfers between devices  3.55 us (6%)
  between operations  0.66 us (1%)
    all_to_all x1, blocking collectives, on_device(): lax.all_to_all(summed, 'leaf', 0, 0, axis_index_groups=chips, tiled=True)  14.2 us
    pallas_call x1, Pallas kernels, run_forward(): pl.pallas_call(forward_kernel, out_shape=(pltpu.HBM((LB, height, NB), BF1...  11 us
    all_to_all x1, blocking collectives, on_device(): mine = lax.all_to_all(solved, 'rep', 0, 0, tiled=True).reshape(half, height)  11 us
    all_to_all x1, starting transfers between devices, on_device(): lax.all_to_all(total.reshape(reps, CH, height), 'rep', 0, 0, tiled=True)  6.13 us
    pallas_call x1, Pallas kernels, run_separator(): pl.pallas_call(separator_kernel, out_shape=(pltpu.HBM(forward_t.shape, F3...  6.01 us
    ppermute x1, starting transfers between devices, on_device(): other = lax.ppermute(mine, 'leaf', pairs)  3.43 us
    pallas_call x1, Pallas kernels, on_device(): pl.pallas_call(finish_kernel, out_shape=(pltpu.HBM((rows, columns), F32),...  2.45 us
    pallas_call x1, Pallas kernels, on_device(): pl.pallas_call(tree_kernel, out_shape=shape((reps, CH, height)), in_specs...  2.36 us
  transfers between devices with their start and end apart: 3, of which 3 were waited for; matrix products, arithmetic and copies ran while one was open for 0% of the time, Pallas kernels for 9%

profile of v8, /device:TPU:1, one launch (start us, length us, event | category | flops | bytes accessed | tf_op | source)
XLA Modules:
  0.0 63.4 jit_solution(15514739667765625463)
XLA Ops:
  0.6 0.1 pad_add_fusion.place
  0.7 11.0 %forward.1 = (bf16[16,1536,128]{2,1,0:T(8,128)(2,1)}, bf16[16,128,128]{2,1,0:T(8,128)(2,1)}, bf16[16,256,128]{2,1,0:T(8,128)(2,1)}, f32[64,1536]{1,0:T(8,128)S(1)}, f32[64,1536]{1,0:T(8,128)S(1)}) custom-call(s32[2]{0:T(128)S(1)} %pad_add_fusion.place, s32[1,1,15]{2,1,0:T(1,128)} %parent_hbm.3, f32[16,128,128]{2,1,0:T(8,128)} %bitcast.15, ...), custom_call_target="tpu_custom_call" | custom-call | tf_op jit(solution)/shard_map/forward/pallas_call | solution.py:328
  11.8 1.5 %collective-permute-start = (f32[64,1536]{1,0:T(8,128)S(1)}, f32[64,1536]{1,0:T(8,128)S(1)}, u32[]{:S(2)}, u32[]{:S(2)}) collective-permute-start(f32[64,1536]{1,0:T(8,128)S(1)} %get-tuple-element.20), channel_id=1, source_target_pairs={{0,8},{8,0},{16,24},{24,16},{32,40},{40,32},{48,56},{56,48},{64,72... | collective-permute-start | bytes 1179656 | tf_op jit(solution)/shard_map/ppermute | solution.py:421
  13.3 1.3 %collective-permute-done.second = f32[64,1536]{1,0:T(8,128)S(1)} collective-permute-done((f32[64,1536]{1,0:T(8,128)S(1)}, f32[64,1536]{1,0:T(8,128)S(1)}, u32[]{:S(2)}, u32[]{:S(2)}) %collective-permute-start) | collective-permute-done | bytes 393248 | tf_op jit(solution)/shard_map/ppermute | solution.py:421
  14.6 0.8 %sum.1 = f32[64,1536]{1,0:T(8,128)} custom-call(f32[64,1536]{1,0:T(8,128)S(1)} %get-tuple-element.19.first, f32[64,1536]{1,0:T(8,128)S(1)} %collective-permute-done.second), custom_call_target="tpu_custom_call" | custom-call | tf_op jit(solution)/shard_map/sum/pallas_call | solution.py:414
  15.4 6.1 %all-to-all-start = ((f32[8,8,1536]{2,1,0:T(8,128)}), f32[8,8,1536]{2,1,0:T(8,128)S(1)}, u32[]{:S(2)}, u32[]{:S(2)}) async-start(f32[8,8,1536]{2,1,0:T(8,128)} %bitcast.6), calls=%async_computation | async-start | bytes 786432 | tf_op jit(solution)/shard_map/all_to_all | solution.py:422
  21.5 6.0 %separator.1 = (f32[16,128,128]{2,1,0:T(8,128)}, bf16[4,6,128,128]{3,2,1,0:T(8,128)(2,1)S(1)}, bf16[7,384,384]{2,1,0:T(8,128)(2,1)S(1)}) custom-call(s32[2]{0:T(128)S(1)} %pad_add_fusion.place, bf16[15,3,128,128]{3,2,1,0:T(8,128)(2,1)} %inverse_hbm.1, bf16[15,384,384]{2,1,0:T(8,128)(2,1)} %lower_hbm.1, bf16[14,384,384]{2,1,0:T(8,128)(2,1)} %coupling_hbm.1, ...), custom_call_target="tpu_custom_call" | custom-call | flops 6000000000 | bytes 20000000 | tf_op jit(solution)/shard_map/separator/pallas_call | solution.py:361
  27.5 0.9 %all-to-all-done.parts = f32[8,8,1536]{2,1,0:T(8,128)S(1)} async-done(((f32[8,8,1536]{2,1,0:T(8,128)}), f32[8,8,1536]{2,1,0:T(8,128)S(1)}, u32[]{:S(2)}, u32[]{:S(2)}) %all-to-all-start) | async-done | bytes 393248 | tf_op jit(solution)/shard_map/all_to_all | solution.py:422
  28.4 0.2 level.1
  28.6 14.2 %all_to_all.15.gathered = f32[8,8,1152]{2,1,0:T(8,128)S(1)} all-to-all(f32[8,8,1152]{2,1,0:T(8,128)S(1)} %get-tuple-element.30), channel_id=1, replica_groups={{0,16,32,48,64,80,96,112},{8,24,40,56,72,88,104,120},{1,17,33,49,65,81,..., dimensions={0} | all-to-all | bytes 589824 | tf_op jit(solution)/shard_map/all_to_all | solution.py:436
  42.8 0.0 slice-start
  42.8 0.0 slice-start.1
  42.8 0.0 copy-start
  42.8 2.4 %tree.1 = f32[8,8,1536]{2,1,0:T(8,128)S(1)} custom-call(s32[2]{0:T(128)S(1)} %pad_add_fusion.place, f32[8,8,1152]{2,1,0:T(8,128)S(1)} %all_to_all.15.gathered, f32[8,384]{1,0:T(8,128)S(1)} %get-tuple-element.31.residue, bf16[4,6,128,128]{3,2,1,0:T(8,128)(2,1)S(1)} %get-tuple-element.29._full.full, bf16[7,384,384]{2,1,0:T(8,128)(2,1)S(1)} %get-tuple-element.28.product), custom_call_target="tpu_custom_call" | custom-call | flops 6000000000 | bytes 40000000 | tf_op jit(solution)/shard_map/tree/pallas_call | solution.py:437
  45.2 11.0 %all_to_all.16 = f32[8,8,1536]{2,1,0:T(8,128)S(1)} all-to-all(f32[8,8,1536]{2,1,0:T(8,128)S(1)} %tree.1), channel_id=1, replica_groups=mesh['leaf'=16,'rep'=8] {'rep'}, dimensions={0} | all-to-all | bytes 786432 | tf_op jit(solution)/shard_map/all_to_all | solution.py:450
  56.2 3.4 %collective-permute-start.1 = (f32[64,1536]{1,0:T(8,128)S(1)}, f32[64,1536]{1,0:T(8,128)S(1)}, u32[]{:S(2)}, u32[]{:S(2)}) collective-permute-start(f32[64,1536]{1,0:T(8,128)S(1)} %bitcast.12), channel_id=1, source_target_pairs={{0,8},{8,0},{16,24},{24,16},{32,40},{40,32},{48,56},{56,48},{64,72... | collective-permute-start | bytes 1179656 | tf_op jit(solution)/shard_map/ppermute | solution.py:451
  59.6 1.3 %collective-permute-done.1.other = f32[64,1536]{1,0:T(8,128)S(1)} collective-permute-done((f32[64,1536]{1,0:T(8,128)S(1)}, f32[64,1536]{1,0:T(8,128)S(1)}, u32[]{:S(2)}, u32[]{:S(2)}) %collective-permute-start.1) | collective-permute-done | bytes 393248 | tf_op jit(solution)/shard_map/ppermute | solution.py:451
  61.0 0.0 slice-done
  61.0 0.0 slice-done.1
  61.0 0.0 copy-done
  61.0 2.5 %finish.1 = (f32[2048,128]{1,0:T(8,128)}, f32[1536,128]{1,0:T(8,128)}) custom-call(s32[2]{0:T(128)S(1)} %pad_add_fusion.place, f32[64,1536]{1,0:T(8,128)S(1)} %bitcast.13, f32[64,1536]{1,0:T(8,128)S(1)} %collective-permute-done.1.other, f32[16,128,128]{2,1,0:T(8,128)S(1)} %copy-done, bf16[16,1536,128]{2,1,0:T(8,128)(2,1)S(1)} %bitcast.11), custom_call_target="tpu_custom_call" | custom-call | tf_op jit(solution)/shard_map/finish/pallas_call | solution.py:452
  (1 shorter events, 0.0 us)
Async XLA Ops:
  11.8 2.9 %collective-permute-start = (f32[64,1536]{1,0:T(8,128)S(1)}, f32[64,1536]{1,0:T(8,128)S(1)}, u32[]{:S(2)}, u32[]{:S(2)}) collective-permute-start(f32[64,1536]{1,0:T(8,128)S(1)} %get-tuple-element.20), channel_id=1, source_target_pairs={{0,8},{8,0},{16,24},{24,16},{32,40},{40,32},{48,56},{56,48},{64,72... | collective-permute-start | bytes 1179656 | tf_op jit(solution)/shard_map/ppermute | solution.py:421
  15.4 13.0 %all-to-all-start = ((f32[8,8,1536]{2,1,0:T(8,128)}), f32[8,8,1536]{2,1,0:T(8,128)S(1)}, u32[]{:S(2)}, u32[]{:S(2)}) async-start(f32[8,8,1536]{2,1,0:T(8,128)} %bitcast.6), calls=%async_computation | async-start | bytes 786432 | tf_op jit(solution)/shard_map/all_to_all | solution.py:422
  42.8 18.2 %slice-start = ((s8[6291456]{0:T(1024)(128)(4,1)}), s8[4194304]{0:T(1024)(128)(4,1)S(1)}, s32[]{:S(2)}) async-start(s8[6291456]{0:T(1024)(128)(4,1)} %bitcast.10), calls=%async_computation.3 | async-start | bytes 8388608
  42.8 18.2 %slice-start.1 = ((s8[6291456]{0:T(1024)(128)(4,1)}), s8[2097152]{0:T(1024)(128)(4,1)S(1)}, s32[]{:S(2)}) async-start(s8[6291456]{0:T(1024)(128)(4,1)} %bitcast.10), calls=%async_computation.4 | async-start | bytes 4194304
  42.8 18.2 %copy-start = (f32[16,128,128]{2,1,0:T(8,128)S(1)}, f32[16,128,128]{2,1,0:T(8,128)}, u32[]{:S(2)}) copy-start(f32[16,128,128]{2,1,0:T(8,128)} %get-tuple-element.32.base) | copy-start | bytes 3145732
  56.2 4.8 %collective-permute-start.1 = (f32[64,1536]{1,0:T(8,128)S(1)}, f32[64,1536]{1,0:T(8,128)S(1)}, u32[]{:S(2)}, u32[]{:S(2)}) collective-permute-start(f32[64,1536]{1,0:T(8,128)S(1)} %bitcast.12), channel_id=1, source_target_pairs={{0,8},{8,0},{16,24},{24,16},{32,40},{40,32},{48,56},{56,48},{64,72... | collective-permute-start | bytes 1179656 | tf_op jit(solution)/shard_map/ppermute | solution.py:451

commit v9 on v8

--- a/solution.py
+++ b/solution.py
@@ -299,12 +299,13 @@
     a, b = mine[...], other[...]
     rows = jnp.concatenate([jnp.where(first_core, a, b), jnp.where(first_core, b, a)], axis=0)
     low = rows.astype(BF16)
-    for i in range(rows.shape[1] // NB):
-        separators[i * NB : (i + 1) * NB, :] = rows[:, i * NB : (i + 1) * NB].T
     outward = [pltpu.make_async_copy(separators, separators_hbm, out_sem.at[0])]
-    outward[0].start()
     for k in range(0, LB, 2):
         terms = mm(low, jnp.concatenate([weights[k], weights[k + 1]], axis=1))
+        for i in range(2 * k, min(2 * k + 4, rows.shape[1] // NB)):
+            separators[i * NB : (i + 1) * NB, :] = rows[:, i * NB : (i + 1) * NB].T
+        if k == 4:
+            outward[0].start()
         for j in range(2):
             value = base[k + j] - terms[:, j * NB : (j + 1) * NB]
             local[(k + j) * NB : (k + j + 1) * NB, :] = value.T

time: 63.7 us -> 63.9 us (level)
  no operation moved by 1% of the time
where the time goes in v9:
time: 63.9 us; the launch traced here: 63.7 us
  blocking collectives  25.2 us (39%)
  Pallas kernels  23.1 us (36%)
  starting transfers between devices  11.1 us (17%)
  waiting for transfers between devices  3.55 us (6%)
  between operations  0.66 us (1%)
    all_to_all x1, blocking collectives, on_device(): lax.all_to_all(summed, 'leaf', 0, 0, axis_index_groups=chips, tiled=True)  14.2 us
    pallas_call x1, Pallas kernels, run_forward(): pl.pallas_call(forward_kernel, out_shape=(pltpu.HBM((LB, height, NB), BF1...  11 us
    all_to_all x1, blocking collectives, on_device(): mine = lax.all_to_all(solved, 'rep', 0, 0, tiled=True).reshape(half, height)  11 us
    all_to_all x1, starting transfers between devices, on_device(): lax.all_to_all(total.reshape(reps, CH, height), 'rep', 0, 0, tiled=True)  6.13 us
    pallas_call x1, Pallas kernels, run_separator(): pl.pallas_call(separator_kernel, out_shape=(pltpu.HBM(forward_t.shape, F3...  6.01 us
    ppermute x1, starting transfers between devices, on_device(): other = lax.ppermute(mine, 'leaf', pairs)  3.43 us
    pallas_call x1, Pallas kernels, on_device(): pl.pallas_call(finish_kernel, out_shape=(pltpu.HBM((rows, columns), F32),...  2.71 us
    pallas_call x1, Pallas kernels, on_device(): pl.pallas_call(tree_kernel, out_shape=shape((reps, CH, height)), in_specs...  2.36 us
  transfers between devices with their start and end apart: 3, of which 3 were waited for; matrix products, arithmetic and copies ran while one was open for 0% of the time, Pallas kernels for 9%

profile of v9, /device:TPU:1, one launch (start us, length us, event | category | flops | bytes accessed | tf_op | source)
XLA Modules:
  0.0 63.7 jit_solution(8862392587983617330)
XLA Ops:
  0.6 0.1 pad_add_fusion.place
  0.7 11.0 %forward.1 = (bf16[16,1536,128]{2,1,0:T(8,128)(2,1)}, bf16[16,128,128]{2,1,0:T(8,128)(2,1)}, bf16[16,256,128]{2,1,0:T(8,128)(2,1)}, f32[64,1536]{1,0:T(8,128)S(1)}, f32[64,1536]{1,0:T(8,128)S(1)}) custom-call(s32[2]{0:T(128)S(1)} %pad_add_fusion.place, s32[1,1,15]{2,1,0:T(1,128)} %parent_hbm.3, f32[16,128,128]{2,1,0:T(8,128)} %bitcast.15, ...), custom_call_target="tpu_custom_call" | custom-call | tf_op jit(solution)/shard_map/forward/pallas_call | solution.py:329
  11.8 1.5 %collective-permute-start = (f32[64,1536]{1,0:T(8,128)S(1)}, f32[64,1536]{1,0:T(8,128)S(1)}, u32[]{:S(2)}, u32[]{:S(2)}) collective-permute-start(f32[64,1536]{1,0:T(8,128)S(1)} %get-tuple-element.20), channel_id=1, source_target_pairs={{0,8},{8,0},{16,24},{24,16},{32,40},{40,32},{48,56},{56,48},{64,72... | collective-permute-start | bytes 1179656 | tf_op jit(solution)/shard_map/ppermute | solution.py:422
  13.3 1.3 %collective-permute-done.second = f32[64,1536]{1,0:T(8,128)S(1)} collective-permute-done((f32[64,1536]{1,0:T(8,128)S(1)}, f32[64,1536]{1,0:T(8,128)S(1)}, u32[]{:S(2)}, u32[]{:S(2)}) %collective-permute-start) | collective-permute-done | bytes 393248 | tf_op jit(solution)/shard_map/ppermute | solution.py:422
  14.6 0.8 %sum.1 = f32[64,1536]{1,0:T(8,128)} custom-call(f32[64,1536]{1,0:T(8,128)S(1)} %get-tuple-element.19.first, f32[64,1536]{1,0:T(8,128)S(1)} %collective-permute-done.second), custom_call_target="tpu_custom_call" | custom-call | tf_op jit(solution)/shard_map/sum/pallas_call | solution.py:415
  15.4 6.1 %all-to-all-start = ((f32[8,8,1536]{2,1,0:T(8,128)}), f32[8,8,1536]{2,1,0:T(8,128)S(1)}, u32[]{:S(2)}, u32[]{:S(2)}) async-start(f32[8,8,1536]{2,1,0:T(8,128)} %bitcast.6), calls=%async_computation | async-start | bytes 786432 | tf_op jit(solution)/shard_map/all_to_all | solution.py:423
  21.5 6.0 %separator.1 = (f32[16,128,128]{2,1,0:T(8,128)}, bf16[4,6,128,128]{3,2,1,0:T(8,128)(2,1)S(1)}, bf16[7,384,384]{2,1,0:T(8,128)(2,1)S(1)}) custom-call(s32[2]{0:T(128)S(1)} %pad_add_fusion.place, bf16[15,3,128,128]{3,2,1,0:T(8,128)(2,1)} %inverse_hbm.1, bf16[15,384,384]{2,1,0:T(8,128)(2,1)} %lower_hbm.1, bf16[14,384,384]{2,1,0:T(8,128)(2,1)} %coupling_hbm.1, ...), custom_call_target="tpu_custom_call" | custom-call | flops 6000000000 | bytes 20000000 | tf_op jit(solution)/shard_map/separator/pallas_call | solution.py:362
  27.5 0.9 %all-to-all-done.parts = f32[8,8,1536]{2,1,0:T(8,128)S(1)} async-done(((f32[8,8,1536]{2,1,0:T(8,128)}), f32[8,8,1536]{2,1,0:T(8,128)S(1)}, u32[]{:S(2)}, u32[]{:S(2)}) %all-to-all-start) | async-done | bytes 393248 | tf_op jit(solution)/shard_map/all_to_all | solution.py:423
  28.4 0.2 level.1
  28.6 14.2 %all_to_all.15.gathered = f32[8,8,1152]{2,1,0:T(8,128)S(1)} all-to-all(f32[8,8,1152]{2,1,0:T(8,128)S(1)} %get-tuple-element.30), channel_id=1, replica_groups={{0,16,32,48,64,80,96,112},{8,24,40,56,72,88,104,120},{1,17,33,49,65,81,..., dimensions={0} | all-to-all | bytes 589824 | tf_op jit(solution)/shard_map/all_to_all | solution.py:437
  42.8 0.0 slice-start
  42.8 0.0 slice-start.1
  42.8 0.0 copy-start
  42.8 2.4 %tree.1 = f32[8,8,1536]{2,1,0:T(8,128)S(1)} custom-call(s32[2]{0:T(128)S(1)} %pad_add_fusion.place, f32[8,8,1152]{2,1,0:T(8,128)S(1)} %all_to_all.15.gathered, f32[8,384]{1,0:T(8,128)S(1)} %get-tuple-element.31.residue, bf16[4,6,128,128]{3,2,1,0:T(8,128)(2,1)S(1)} %get-tuple-element.29._full.full, bf16[7,384,384]{2,1,0:T(8,128)(2,1)S(1)} %get-tuple-element.28.product), custom_call_target="tpu_custom_call" | custom-call | flops 6000000000 | bytes 40000000 | tf_op jit(solution)/shard_map/tree/pallas_call | solution.py:438
  45.2 11.0 %all_to_all.16 = f32[8,8,1536]{2,1,0:T(8,128)S(1)} all-to-all(f32[8,8,1536]{2,1,0:T(8,128)S(1)} %tree.1), channel_id=1, replica_groups=mesh['leaf'=16,'rep'=8] {'rep'}, dimensions={0} | all-to-all | bytes 786432 | tf_op jit(solution)/shard_map/all_to_all | solution.py:451
  56.2 3.4 %collective-permute-start.1 = (f32[64,1536]{1,0:T(8,128)S(1)}, f32[64,1536]{1,0:T(8,128)S(1)}, u32[]{:S(2)}, u32[]{:S(2)}) collective-permute-start(f32[64,1536]{1,0:T(8,128)S(1)} %bitcast.12), channel_id=1, source_target_pairs={{0,8},{8,0},{16,24},{24,16},{32,40},{40,32},{48,56},{56,48},{64,72... | collective-permute-start | bytes 1179656 | tf_op jit(solution)/shard_map/ppermute | solution.py:452
  59.6 1.3 %collective-permute-done.1.other = f32[64,1536]{1,0:T(8,128)S(1)} collective-permute-done((f32[64,1536]{1,0:T(8,128)S(1)}, f32[64,1536]{1,0:T(8,128)S(1)}, u32[]{:S(2)}, u32[]{:S(2)}) %collective-permute-start.1) | collective-permute-done | bytes 393248 | tf_op jit(solution)/shard_map/ppermute | solution.py:452
  61.0 0.0 slice-done
  61.0 0.0 slice-done.1
  61.0 0.0 copy-done
  61.0 2.7 %finish.1 = (f32[2048,128]{1,0:T(8,128)}, f32[1536,128]{1,0:T(8,128)}) custom-call(s32[2]{0:T(128)S(1)} %pad_add_fusion.place, f32[64,1536]{1,0:T(8,128)S(1)} %bitcast.13, f32[64,1536]{1,0:T(8,128)S(1)} %collective-permute-done.1.other, f32[16,128,128]{2,1,0:T(8,128)S(1)} %copy-done, bf16[16,1536,128]{2,1,0:T(8,128)(2,1)S(1)} %bitcast.11), custom_call_target="tpu_custom_call" | custom-call | tf_op jit(solution)/shard_map/finish/pallas_call | solution.py:453
  (1 shorter events, 0.0 us)
Async XLA Ops:
  11.8 2.9 %collective-permute-start = (f32[64,1536]{1,0:T(8,128)S(1)}, f32[64,1536]{1,0:T(8,128)S(1)}, u32[]{:S(2)}, u32[]{:S(2)}) collective-permute-start(f32[64,1536]{1,0:T(8,128)S(1)} %get-tuple-element.20), channel_id=1, source_target_pairs={{0,8},{8,0},{16,24},{24,16},{32,40},{40,32},{48,56},{56,48},{64,72... | collective-permute-start | bytes 1179656 | tf_op jit(solution)/shard_map/ppermute | solution.py:422
  15.4 13.0 %all-to-all-start = ((f32[8,8,1536]{2,1,0:T(8,128)}), f32[8,8,1536]{2,1,0:T(8,128)S(1)}, u32[]{:S(2)}, u32[]{:S(2)}) async-start(f32[8,8,1536]{2,1,0:T(8,128)} %bitcast.6), calls=%async_computation | async-start | bytes 786432 | tf_op jit(solution)/shard_map/all_to_all | solution.py:423
  42.8 18.2 %slice-start = ((s8[6291456]{0:T(1024)(128)(4,1)}), s8[4194304]{0:T(1024)(128)(4,1)S(1)}, s32[]{:S(2)}) async-start(s8[6291456]{0:T(1024)(128)(4,1)} %bitcast.10), calls=%async_computation.3 | async-start | bytes 8388608
  42.8 18.2 %slice-start.1 = ((s8[6291456]{0:T(1024)(128)(4,1)}), s8[2097152]{0:T(1024)(128)(4,1)S(1)}, s32[]{:S(2)}) async-start(s8[6291456]{0:T(1024)(128)(4,1)} %bitcast.10), calls=%async_computation.4 | async-start | bytes 4194304
  42.8 18.2 %copy-start = (f32[16,128,128]{2,1,0:T(8,128)S(1)}, f32[16,128,128]{2,1,0:T(8,128)}, u32[]{:S(2)}) copy-start(f32[16,128,128]{2,1,0:T(8,128)} %get-tuple-element.32.base) | copy-start | bytes 3145732
  56.2 4.8 %collective-permute-start.1 = (f32[64,1536]{1,0:T(8,128)S(1)}, f32[64,1536]{1,0:T(8,128)S(1)}, u32[]{:S(2)}, u32[]{:S(2)}) collective-permute-start(f32[64,1536]{1,0:T(8,128)S(1)} %bitcast.12), channel_id=1, source_target_pairs={{0,8},{8,0},{16,24},{24,16},{32,40},{40,32},{48,56},{56,48},{64,72... | collective-permute-start | bytes 1179656 | tf_op jit(solution)/shard_map/ppermute | solution.py:452
